TPU v7x, 32 devices: a whole 2x2x4 slice. The times are simulated.
32 devices in a mesh: rows: 8 (over z, x), grp: 4 (over y, core).
Axes of the slice: x: 2, y: 2, z: 4, core: 2. Of those that a mesh axis runs over, the one named last changes fastest.
Arguments:
- layer_input: bfloat16 [128, 768, 512], P('rows', 'grp'), may hold values from -6 to 6
- segment_ids: int32 [128, 512], P('rows'), may hold values from 0 to 3, never falling along the last dimension, each value on 1 to 256 neighbouring positions
- qkv_weight: bfloat16 [4, 192, 576], P('grp'), may hold values from -0.4375 to 0.4375
- qv_bias: float32 [4, 384], P('grp'), may hold values from -4 to 4
- out_weight: bfloat16 [768, 768], replicated, may hold values from -0.875 to 0.875
- out_bias: float32 [768], replicated, may hold values from -4 to 4
- gain_one: float32 [768], replicated, may hold values from 0.1 to 1.9
- shift_one: float32 [768], replicated, may hold values from -4 to 4
- up_weight: bfloat16 [4, 192, 768], P('grp'), may hold values from -0.4375 to 0.4375
- up_bias: float32 [4, 768], P('grp'), may hold values from -4 to 4
- down_weight: bfloat16 [4, 192, 768], P('grp'), may hold values from -0.21875 to 0.21875
- down_bias: float32 [4, 192], P('grp'), may hold values from -4 to 4
- gain_two: float32 [768], P('grp'), may hold values from 0.1 to 1.9
- shift_two: float32 [768], P('grp'), may hold values from -4 to 4
- out_grad: bfloat16 [128, 768, 512], P('rows', 'grp'), may hold values from -6 to 6
Outputs:
- layer_output: float32 [128, 768, 512], P('rows', 'grp')
- input_grad: float32 [128, 768, 512], P('rows', 'grp')
- qkv_weight_grad: float32 [4, 192, 576], P('grp')
- qv_bias_grad: float32 [4, 384], P('grp')
- out_weight_grad: float32 [768, 768], replicated
- out_bias_grad: float32 [768], replicated
- gain_one_grad: float32 [768], replicated
- shift_one_grad: float32 [768], replicated
- up_weight_grad: float32 [4, 192, 768], P('grp')
- up_bias_grad: float32 [4, 768], P('grp')
- down_weight_grad: float32 [4, 192, 768], P('grp')
- down_bias_grad: float32 [4, 192], P('grp')
- gain_two_grad: float32 [768], P('grp')
- shift_two_grad: float32 [768], P('grp')
Inputs may be any that keep to these rules, and one draw needn't show every extreme that they name: `segment_ids`: in each packed sequence the segment numbers never fall, start at 0, and each segment has 1 to 256 tokens; one segment of each sequence has exactly 256.
All inputs are finite; a program needn't handle non-finite values.
Results may differ from a plain program's by a relative error of at most 0.02.
Values may be sent and summed in bfloat16 or wider, within the bound.
A program may use at most 256 MiB of HBM per device.

v0:
```python
from functools import partial

import jax
import jax.numpy as jnp
from jax import lax
from jax.sharding import PartitionSpec as P

D = 768
HEAD_DIM = 64
SEQ_LEN = 512
SEQ_DEV = 16


epsilon = 1e-05
masked = -1e30


def product(left_side, right_side):
    return jnp.dot(left_side, right_side, preferred_element_type=jnp.float32)


def left_inner(left_side, right_side):
    return lax.dot_general(
        left_side, right_side, (((0,), (0,)), ((), ())), preferred_element_type=jnp.float32
    )


def right_inner(left_side, right_side):
    return lax.dot_general(
        left_side, right_side, (((1,), (1,)), ((), ())), preferred_element_type=jnp.float32
    )


def split_heads(block_rows):
    return block_rows.reshape(block_rows.shape[0], -1, HEAD_DIM)


def sequence_view(block_rows):
    return block_rows.reshape(SEQ_DEV, SEQ_LEN, -1)


def token_major(channel_first):
    return jnp.transpose(channel_first, (0, 2, 1)).reshape(-1, channel_first.shape[1])


def channel_major(token_rows):
    return jnp.transpose(token_rows.reshape(-1, SEQ_LEN, token_rows.shape[1]), (0, 2, 1))


def scores_of(queries, keys, labels):
    same_doc = (labels[:, None] == labels[None, :])[None]
    raw_scores = jnp.einsum(
        "qhd,khd->hqk", split_heads(queries), split_heads(keys), preferred_element_type=jnp.float32
    ) * HEAD_DIM ** (-0.5)
    return jnp.where(same_doc, raw_scores, masked)


def attend_one(pieces):
    queries, keys, values, labels = pieces
    scores = scores_of(queries, keys, labels)
    largest = jnp.max(scores, axis=-1, keepdims=True)
    weights = jnp.exp(scores - largest)
    totals = jnp.sum(weights, axis=-1, keepdims=True)
    probability = (weights / totals).astype(jnp.bfloat16)
    context = jnp.einsum(
        "hqk,khd->qhd", probability, split_heads(values), preferred_element_type=jnp.float32
    )
    return (context.reshape(SEQ_LEN, -1).astype(jnp.bfloat16), (largest + jnp.log(totals))[..., 0])


def attend_back(pieces):
    queries, keys, values, labels, log_totals, context_grad = pieces
    scores = scores_of(queries, keys, labels)
    probability = jnp.exp(scores - log_totals[..., None])
    grad_heads = split_heads(context_grad)
    value_grad = jnp.einsum(
        "hqk,qhd->khd",
        probability.astype(jnp.bfloat16),
        grad_heads,
        preferred_element_type=jnp.float32,
    )
    prob_grad = jnp.einsum(
        "qhd,khd->hqk", grad_heads, split_heads(values), preferred_element_type=jnp.float32
    )
    middle = jnp.sum(probability * prob_grad, axis=-1, keepdims=True)
    score_grad = (probability * (prob_grad - middle)).astype(jnp.bfloat16)
    scaling = HEAD_DIM ** (-0.5)
    query_grad = (
        jnp.einsum(
            "hqk,khd->qhd", score_grad, split_heads(keys), preferred_element_type=jnp.float32
        )
        * scaling
    )
    key_grad = (
        jnp.einsum(
            "hqk,qhd->khd", score_grad, split_heads(queries), preferred_element_type=jnp.float32
        )
        * scaling
    )
    joined = jnp.concatenate(
        [
            query_grad.reshape(SEQ_LEN, -1),
            key_grad.reshape(SEQ_LEN, -1),
            value_grad.reshape(SEQ_LEN, -1),
        ],
        axis=1,
    )
    return joined.astype(jnp.bfloat16)


def channel_sums(summed):
    return (jnp.sum(summed, axis=1, keepdims=True), jnp.sum(summed * summed, axis=1, keepdims=True))


def standardize(summed, sums):
    center = sums[0] / D
    spread = sums[1] / D - center * center
    inverse = lax.rsqrt(spread + epsilon)
    return ((summed - center) * inverse, inverse)


def back_sums(scaled, normed):
    return (jnp.sum(scaled, axis=1, keepdims=True), jnp.sum(scaled * normed, axis=1, keepdims=True))


def norm_back(scaled, normed, inverse, sums):
    return inverse * (scaled - sums[0] / D - normed * sums[1] / D)


def local(
    layer_input,
    segment_ids,
    qkv_weight,
    qv_bias,
    out_weight,
    out_bias,
    gain_one,
    shift_one,
    up_weight,
    up_bias,
    down_weight,
    down_bias,
    gain_two,
    shift_two,
    out_grad,
):
    group_width = layer_input.shape[1]
    token_input = token_major(layer_input)
    projected = product(token_input, qkv_weight[0])
    queries = (projected[:, :group_width] + qv_bias[0, :group_width]).astype(jnp.bfloat16)
    keys = projected[:, group_width : 2 * group_width].astype(jnp.bfloat16)
    values = (projected[:, 2 * group_width :] + qv_bias[0, group_width:]).astype(jnp.bfloat16)
    context, log_totals = lax.map(
        attend_one,
        (sequence_view(queries), sequence_view(keys), sequence_view(values), segment_ids),
    )
    moved_context, moved_input = (
        lax.all_to_all(context, "grp", split_axis=1, concat_axis=2, tiled=True),
        lax.all_to_all(sequence_view(token_input), "grp", split_axis=1, concat_axis=2, tiled=True),
    )
    slice_context = moved_context.reshape(-1, D)
    branch = (product(slice_context, out_weight) + out_bias).astype(jnp.bfloat16)
    summed = branch.astype(jnp.float32) + moved_input.reshape(-1, D).astype(jnp.float32)
    normed_one, inverse_one = standardize(summed, channel_sums(summed))
    hidden_slices = (normed_one * gain_one + shift_one).astype(jnp.bfloat16)
    hidden = lax.all_to_all(
        hidden_slices.reshape(SEQ_DEV, -1, D), "grp", split_axis=2, concat_axis=1, tiled=True
    ).reshape(-1, group_width)
    up_value = product(hidden, up_weight[0]) + up_bias[0]
    activated = jax.nn.gelu(up_value, approximate=False).astype(jnp.bfloat16)
    summed_two = hidden.astype(jnp.float32) + right_inner(activated, down_weight[0]) + down_bias[0]
    stats_two = lax.psum(channel_sums(summed_two), "grp")
    normed_two, inverse_two = standardize(summed_two, stats_two)
    layer_output = normed_two * gain_two + shift_two
    cotangent = token_major(out_grad).astype(jnp.float32)
    gain_two_grad = jnp.sum(cotangent * normed_two, axis=0)
    shift_two_grad = jnp.sum(cotangent, axis=0)
    scaled_two = cotangent * gain_two
    sums_two = lax.psum(back_sums(scaled_two, normed_two), "grp")
    summed_two_grad = norm_back(scaled_two, normed_two, inverse_two, sums_two).astype(jnp.bfloat16)
    down_weight_grad = left_inner(summed_two_grad, activated)
    down_bias_grad = jnp.sum(summed_two_grad.astype(jnp.float32), axis=0)
    activated_grad = product(summed_two_grad, down_weight[0])
    unused_value, gelu_back = jax.vjp(partial(jax.nn.gelu, approximate=False), up_value)
    up_grad = gelu_back(activated_grad)[0].astype(jnp.bfloat16)
    up_weight_grad = left_inner(hidden, up_grad)
    up_bias_grad = jnp.sum(up_grad.astype(jnp.float32), axis=0)
    hidden_grad = (summed_two_grad.astype(jnp.float32) + right_inner(up_grad, up_weight[0])).astype(
        jnp.bfloat16
    )
    hidden_slice_grad = lax.all_to_all(
        sequence_view(hidden_grad), "grp", split_axis=1, concat_axis=2, tiled=True
    )
    hidden_slice_grad = hidden_slice_grad.reshape(-1, D).astype(jnp.float32)
    gain_one_grad = jnp.sum(hidden_slice_grad * normed_one, axis=0)
    shift_one_grad = jnp.sum(hidden_slice_grad, axis=0)
    scaled_one = hidden_slice_grad * gain_one
    summed_grad = norm_back(
        scaled_one, normed_one, inverse_one, back_sums(scaled_one, normed_one)
    ).astype(jnp.bfloat16)
    out_weight_grad = left_inner(slice_context, summed_grad)
    out_bias_grad = jnp.sum(summed_grad.astype(jnp.float32), axis=0)
    context_slices = right_inner(summed_grad, out_weight).astype(jnp.bfloat16)
    context_grad, residual_grad = (
        lax.all_to_all(
            context_slices.reshape(SEQ_DEV, -1, D), "grp", split_axis=2, concat_axis=1, tiled=True
        ),
        lax.all_to_all(
            summed_grad.reshape(SEQ_DEV, -1, D), "grp", split_axis=2, concat_axis=1, tiled=True
        ),
    )
    qkv_grad = lax.map(
        attend_back,
        (
            sequence_view(queries),
            sequence_view(keys),
            sequence_view(values),
            segment_ids,
            log_totals,
            context_grad,
        ),
    )
    qkv_grad = qkv_grad.reshape(-1, 3 * group_width)
    qkv_weight_grad = left_inner(token_input, qkv_grad)
    qkv_grad_wide = qkv_grad.astype(jnp.float32)
    qv_bias_grad = jnp.concatenate(
        [
            jnp.sum(qkv_grad_wide[:, :group_width], axis=0),
            jnp.sum(qkv_grad_wide[:, 2 * group_width :], axis=0),
        ]
    )
    input_grad = residual_grad.reshape(-1, group_width).astype(jnp.float32) + right_inner(
        qkv_grad, qkv_weight[0]
    )
    shared = lax.psum(
        (out_weight_grad, out_bias_grad, gain_one_grad, shift_one_grad), ("rows", "grp")
    )
    grouped = (
        lax.psum(qkv_weight_grad[None].astype(jnp.bfloat16), "rows").astype(jnp.float32),
        lax.psum(qv_bias_grad[None].astype(jnp.bfloat16), "rows").astype(jnp.float32),
        lax.psum(up_weight_grad[None].astype(jnp.bfloat16), "rows").astype(jnp.float32),
        lax.psum(up_bias_grad[None].astype(jnp.bfloat16), "rows").astype(jnp.float32),
        lax.psum(down_weight_grad[None].astype(jnp.bfloat16), "rows").astype(jnp.float32),
        lax.psum(down_bias_grad[None].astype(jnp.bfloat16), "rows").astype(jnp.float32),
        lax.psum(gain_two_grad.astype(jnp.bfloat16), "rows").astype(jnp.float32),
        lax.psum(shift_two_grad.astype(jnp.bfloat16), "rows").astype(jnp.float32),
    )
    return (
        channel_major(layer_output),
        channel_major(input_grad),
        grouped[0],
        grouped[1],
        shared[0],
        shared[1],
        shared[2],
        shared[3],
        grouped[2],
        grouped[3],
        grouped[4],
        grouped[5],
        grouped[6],
        grouped[7],
    )


def solution(mesh):
    in_specs = (
        P("rows", "grp", None),
        P("rows", None),
        P("grp", None, None),
        P("grp", None),
        P(),
        P(),
        P(),
        P(),
        P("grp", None, None),
        P("grp", None),
        P("grp", None, None),
        P("grp", None),
        P("grp"),
        P("grp"),
        P("rows", "grp", None),
    )
    out_specs = (
        P("rows", "grp", None),
        P("rows", "grp", None),
        P("grp", None, None),
        P("grp", None),
        P(),
        P(),
        P(),
        P(),
        P("grp", None, None),
        P("grp", None),
        P("grp", None, None),
        P("grp", None),
        P("grp"),
        P("grp"),
    )
    return jax.shard_map(local, mesh=mesh, in_specs=in_specs, out_specs=out_specs, check_vma=False)
```

profile of v0, /device:TPU:0, one launch (start us, length us, event | category | flops | bytes accessed | tf_op | source)
XLA Modules:
  0.0 1092.2 jit_solution(13848970402981251746)
XLA Ops:
  24.9 109.0 %while.22 = (s32[]{:T(128)}, bf16[16,512,192]{1,2,0:T(8,128)(2,1)}, f32[16,3,512]{2,1,0:T(4,128)}, bf16[16,512,192]{1,2,0:T(8,128)(2,1)}, s32[16,512]{1,0:T(8,12...) while((s32[]{:T(128)}, bf16[16,512,192]{1,2,0:T(8,128)(2,1)}, ...), condition=%wide.region_3.4_spmd, body=%wide.region_0.3_spmd.sunk | while | flops 211122688 | bytes 12903521 | solution.py:153
  154.0 41.3 %all-to-all-done = bf16[16,512,192]{2,0,1:T(8,128)(2,1)} async-done(((bf16[16,512,192]{2,0,1:T(8,128)(2,1)}), bf16[16,512,192]{2,0,1:T(8,128)(2,1)}, u32[]{:S(2)}, u32[]{:S(2)}) %all-to-all-start) | async-done | bytes 3145760 | tf_op jit(solution)/shard_map/all_to_all | solution.py:158
  200.6 8.3 copy.185
  208.9 39.9 %all-to-all-done.1 = bf16[16,512,192]{2,0,1:T(8,128)(2,1)} async-done(((bf16[16,512,192]{2,0,1:T(8,128)(2,1)}), bf16[16,512,192]{2,0,1:T(8,128)(2,1)}, u32[]{:S(2)}, u32[]{:S(2)}) %all-to-all-start.1) | async-done | bytes 3145760 | tf_op jit(solution)/shard_map/all_to_all | solution.py:159
  248.8 8.5 copy.186
  257.3 8.5 copy.250
  272.5 8.0 fusion.56
  298.5 33.5 %all-to-all-done.2 = bf16[16,128,768]{1,0,2:T(8,128)(2,1)} async-done(((bf16[16,128,768]{1,0,2:T(8,128)(2,1)}), bf16[16,128,768]{1,0,2:T(8,128)(2,1)}, u32[]{:S(2)}, u32[]{:S(2)}) %all-to-all-start.2) | async-done | bytes 3145760 | tf_op jit(solution)/shard_map/all_to_all | solution.py:166
  345.8 60.5 %multiply_convert_fusion.1 = (bf16[8192,768]{1,0:T(8,128)(2,1)S(1)}, f32[8192,768]{1,0:T(8,128)}, f32[8192,768]{1,0:T(8,128)}) fusion(f32[768]{0:T(1024)S(1)} %reduce.9, bf16[8192,192]{0,1:T(8,128)(2,1)} %reshape.380, bf16[1,192,768]{2,1,0:T(8,128)(2,1)S(1)} %copy-done.26), kind=kOutput, calls=%fused_computation.37 | convolution fusion | flops 2831155200 | bytes 66358272 | tf_op jit(solution)/shard_map/dot_general | solution.py:19
  422.5 23.6 %all-reduce.14.cloned.1.call-done = (f32[8192,1]{0,1:T(1,128)}, f32[8192,1]{0,1:T(1,128)}) async-done(((f32[8192,1]{0,1:T(1,128)}, f32[8192,1]{0,1:T(1,128)}), (f32[8192,1]{0,1:T(1,128)}, f32[8192,1]{0,1:T(1,128)})) %all-reduce.14.cloned.1.call-update) | async-done | bytes 65552 | tf_op jit(solution)/shard_map/psum | solution.py:172
  446.9 8.5 multiply_reduce_fusion.1
  455.4 31.3 %all-reduce.12.cloned.1.call-done = (f32[8192]{0:T(1024)}, f32[8192,1]{0,1:T(1,128)}) async-done(((f32[8192]{0:T(1024)}, f32[8192,1]{0,1:T(1,128)}), (f32[8192]{0:T(1024)}, f32[8192,1]{0,1:T(1,128)})) %all-reduce.12.cloned.1.call-update) | async-done | bytes 65552 | tf_op jit(solution)/shard_map/psum | solution.py:179
  487.5 7.7 fusion.57
  495.3 26.3 %fusion.61 = (bf16[768]{0:T(1024)(128)(2,1)S(1)}, bf16[8192,768]{1,0:T(8,128)(2,1)}) fusion(f32[8192,768]{1,0:T(8,128)} %get-tuple-element.249, bf16[8192,192]{0,1:T(8,128)(2,1)} %get-tuple-element.247, bf16[1,192,768]{2,1,0:T(8,128)(2,1)S(1)} %copy-done.25, f32[8192,768]{1,0:T(8,128)} %get-tuple-element.272, f32[768]{0:T(1024)S(1)} %reduce.9), kind=kOutput, calls=%fused_computation.126 | convolution fusion | flops 2516581632 | bytes 66359808 | tf_op jit(solution)/shard_map/dot_general | solution.py:19
  521.6 9.7 fusion.19
  534.3 8.1 copy.193
  547.9 48.0 %all-to-all-done.3 = bf16[16,512,192]{2,0,1:T(8,128)(2,1)} async-done(((bf16[16,512,192]{2,0,1:T(8,128)(2,1)}), bf16[16,512,192]{2,0,1:T(8,128)(2,1)}, u32[]{:S(2)}, u32[]{:S(2)}) %all-to-all-start.3) | async-done | bytes 3145760 | tf_op jit(solution)/shard_map/all_to_all | solution.py:191
  595.9 7.6 copy.194
  610.1 12.2 %copy.220 = f32[16,128,4,192]{3,2,1,0:T(4,128)} copy(f32[16,128,4,192]{1,2,3,0:T(4,128)} %bitcast.255) | data formatting | bytes 12582912 | tf_op jit(solution)/shard_map/convert_element_type | solution.py:194
  622.3 10.0 reshape.397
  660.3 9.0 fusion.40
  669.3 7.9 fusion.39
  682.3 14.9 %all-to-all-done.5 = bf16[16,128,768]{1,0,2:T(8,128)(2,1)} async-done(((bf16[16,128,768]{1,0,2:T(8,128)(2,1)}), bf16[16,128,768]{1,0,2:T(8,128)(2,1)}, u32[]{:S(2)}, u32[]{:S(2)}) %all-to-all-start.5) | async-done | bytes 3145760 | tf_op jit(solution)/shard_map/all_to_all | solution.py:205
  713.9 141.5 %while.23 = (s32[]{:T(128)}, bf16[16,512,576]{1,2,0:T(8,128)(2,1)}, bf16[16,512,192]{1,2,0:T(8,128)(2,1)}, s32[16,512]{1,0:T(8,128)}, bf16[16,512,192]{1,2,0:T(8...) while((s32[]{:T(128)}, bf16[16,512,576]{1,2,0:T(8,128)(2,1)}, ...), condition=%wide.region_18.19_spmd, body=%wide.region_16.18_spmd.sunk | while | flops 512915968 | bytes 28873324 | solution.py:212
  855.4 8.8 fusion.41
  877.9 41.1 %all-reduce = (f32[768]{0:T(1024)}, f32[768]{0:T(1024)}, f32[768]{0:T(1024)}) all-reduce(f32[768]{0:T(1024)S(1)} %get-tuple-element.244, f32[768]{0:T(1024)S(1)} %get-tuple-element.191, f32[768]{0:T(1024)S(1)} %reduce_sum.195), channel_id=1, replica_groups=mesh['rows'=8,'grp'=4] {'rows','grp'}, use_global_device_ids=true, to_apply=%region_25.26 | all-reduce | flops 2304 | bytes 18432 | tf_op jit(solution)/shard_map/psum | solution.py:235
  918.9 8.8 copy.229
  927.7 12.8 %convert_element_type.252 = f32[8192,576]{0,1:T(8,128)} convert(bf16[8192,576]{0,1:T(8,128)(2,1)} %bitcast.253) | non-fusion elementwise | flops 4718592 | bytes 28311552 | tf_op jit(solution)/shard_map/convert_element_type | solution.py:225
  945.9 22.3 %all-reduce.3 = (bf16[1,384]{1,0:T(2,128)(2,1)S(1)}, bf16[1,768]{1,0:T(2,128)(2,1)S(1)}, bf16[1,192]{1,0:T(2,128)(2,1)S(1)}, bf16[192]{0:T(256)(128)(2,1)S(1)}, bf16[192]{0:T(256)(128)(2,1)S(1)}) all-reduce(bf16[1,384]{1,0:T(2,128)(2,1)S(1)} %pad_maximum_fusion, ...), channel_id=1, replica_groups=mesh['rows'=8,'grp'=4] {'rows'}, use_global_device_ids=true, to_apply=%region_22.23 | all-reduce | flops 1728 | bytes 6912 | tf_op jit(solution)/shard_map/psum | solution.py:240
  981.3 8.1 reshape.391
  989.5 8.2 convolution_add_fusion
  1006.5 75.5 %all-reduce.10.cloned.1.call-done = f32[768,768]{1,0:T(8,128)} async-done(((f32[768,768]{1,0:T(8,128)}), f32[768,768]{1,0:T(8,128)}) %all-reduce.10.cloned.1.call-update) | async-done | bytes 2359312 | tf_op jit(solution)/shard_map/psum | solution.py:235
  (474 shorter events, 457.4 us)
Async XLA Ops:
  7.2 265.3 %copy-start = (bf16[768,768]{1,0:T(8,128)(2,1)S(1)}, bf16[768,768]{1,0:T(8,128)(2,1)}, u32[]{:S(2)}) copy-start(bf16[768,768]{1,0:T(8,128)(2,1)} %param.23) | copy-start | bytes 3538948
  141.5 53.7 %all-to-all-start = ((bf16[16,512,192]{2,0,1:T(8,128)(2,1)}), bf16[16,512,192]{2,0,1:T(8,128)(2,1)}, u32[]{:S(2)}, u32[]{:S(2)}) async-start(bf16[16,512,192]{2,0,1:T(8,128)(2,1)} %copy.184), calls=%async_computation | async-start | bytes 8388608 | tf_op jit(solution)/shard_map/all_to_all | solution.py:158
  195.3 53.5 %all-to-all-start.1 = ((bf16[16,512,192]{2,0,1:T(8,128)(2,1)}), bf16[16,512,192]{2,0,1:T(8,128)(2,1)}, u32[]{:S(2)}, u32[]{:S(2)}) async-start(bf16[16,512,192]{2,0,1:T(8,128)(2,1)} %bitcast.275), calls=%async_computation.1 | async-start | bytes 8388608 | tf_op jit(solution)/shard_map/all_to_all | solution.py:159
  265.9 6.6 copy-start.27
  272.4 10.6 copy-start.14
  272.4 10.6 copy-start.18
  285.3 9.9 copy-start.19
  285.3 9.9 copy-start.16
  290.3 41.7 %all-to-all-start.2 = ((bf16[16,128,768]{1,0,2:T(8,128)(2,1)}), bf16[16,128,768]{1,0,2:T(8,128)(2,1)}, u32[]{:S(2)}, u32[]{:S(2)}) async-start(bf16[16,128,768]{1,0,2:T(8,128)(2,1)} %copy.188), calls=%async_computation.2 | async-start | bytes 6291456 | tf_op jit(solution)/shard_map/all_to_all | solution.py:166
  295.0 151.1 %all-reduce.14.cloned.1.call-start = ((), (), s32[]{:S(2)}) async-start(), calls=%async_computation.8 | async-start | bytes 131072 | tf_op jit(solution)/shard_map/psum | solution.py:172
  332.0 13.8 %copy-start.26 = (bf16[1,192,768]{2,1,0:T(8,128)(2,1)S(1)}, bf16[1,192,768]{2,1,0:T(8,128)(2,1)}, u32[]{:S(2)}) copy-start(bf16[1,192,768]{2,1,0:T(8,128)(2,1)} %param.27) | copy-start | bytes 884740
  345.8 60.5 %copy-start.5 = (bf16[8192,192]{0,1:T(8,128)(2,1)S(1)}, bf16[8192,192]{0,1:T(8,128)(2,1)}, u32[]{:S(2)}) copy-start(bf16[8192,192]{0,1:T(8,128)(2,1)} %reshape.380) | copy-start | bytes 9437188
  345.8 60.5 %copy-start.25 = (bf16[1,192,768]{2,1,0:T(8,128)(2,1)S(1)}, bf16[1,192,768]{2,1,0:T(8,128)(2,1)}, u32[]{:S(2)}) copy-start(bf16[1,192,768]{2,1,0:T(8,128)(2,1)} %param.29) | copy-start | bytes 884740
  345.8 60.5 %copy-start.28 = (f32[1,192]{1,0:T(1,128)S(1)}, f32[1,192]{1,0:T(1,128)}, u32[]{:S(2)}) copy-start(f32[1,192]{1,0:T(1,128)} %param.30) | copy-start | bytes 2308
  406.2 7.4 copy-start.29
  413.6 73.1 %all-reduce.12.cloned.1.call-start = ((), (), s32[]{:S(2)}) async-start(), calls=%async_computation.7 | async-start | bytes 131072 | tf_op jit(solution)/shard_map/psum | solution.py:179
  418.4 28.5 %copy-start.17 = (f32[192]{0:T(256)S(1)}, f32[192]{0:T(256)}, u32[]{:S(2)}) copy-start(f32[192]{0:T(256)} %param.31) | copy-start | bytes 2308
  418.4 28.5 %copy-start.23 = (f32[192]{0:T(256)S(1)}, f32[192]{0:T(256)}, u32[]{:S(2)}) copy-start(f32[192]{0:T(256)} %param.32) | copy-start | bytes 2308
  534.3 13.4 %copy-start.15 = (f32[768]{0:T(1024)S(1)}, f32[768]{0:T(1024)}, u32[]{:S(2)}) copy-start(f32[768]{0:T(1024)} %param.25) | copy-start | bytes 9220
  542.4 53.5 %all-to-all-start.3 = ((bf16[16,512,192]{2,0,1:T(8,128)(2,1)}), bf16[16,512,192]{2,0,1:T(8,128)(2,1)}, u32[]{:S(2)}, u32[]{:S(2)}) async-start(bf16[16,512,192]{2,0,1:T(8,128)(2,1)} %copy.193), calls=%async_computation.3 | async-start | bytes 8388608 | tf_op jit(solution)/shard_map/all_to_all | solution.py:191
  622.3 10.1 copy-start.10
  622.3 10.1 copy-start.12
  632.3 6.4 copy-start.2
  655.5 41.8 %all-to-all-start.5 = ((bf16[16,128,768]{1,0,2:T(8,128)(2,1)}), bf16[16,128,768]{1,0,2:T(8,128)(2,1)}, u32[]{:S(2)}, u32[]{:S(2)}) async-start(bf16[16,128,768]{1,0,2:T(8,128)(2,1)} %copy.201), calls=%async_computation.5 | async-start | bytes 6291456 | tf_op jit(solution)/shard_map/all_to_all | solution.py:205
  660.3 9.0 copy-start.6
  697.3 273.8 %all-to-all-start.4 = ((bf16[16,128,768]{1,0,2:T(8,128)(2,1)}), bf16[16,128,768]{1,0,2:T(8,128)(2,1)}, u32[]{:S(2)}, u32[]{:S(2)}) async-start(bf16[16,128,768]{1,0,2:T(8,128)(2,1)} %copy.198), calls=%async_computation.4 | async-start | bytes 6291456 | tf_op jit(solution)/shard_map/all_to_all | solution.py:208
  702.0 299.2 %all-reduce.16.cloned.1.call-start = ((), (), s32[]{:S(2)}) async-start(), calls=%async_computation.9 | async-start | bytes 1671168 | tf_op jit(solution)/shard_map/psum | solution.py:239
  864.2 217.8 %all-reduce.10.cloned.1.call-start = ((), (), s32[]{:S(2)}) async-start(), calls=%async_computation.6 | async-start | bytes 4718592 | tf_op jit(solution)/shard_map/psum | solution.py:235
  864.3 6.5 copy-start.24
  940.5 5.4 copy-start.21
  940.5 5.4 copy-start.22
  981.3 8.1 copy-start.8
  (8 other events, 27.6 us)
Sparse Core Ops, SparseCore 0:
  413.8 32.2 all-reduce.13
  455.6 31.1 all-reduce.11
  864.3 77.4 all-reduce.15
  947.8 134.0 all-reduce.9
where the time goes:
time: 1110 us; the launch traced here: 1090 us
  waiting for transfers between devices  308 us (28%)
  local copies, waits for them, and re-layouts  307 us (28%)
  matrix products  242 us (22%)
  other arithmetic  125 us (11%)
  blocking collectives  63.4 us (6%)
  starting transfers between devices  29.9 us (3%)
  between operations  14.6 us (1%)
    dot_general x4, matrix products, product(): return jnp.dot(left_side, right_side, preferred_element_type=jnp.float32)  97.4 us
    dynamic_slice x96, local copies, waits for them, and re-layouts, local(): lax.map(attend_one, (sequence_view(queries), sequence_view(keys), sequenc...  88.7 us
    psum x1, waiting for transfers between devices, local(): lax.psum((out_weight_grad, out_bias_grad, gain_one_grad, shift_one_grad),...  75.5 us
    all_to_all x1, waiting for transfers between devices, local(): lax.all_to_all(sequence_view(hidden_grad), 'grp', split_axis=1, concat_ax...  48 us
    all_to_all x1, waiting for transfers between devices, local(): lax.all_to_all(context, 'grp', split_axis=1, concat_axis=2, tiled=True)  41.3 us
    psum x1, blocking collectives, local(): lax.psum((out_weight_grad, out_bias_grad, gain_one_grad, shift_one_grad),...  41.1 us
    all_to_all x1, waiting for transfers between devices, local(): lax.all_to_all(sequence_view(token_input), 'grp', split_axis=1, concat_ax...  39.9 us
    all_to_all x1, waiting for transfers between devices, local(): lax.all_to_all(hidden_slices.reshape(SEQ_DEV, -1, D), 'grp', split_axis=2...  33.5 us
  transfers between devices with their start and end apart: 10, of which 8 were waited for; matrix products, arithmetic and copies ran while one was open for 26% of the time, Pallas kernels for 0%

commit v1 on v0

v1 whole, which is shorter than its diff:
```python
import jax
import jax.numpy as jnp
from jax import lax
from jax.experimental import pallas as pl
from jax.experimental.pallas import tpu as pltpu
from jax.sharding import PartitionSpec as P

D = 768
HEAD_DIM = 64
SEQ_LEN = 512
GROUPS = 4
WIDTH = D // GROUPS
HEADS_GROUP = WIDTH // HEAD_DIM
HEADS = D // HEAD_DIM
QKV = 3 * WIDTH
UNITS = 768
PAD = HEAD_DIM + 16
MASKED = -1e30
EPS = 1e-05
UNROLL = 4
SCALE = HEAD_DIM ** (-0.5)

F32 = jnp.float32
BF16 = jnp.bfloat16

Q_BIAS, V_BIAS, UP_BIAS, DOWN_BIAS, GAIN_TWO, SHIFT_TWO = 0, 1, 2, 6, 7, 8
GROUP_COLS = 9
OUT_BIAS, GAIN_ONE, SHIFT_ONE = GROUPS * GROUP_COLS, GROUPS * GROUP_COLS + GROUPS, GROUPS * GROUP_COLS + 2 * GROUPS
COLS = GROUPS * GROUP_COLS + 3 * GROUPS


def nn(a, b):
    return lax.dot_general(a, b, (((1,), (0,)), ((), ())), preferred_element_type=F32)


def nt(a, b):
    return lax.dot_general(a, b, (((1,), (1,)), ((), ())), preferred_element_type=F32)


def tn(a, b):
    return lax.dot_general(a, b, (((0,), (0,)), ((), ())), preferred_element_type=F32)


def lane_part(value):
    total = value[:, 0:128]
    for at in range(128, SEQ_LEN, 128):
        total = total + value[:, at : at + 128]
    return total


def channel_sum(value):
    return jnp.sum(value, axis=0, keepdims=True)


def fold(value):
    return jnp.sum(value.reshape(value.shape[0] // 8, 8, SEQ_LEN), axis=0)


def spread(column):
    return jnp.concatenate([column] * (SEQ_LEN // 128), axis=1)


def gelu_pair(u):
    half_erf = 0.5 * lax.erf(u * 0.7071067811865476) + 0.5
    density = jnp.exp(u * u * -0.5) * 0.3989422804014327
    return u * half_erf, half_erf + u * density


def layer_kernel(
    x, dy, seg, wqkv, wup, wdown, wout, params,
    lo, dx, g_qkv, g_up, g_down, g_out, g_vec,
    wqkv_t, wup_t, wdown_t, wout_t, cols, vec,
    q_s, k_s, v_s, e_s, linv_s, ctx_s, summed_s, hidden_s, act_s, slope_s, summed2_s, grad2_s,
    up_grad_s, hidden_grad_s, summed_grad_s, ctx_grad_s, qkv_grad_s,
):
    step = pl.program_id(0)
    zero = jnp.zeros((8, SEQ_LEN), F32)

    @pl.when(step == 0)
    def _():
        def turn(g, carry):
            wqkv_t[g] = wqkv[g].T
            wup_t[g] = wup[g].T
            wdown_t[g] = wdown[g].T
            return carry

        lax.fori_loop(0, GROUPS, turn, 0)
        wout_t[...] = wout[...].T
        table = params[...].T
        for at in range(COLS):
            cols[at] = jnp.broadcast_to(table[:, at : at + 1], (WIDTH, 128))
        g_qkv[...] = jnp.zeros_like(g_qkv)
        g_up[...] = jnp.zeros_like(g_up)
        g_down[...] = jnp.zeros_like(g_down)
        g_out[...] = jnp.zeros_like(g_out)
        vec[...] = jnp.zeros_like(vec)

    def col(at):
        return spread(cols[at])

    def over_groups(body, init=0):
        return lax.fori_loop(0, GROUPS, body, init)

    def rows_of(g):
        return pl.ds(pl.multiple_of(g * WIDTH, WIDTH), WIDTH)

    label = seg[0:1, :]
    ids = lax.broadcasted_iota(jnp.int32, (16, SEQ_LEN), 0)
    hot = (ids == label).astype(F32)
    hot_k = hot.astype(BF16)
    hot_q = jnp.where(ids < 4, (1.0 - hot) * MASKED, 0.0).astype(BF16)

    def project(g, carry):
        xg = x[g]
        base = g * GROUP_COLS
        q = (nn(wqkv_t[g, 0:WIDTH, :], xg) + col(base + Q_BIAS)).astype(BF16) * jnp.asarray(SCALE, BF16)
        k = nn(wqkv_t[g, WIDTH : 2 * WIDTH, :], xg).astype(BF16)
        v = (nn(wqkv_t[g, 2 * WIDTH :, :], xg) + col(base + V_BIAS)).astype(BF16)
        for h in range(HEADS_GROUP):
            at = g * HEADS_GROUP + h
            q_s[at, 0:HEAD_DIM, :] = q[h * HEAD_DIM : (h + 1) * HEAD_DIM]
            k_s[at, 0:HEAD_DIM, :] = k[h * HEAD_DIM : (h + 1) * HEAD_DIM]
            v_s[at] = v[h * HEAD_DIM : (h + 1) * HEAD_DIM]
            q_s[at, HEAD_DIM:PAD, :] = hot_q
            k_s[at, HEAD_DIM:PAD, :] = hot_k
        return carry

    over_groups(project)

    def attend(h, carry):
        scores = tn(k_s[h], q_s[h])
        largest = jnp.max(scores, axis=0, keepdims=True)
        weights = jnp.exp(scores - largest)
        inverse = 1.0 / channel_sum(weights)
        e = weights.astype(BF16)
        e_s[h] = e
        linv_s[h] = inverse
        ctx_s[h] = (nn(v_s[h], e) * inverse).astype(BF16)
        return carry

    lax.fori_loop(0, HEADS, attend, 0, unroll=UNROLL)

    def mix(g, carry):
        total, square = carry
        ctx = ctx_s[...].reshape(D, SEQ_LEN)
        branch = (nn(wout_t[rows_of(g), :], ctx) + col(OUT_BIAS + g)).astype(BF16)
        summed = branch.astype(F32) + x[g].astype(F32)
        summed_s[g] = summed
        return total + fold(summed), square + fold(summed * summed)

    total, square = over_groups(mix, (zero, zero))
    center1 = channel_sum(total) / D
    inverse1 = lax.rsqrt(channel_sum(square) / D - center1 * center1 + EPS)

    def feed(g, carry):
        total, square = carry
        base = g * GROUP_COLS
        normed = (summed_s[g] - center1) * inverse1
        hidden = (normed * col(GAIN_ONE + g) + col(SHIFT_ONE + g)).astype(BF16)
        hidden_s[g] = hidden
        for part in range(UNITS // WIDTH):
            rows = slice(part * WIDTH, (part + 1) * WIDTH)
            u = nn(wup_t[g, rows, :], hidden) + col(base + UP_BIAS + part)
            act, slope = gelu_pair(u)
            act_s[g, rows, :] = act.astype(BF16)
            slope_s[g, rows, :] = slope.astype(BF16)
        summed2 = hidden.astype(F32) + nn(wdown[g], act_s[g]) + col(base + DOWN_BIAS)
        summed2_s[g] = summed2
        return total + fold(summed2), square + fold(summed2 * summed2)

    total, square = over_groups(feed, (zero, zero))
    center2 = channel_sum(total) / D
    inverse2 = lax.rsqrt(channel_sum(square) / D - center2 * center2 + EPS)

    def finish(g, carry):
        sum_e, sum_en = carry
        base = g * GROUP_COLS
        normed = (summed2_s[g] - center2) * inverse2
        gain = col(base + GAIN_TWO)
        lo[g] = (normed * gain + col(base + SHIFT_TWO)).astype(BF16)
        grad = dy[g].astype(F32)
        product = grad * normed
        vec[base + GAIN_TWO] += lane_part(product)
        vec[base + SHIFT_TWO] += lane_part(grad)
        summed2_s[g] = normed
        return sum_e + fold(grad * gain), sum_en + fold(product * gain)

    sum_e, sum_en = over_groups(finish, (zero, zero))
    mean_e = channel_sum(sum_e) / D
    mean_en = channel_sum(sum_en) / D

    def feed_back(g, carry):
        sum_h, sum_hn = carry
        base = g * GROUP_COLS
        normed2 = summed2_s[g]
        scaled = dy[g].astype(F32) * col(base + GAIN_TWO)
        grad2 = (inverse2 * (scaled - mean_e - normed2 * mean_en)).astype(BF16)
        wide = grad2.astype(F32)
        vec[base + DOWN_BIAS] += lane_part(wide)
        for part in range(UNITS // WIDTH):
            rows = slice(part * WIDTH, (part + 1) * WIDTH)
            up_grad = (nn(wdown_t[g, rows, :], grad2) * slope_s[g, rows, :].astype(F32)).astype(BF16)
            up_grad_s[rows, :] = up_grad
            vec[base + UP_BIAS + part] += lane_part(up_grad.astype(F32))
        g_up[g] += nt(hidden_s[g], up_grad_s[...])
        g_down[g] += nt(grad2, act_s[g])
        hidden_grad = (wide + nn(wup[g], up_grad_s[...])).astype(BF16)
        hidden_grad_s[g] = hidden_grad
        grad1 = hidden_grad.astype(F32)
        normed1 = (summed_s[g] - center1) * inverse1
        product = grad1 * normed1
        gain = col(GAIN_ONE + g)
        vec[GAIN_ONE + g] += lane_part(product)
        vec[SHIFT_ONE + g] += lane_part(grad1)
        return sum_h + fold(grad1 * gain), sum_hn + fold(product * gain)

    sum_h, sum_hn = over_groups(feed_back, (zero, zero))
    mean_h = channel_sum(sum_h) / D
    mean_hn = channel_sum(sum_hn) / D

    def norm_back(g, carry):
        normed1 = (summed_s[g] - center1) * inverse1
        scaled = hidden_grad_s[g].astype(F32) * col(GAIN_ONE + g)
        summed_grad = (inverse1 * (scaled - mean_h - normed1 * mean_hn)).astype(BF16)
        summed_grad_s[rows_of(g), :] = summed_grad
        vec[OUT_BIAS + g] += lane_part(summed_grad.astype(F32))
        return carry

    over_groups(norm_back)

    def mix_back(g, carry):
        summed_grad = summed_grad_s[...]
        ctx = ctx_s[pl.ds(g * HEADS_GROUP, HEADS_GROUP)].reshape(WIDTH, SEQ_LEN)
        g_out[rows_of(g), :] += nt(ctx, summed_grad)
        ctx_grad = nn(wout[rows_of(g), :], summed_grad).astype(BF16)
        for h in range(HEADS_GROUP):
            ctx_grad_s[g * HEADS_GROUP + h] = ctx_grad[h * HEAD_DIM : (h + 1) * HEAD_DIM]
        return carry

    over_groups(mix_back)

    def attend_back(h, carry):
        e = e_s[h]
        grad = (ctx_grad_s[h].astype(F32) * linv_s[h]).astype(BF16)
        middle = channel_sum(grad.astype(F32) * ctx_s[h].astype(F32))
        q = q_s[h, 0:HEAD_DIM, :]
        k = k_s[h, 0:HEAD_DIM, :]
        value_grad = nt(grad, e)
        prob_grad = tn(v_s[h], grad)
        score_grad = (e.astype(F32) * (prob_grad - middle)).astype(BF16)
        qkv_grad_s[0, h] = (nn(k, score_grad) * SCALE).astype(BF16)
        qkv_grad_s[1, h] = nt(q, score_grad).astype(BF16)
        qkv_grad_s[2, h] = value_grad.astype(BF16)
        return carry

    lax.fori_loop(0, HEADS, attend_back, 0, unroll=UNROLL)

    def project_back(g, carry):
        base = g * GROUP_COLS
        xg = x[g]
        into = summed_grad_s[rows_of(g), :].astype(F32)
        for part in range(3):
            grads = qkv_grad_s[part, pl.ds(g * HEADS_GROUP, HEADS_GROUP)].reshape(WIDTH, SEQ_LEN)
            columns = slice(part * WIDTH, (part + 1) * WIDTH)
            g_qkv[g, columns, :] += nt(grads, xg)
            into = into + nn(wqkv[g, :, columns], grads)
            if part != 1:
                vec[base + (Q_BIAS if part == 0 else V_BIAS)] += lane_part(grads.astype(F32))
        dx[g] = into.astype(BF16)
        return carry

    over_groups(project_back)

    @pl.when(step == pl.num_programs(0) - 1)
    def _():
        def close(at, carry):
            g_vec[at] = jnp.sum(vec[at].T, axis=0, keepdims=True)
            return carry

        lax.fori_loop(0, COLS, close, 0)


def layer(x, dy, seg, wqkv, wup, wdown, wout, params):
    count = x.shape[1]
    data = pl.BlockSpec((GROUPS, None, WIDTH, SEQ_LEN), lambda i: (0, i, 0, 0))

    def whole(shape):
        return pl.BlockSpec(shape, lambda i: (0,) * len(shape), pipeline_mode=pl.Buffered(1))

    grads = [
        (GROUPS, QKV, WIDTH),
        (GROUPS, WIDTH, UNITS),
        (GROUPS, WIDTH, UNITS),
        (D, D),
        (COLS, 1, WIDTH),
    ]
    token = (GROUPS, WIDTH, SEQ_LEN)
    return pl.pallas_call(
        layer_kernel,
        grid=(count,),
        out_shape=[jax.ShapeDtypeStruct(x.shape, BF16)] * 2 + [jax.ShapeDtypeStruct(s, F32) for s in grads],
        in_specs=[
            data,
            data,
            pl.BlockSpec((None, 1, SEQ_LEN), lambda i: (i, 0, 0)),
        ]
        + [whole(a.shape) for a in (wqkv, wup, wdown, wout, params)],
        out_specs=[data, data] + [whole(s) for s in grads],
        scratch_shapes=[
            pltpu.VMEM((GROUPS, QKV, WIDTH), BF16),
            pltpu.VMEM((GROUPS, UNITS, WIDTH), BF16),
            pltpu.VMEM((GROUPS, UNITS, WIDTH), BF16),
            pltpu.VMEM((D, D), BF16),
            pltpu.VMEM((COLS, WIDTH, 128), F32),
            pltpu.VMEM((COLS, WIDTH, 128), F32),
            pltpu.VMEM((HEADS, PAD, SEQ_LEN), BF16),
            pltpu.VMEM((HEADS, PAD, SEQ_LEN), BF16),
            pltpu.VMEM((HEADS, HEAD_DIM, SEQ_LEN), BF16),
            pltpu.VMEM((HEADS, SEQ_LEN, SEQ_LEN), BF16),
            pltpu.VMEM((HEADS, 1, SEQ_LEN), F32),
            pltpu.VMEM((HEADS, HEAD_DIM, SEQ_LEN), BF16),
            pltpu.VMEM(token, F32),
            pltpu.VMEM(token, BF16),
            pltpu.VMEM((GROUPS, UNITS, SEQ_LEN), BF16),
            pltpu.VMEM((GROUPS, UNITS, SEQ_LEN), BF16),
            pltpu.VMEM(token, F32),
            pltpu.VMEM(token, BF16),
            pltpu.VMEM((UNITS, SEQ_LEN), BF16),
            pltpu.VMEM(token, BF16),
            pltpu.VMEM((D, SEQ_LEN), BF16),
            pltpu.VMEM((HEADS, HEAD_DIM, SEQ_LEN), BF16),
            pltpu.VMEM((3, HEADS, HEAD_DIM, SEQ_LEN), BF16),
        ],
        compiler_params=pltpu.CompilerParams(vmem_limit_bytes=60 << 20),
    )(x, dy, seg, wqkv, wup, wdown, wout, params)


def local(
    layer_input, segment_ids, qkv_weight, qv_bias, out_weight, out_bias, gain_one, shift_one,
    up_weight, up_bias, down_weight, down_bias, gain_two, shift_two, out_grad,
):
    count = layer_input.shape[0] // GROUPS

    def scatter(a):
        a = a.reshape(GROUPS, count, WIDTH, SEQ_LEN)
        return lax.all_to_all(a, "grp", split_axis=0, concat_axis=0, tiled=True)

    own = jnp.concatenate(
        [
            qv_bias.reshape(2, WIDTH),
            up_bias.reshape(UNITS // WIDTH, WIDTH),
            down_bias.reshape(1, WIDTH),
            gain_two.reshape(1, WIDTH),
            shift_two.reshape(1, WIDTH),
        ]
    )
    params = jnp.concatenate(
        [lax.all_gather(own, "grp", axis=0, tiled=True)]
        + [a.reshape(GROUPS, WIDTH) for a in (out_bias, gain_one, shift_one)]
    )
    gather = lambda a: lax.all_gather(a, "grp", axis=0, tiled=True)
    seg = lax.dynamic_slice_in_dim(segment_ids, lax.axis_index("grp") * count, count, 0)
    lo, dx, g_qkv, g_up, g_down, g_out, g_vec = layer(
        scatter(layer_input),
        scatter(out_grad),
        seg[:, None, :],
        gather(qkv_weight),
        gather(up_weight),
        gather(down_weight),
        out_weight,
        params,
    )
    back = lambda a: scatter(a).reshape(layer_input.shape).astype(F32)

    def total(a):
        a = lax.psum_scatter(a, "grp", scatter_dimension=0, tiled=True)
        return lax.psum(a.astype(BF16), "rows").astype(F32)

    g_vec = g_vec[:, 0, :]
    g_vec = lax.psum(g_vec, ("rows", "grp"))
    shared = g_vec[GROUPS * GROUP_COLS :].reshape(3, D)
    mine = lax.dynamic_slice_in_dim(g_vec, lax.axis_index("grp") * GROUP_COLS, GROUP_COLS, 0)
    g_out = lax.psum(g_out, ("rows", "grp"))
    return (
        back(lo),
        back(dx),
        jnp.swapaxes(total(g_qkv), 1, 2),
        mine[Q_BIAS : V_BIAS + 1].reshape(1, 2 * WIDTH),
        g_out,
        shared[0],
        shared[1],
        shared[2],
        total(g_up),
        mine[UP_BIAS:DOWN_BIAS].reshape(1, UNITS),
        total(g_down),
        mine[DOWN_BIAS].reshape(1, WIDTH),
        mine[GAIN_TWO],
        mine[SHIFT_TWO],
    )


def solution(mesh):
    group = P("grp", None, None)
    data = P("rows", "grp", None)
    in_specs = (
        data, P("rows", None), group, P("grp", None), P(), P(), P(), P(),
        group, P("grp", None), group, P("grp", None), P("grp"), P("grp"), data,
    )
    out_specs = (
        data, data, group, P("grp", None), P(), P(), P(), P(),
        group, P("grp", None), group, P("grp", None), P("grp"), P("grp"),
    )
    return jax.shard_map(local, mesh=mesh, in_specs=in_specs, out_specs=out_specs, check_vma=False)
```

time: 1110 us -> 629 us (0.57); the launches traced: 1090 us -> 628 us
  local copies, waits for them, and re-layouts: 307 us -> 12.4 us
  matrix products: 242 us -> 0 us
  Pallas kernels: 0 us -> 148 us
  other arithmetic: 125 us -> 19 us
  blocking collectives: 63.4 us -> 146 us
  waiting for transfers between devices: 308 us -> 275 us
  starting transfers between devices: 29.9 us -> 13.2 us
    dot_general x124 -> x0, matrix products: 242 us -> none  [the longest x4 97.4 us: product(): return jnp.dot(left_side, right_side, preferred_element_type=jnp.float32)]
    pallas_call x0 -> x1, Pallas kernels: none -> 148 us  [layer(): pl.pallas_call(layer_kernel, grid=(count,), out_shape=[jax.ShapeDtypeStru...]
    all_to_all x6 -> x3, waiting for transfers between devices: 178 us -> 42.6 us  [scatter(): return lax.all_to_all(a, 'grp', split_axis=0, concat_axis=0, tiled=True)]
    dynamic_slice x96 -> x1, local copies, waits for them, and re-layouts: 88.7 us -> 0.01 us  [local(): lax.dynamic_slice_in_dim(segment_ids, lax.axis_index('grp') * count, coun...]
    reduce_scatter x0 -> x3, waiting for transfers between devices: none -> 68.7 us  [total(): a = lax.psum_scatter(a, 'grp', scatter_dimension=0, tiled=True)]
    convert_element_type x10 -> x0, local copies, waits for them, and re-layouts: 62.2 us -> none  [the longest x3 28.8 us: local(): hidden_slice_grad = hidden_slice_grad.reshape(-1, D).astype(jnp.float32)]
    reduce_sum x24 -> x0, other arithmetic: 53.4 us -> none  [the longest x16 11.2 us: attend_one(): totals = jnp.sum(weights, axis=-1, keepdims=True)]
    all_gather x0 -> x2, blocking collectives: none -> 52.9 us  [the longest x1 42.7 us: local(): lax.all_gather(own, 'grp', axis=0, tiled=True)]
  transfers between devices with their start and end apart: 10 -> 10, of which waited for: 8 -> 5; matrix products, arithmetic and copies ran while one was open for 26% -> 4% of each run, Pallas kernels for 0% -> 0%
where the time goes in v1:
time: 629 us; the launch traced here: 628 us
  waiting for transfers between devices  275 us (44%)
  Pallas kernels  148 us (24%)
  blocking collectives  146 us (23%)
  other arithmetic  19 us (3%)
  between operations  14.3 us (2%)
  starting transfers between devices  13.2 us (2%)
  local copies, waits for them, and re-layouts  12.4 us (2%)
    pallas_call x1, Pallas kernels, layer(): pl.pallas_call(layer_kernel, grid=(count,), out_shape=[jax.ShapeDtypeStru...  148 us
    psum x1, waiting for transfers between devices, local(): g_out = lax.psum(g_out, ('rows', 'grp'))  135 us
    reduce_scatter x3, waiting for transfers between devices, total(): a = lax.psum_scatter(a, 'grp', scatter_dimension=0, tiled=True)  68.7 us
    all_to_all x1, blocking collectives, scatter(): return lax.all_to_all(a, 'grp', split_axis=0, concat_axis=0, tiled=True)  52.9 us
    all_gather x1, blocking collectives, local(): lax.all_gather(own, 'grp', axis=0, tiled=True)  42.7 us
    all_to_all x3, waiting for transfers between devices, scatter(): return lax.all_to_all(a, 'grp', split_axis=0, concat_axis=0, tiled=True)  42.6 us
    psum x1, blocking collectives, local(): g_vec = lax.psum(g_vec, ('rows', 'grp'))  40.4 us
    psum x1, waiting for transfers between devices, total(): return lax.psum(a.astype(BF16), 'rows').astype(F32)  25.7 us
  transfers between devices with their start and end apart: 10, of which 5 were waited for; matrix products, arithmetic and copies ran while one was open for 4% of the time, Pallas kernels for 0%

profile of v1, /device:TPU:0, one launch (start us, length us, event | category | flops | bytes accessed | tf_op | source)
XLA Modules:
  0.0 628.4 jit_solution(15848614635365389729)
XLA Ops:
  7.2 4.2 all-to-all-start
  11.4 0.7 all-gather.4.cloned.1.call-update
  12.2 42.6 %all-to-all-done.x = bf16[4,4,192,512]{3,2,1,0:T(8,128)(2,1)S(1)} async-done(((bf16[4,4,192,512]{3,2,1,0:T(8,128)(2,1)}), bf16[4,4,192,512]{3,2,1,0:T(8,128)(2,1)S(1)}, u32[]{:S(2)}, u32[]{:S(2)}) %all-to-all-start) | async-done | bytes 3145760 | tf_op jit(solution)/shard_map/all_to_all | solution.py:346
  54.8 1.6 copy-done.1
  56.4 4.6 all-to-all-start.1
  61.1 0.7 all-gather.6.cloned.1.call-update
  62.8 42.7 %all-gather = f32[4,9,192]{2,1,0:T(8,128)S(1)} all-gather(f32[1,9,192]{2,1,0:T(8,128)S(1)} %bitcast.21), channel_id=1, replica_groups=mesh['rows'=8,'grp'=4] {'grp'}, dimensions={0}, use_global_device_ids=true | all-gather | bytes 34560 | tf_op jit(solution)/shard_map/all_gather | solution.py:358
  105.7 0.6 pad_maximum_fusion.params
  106.4 10.2 %all_gather.12.wqkv = bf16[4,192,576]{2,1,0:T(8,128)(2,1)} all-gather(bf16[1,192,576]{2,1,0:T(8,128)(2,1)S(1)} %copy-done.3), channel_id=1, replica_groups=mesh['rows'=8,'grp'=4] {'grp'}, dimensions={0}, use_global_device_ids=true | all-gather | bytes 1105920 | tf_op jit(solution)/shard_map/all_gather | solution.py:361
  116.6 148.3 %shard_map.254 = (bf16[4,4,192,512]{3,2,1,0:T(8,128)(2,1)}, bf16[4,4,192,512]{3,2,1,0:T(8,128)(2,1)}, f32[4,576,192]{2,1,0:T(8,128)}, f32[4,192,768]{2,1,0:T(8,1...) custom-call(bf16[4,4,192,512]{3,2,1,0:T(8,128)(2,1)} %copy-done.1, ...), custom_call_target="tpu_custom_call" | custom-call | tf_op jit(solution)/shard_map/pallas_call | solution.py:298
  266.1 0.7 copy-done.2
  266.8 52.9 %all_to_all.20 = bf16[4,4,192,512]{3,2,1,0:T(8,128)(2,1)} all-to-all(bf16[4,4,192,512]{3,2,1,0:T(8,128)(2,1)S(1)} %copy-done.2), channel_id=1, replica_groups=mesh['rows'=8,'grp'=4] {'grp'}, dimensions={0} | all-to-all | bytes 6291456 | tf_op jit(solution)/shard_map/all_to_all | solution.py:346
  319.6 3.8 all-to-all-start.2
  323.6 1.8 convert_bitcast_fusion
  325.4 35.0 %reduce-scatter.6.cloned.1.call-done = f32[1,192,768]{2,1,0:T(8,128)} async-done(((f32[4,192,768]{2,1,0:T(8,128)}), f32[1,192,768]{2,1,0:T(8,128)}) %reduce-scatter.6.cloned.1.call-update) | async-done | bytes 589840 | tf_op jit(solution)/shard_map/reduce_scatter | solution.py:376
  360.4 1.8 convert_element_type.33
  362.2 33.7 %reduce-scatter.8.cloned.1.call-done = f32[1,192,768]{2,1,0:T(8,128)} async-done(((f32[4,192,768]{2,1,0:T(8,128)}), f32[1,192,768]{2,1,0:T(8,128)}) %reduce-scatter.8.cloned.1.call-update) | async-done | bytes 589840 | tf_op jit(solution)/shard_map/reduce_scatter | solution.py:376
  395.9 1.8 convert_element_type.35
  398.5 40.4 %psum.36 = f32[48,192]{1,0:T(8,128)S(1)} all-reduce(f32[48,192]{1,0:T(8,128)S(1)} %bitcast.20), channel_id=1, replica_groups=mesh['rows'=8,'grp'=4] {'rows','grp'}, use_global_device_ids=true, to_apply=%region_2.0 | all-reduce | flops 9216 | bytes 73728 | tf_op jit(solution)/shard_map/psum | solution.py:380
  439.0 0.7 squeeze.19
  439.6 0.7 squeeze.20
  440.3 0.7 squeeze.21
  441.0 0.7 reshape.84
  441.7 0.6 reshape.83
  442.9 5.5 bitcast_convert_fusion
  448.4 3.8 bitcast_convert_fusion.1
  452.1 25.7 %all-reduce.6.cloned.1.call-done = (bf16[1,192,576]{1,2,0:T(8,128)(2,1)}, bf16[1,192,768]{2,1,0:T(8,128)(2,1)}, bf16[1,192,768]{2,1,0:T(8,128)(2,1)}) async-done(((bf16[1,192,576]{1,2,0:T(8,128)(2,1)}, bf16[1,192,768]{2,1,0:T(8,128)(2,1)}, bf16[1,192,768]{2,1,0:T(8,128)(2,1)}), (bf16[1,192,576]{1,2,0:T(8,128)(2,1)}, bf16[1,192,768]{2,1,0:T(8,128)(2,1)}, ...) | async-done | bytes 811024 | tf_op jit(solution)/shard_map/psum | solution.py:377
  477.8 1.8 convert_element_type.34
  479.6 1.8 convert_element_type.36
  481.4 1.9 copy.31
  483.3 135.0 %all-reduce.4.cloned.1.call-done = f32[768,768]{1,0:T(8,128)} async-done(((f32[768,768]{1,0:T(8,128)}), f32[768,768]{1,0:T(8,128)}) %all-reduce.4.cloned.1.call-update) | async-done | bytes 2359312 | tf_op jit(solution)/shard_map/psum | solution.py:383
  618.4 3.2 copy.39
  (56 shorter events, 3.8 us)
Async XLA Ops:
  7.2 54.7 %copy-start = (s32[16,512]{1,0:T(8,128)S(1)}, s32[16,512]{1,0:T(8,128)}, u32[]{:S(2)}) copy-start(s32[16,512]{1,0:T(8,128)} %param.16) | copy-start | bytes 98308
  7.2 47.6 %all-to-all-start = ((bf16[4,4,192,512]{3,2,1,0:T(8,128)(2,1)}), bf16[4,4,192,512]{3,2,1,0:T(8,128)(2,1)S(1)}, u32[]{:S(2)}, u32[]{:S(2)}) async-start(bf16[4,4,192,512]{3,2,1,0:T(8,128)(2,1)} %bitcast.18), calls=%async_computation | async-start | bytes 6291456 | tf_op jit(solution)/shard_map/all_to_all | solution.py:346
  11.4 105.2 %all-gather.4.cloned.1.call-start = ((), (), s32[]{:S(2)}) async-start(), calls=%async_computation.7 | async-start | bytes 1474560 | tf_op jit(solution)/shard_map/all_gather | solution.py:361
  54.8 1.7 copy-start.1
  54.8 7.8 %copy-start.8 = (f32[1,768]{1,0:T(1,128)S(1)}, f32[1,768]{1,0:T(1,128)}, u32[]{:S(2)}) copy-start(f32[1,768]{1,0:T(1,128)} %param.24) | copy-start | bytes 9220
  54.8 7.9 %copy-start.9 = (f32[1,384]{1,0:T(1,128)S(1)}, f32[1,384]{1,0:T(1,128)}, u32[]{:S(2)}) copy-start(f32[1,384]{1,0:T(1,128)} %param.18) | copy-start | bytes 4612
  54.8 8.0 %copy-start.10 = (f32[1,192]{1,0:T(1,128)S(1)}, f32[1,192]{1,0:T(1,128)}, u32[]{:S(2)}) copy-start(f32[1,192]{1,0:T(1,128)} %param.26) | copy-start | bytes 2308
  54.8 8.0 %copy-start.11 = (f32[192]{0:T(256)S(1)}, f32[192]{0:T(256)}, u32[]{:S(2)}) copy-start(f32[192]{0:T(256)} %param.27) | copy-start | bytes 2308
  54.8 7.9 %copy-start.12 = (f32[192]{0:T(256)S(1)}, f32[192]{0:T(256)}, u32[]{:S(2)}) copy-start(f32[192]{0:T(256)} %param.28) | copy-start | bytes 2308
  54.8 50.7 %copy-start.5 = (f32[768]{0:T(1024)S(1)}, f32[768]{0:T(1024)}, u32[]{:S(2)}) copy-start(f32[768]{0:T(1024)} %param.20) | copy-start | bytes 9220
  54.8 50.8 %copy-start.6 = (f32[768]{0:T(1024)S(1)}, f32[768]{0:T(1024)}, u32[]{:S(2)}) copy-start(f32[768]{0:T(1024)} %param.21) | copy-start | bytes 9220
  54.8 50.8 %copy-start.7 = (f32[768]{0:T(1024)S(1)}, f32[768]{0:T(1024)}, u32[]{:S(2)}) copy-start(f32[768]{0:T(1024)} %param.22) | copy-start | bytes 9220
  54.8 51.5 %copy-start.3 = (bf16[1,192,576]{2,1,0:T(8,128)(2,1)S(1)}, bf16[1,192,576]{2,1,0:T(8,128)(2,1)}, u32[]{:S(2)}) copy-start(bf16[1,192,576]{2,1,0:T(8,128)(2,1)} %param.17) | copy-start | bytes 663556
  56.4 60.2 %all-to-all-start.1 = ((bf16[4,4,192,512]{3,2,1,0:T(8,128)(2,1)}), bf16[4,4,192,512]{3,2,1,0:T(8,128)(2,1)}, u32[]{:S(2)}, u32[]{:S(2)}) async-start(bf16[4,4,192,512]{3,2,1,0:T(8,128)(2,1)} %bitcast.19), calls=%async_computation.1 | async-start | bytes 6291456 | tf_op jit(solution)/shard_map/all_to_all | solution.py:346
  61.1 55.5 %all-gather.6.cloned.1.call-start = ((), (), s32[]{:S(2)}) async-start(), calls=%async_computation.8 | async-start | bytes 1474560 | tf_op jit(solution)/shard_map/all_gather | solution.py:361
  61.8 261.7 %reduce-scatter.4.cloned.1.call-start = ((), (), s32[]{:S(2)}) async-start(), calls=%async_computation.9 | async-start | bytes 2949120 | tf_op jit(solution)/shard_map/reduce_scatter | solution.py:376
  264.9 1.9 copy-start.2
  264.9 95.5 %reduce-scatter.6.cloned.1.call-start = ((), (), s32[]{:S(2)}) async-start(), calls=%async_computation.11 | async-start | bytes 2949120 | tf_op jit(solution)/shard_map/reduce_scatter | solution.py:376
  265.5 130.4 %reduce-scatter.8.cloned.1.call-start = ((), (), s32[]{:S(2)}) async-start(), calls=%async_computation.12 | async-start | bytes 2949120 | tf_op jit(solution)/shard_map/reduce_scatter | solution.py:376
  319.6 128.7 %all-to-all-start.2 = ((bf16[4,4,192,512]{3,2,1,0:T(8,128)(2,1)}), bf16[4,4,192,512]{3,2,1,0:T(8,128)(2,1)S(1)}, u32[]{:S(2)}, u32[]{:S(2)}) async-start(bf16[4,4,192,512]{3,2,1,0:T(8,128)(2,1)} %get-tuple-element.21), calls=%async_computation.2 | async-start | bytes 6291456 | tf_op jit(solution)/shard_map/all_to_all | solution.py:346
  323.5 74.5 %copy-start.4 = (f32[48,1,192]{2,1,0:T(1,128)S(1)}, f32[48,1,192]{2,1,0:T(1,128)}, u32[]{:S(2)}) copy-start(f32[48,1,192]{2,1,0:T(1,128)} %get-tuple-element.24) | copy-start | bytes 110596
  323.5 154.3 %all-reduce.6.cloned.1.call-start = ((), (), s32[]{:S(2)}) async-start(), calls=%async_computation.13 | async-start | bytes 1769472 | tf_op jit(solution)/shard_map/psum | solution.py:377
  397.8 220.6 %all-reduce.4.cloned.1.call-start = ((), (), s32[]{:S(2)}) async-start(), calls=%async_computation.10 | async-start | bytes 4718592 | tf_op jit(solution)/shard_map/psum | solution.py:383
Sparse Core Ops, SparseCore 0:
  13.8 26.5 all-gather.3
  63.5 26.3 all-gather.5
  265.0 46.9 reduce-scatter.3
  314.6 45.8 reduce-scatter.5
  362.8 33.0 reduce-scatter.7
  401.1 76.6 all-reduce.5
  484.3 134.0 all-reduce.3

commit v2 on v1

v2 whole, which is shorter than its diff:
```python
import jax
import jax.numpy as jnp
from jax import lax
from jax.experimental import pallas as pl
from jax.experimental.pallas import tpu as pltpu
from jax.sharding import PartitionSpec as P

D = 768
HEAD_DIM = 64
SEQ_LEN = 512
GROUPS = 4
WIDTH = D // GROUPS
HEADS_GROUP = WIDTH // HEAD_DIM
HEADS = D // HEAD_DIM
QKV = 3 * WIDTH
UNITS = 768
PARTS = UNITS // WIDTH
PAD = HEAD_DIM + 16
MASKED = -1e30
EPS = 1e-05
SCALE = HEAD_DIM ** (-0.5)

F32 = jnp.float32
BF16 = jnp.bfloat16
MESH = pl.DeviceIdType.MESH

Q_BIAS, V_BIAS, UP_BIAS, DOWN_BIAS, GAIN_TWO, SHIFT_TWO, OUT_BIAS, GAIN_ONE, SHIFT_ONE = 0, 1, 2, 6, 7, 8, 9, 10, 11
COLS = 12
TABLE = 16

E_AT = 0
Q_AT = HEADS_GROUP * SEQ_LEN
K_AT = Q_AT + HEADS_GROUP * PAD
V_AT = K_AT + HEADS_GROUP * PAD
FWD_ROWS = V_AT + WIDTH
BWD_ROWS = 2 * WIDTH


def nn(a, b):
    return lax.dot_general(a, b, (((1,), (0,)), ((), ())), preferred_element_type=F32)


def nt(a, b):
    return lax.dot_general(a, b, (((1,), (1,)), ((), ())), preferred_element_type=F32)


def tn(a, b):
    return lax.dot_general(a, b, (((0,), (0,)), ((), ())), preferred_element_type=F32)


def lane_part(value):
    total = value[:, 0:128]
    for at in range(128, SEQ_LEN, 128):
        total = total + value[:, at : at + 128]
    return total


def channel_sum(value):
    return jnp.sum(value, axis=0, keepdims=True)


def fold(value):
    return jnp.sum(value.reshape(value.shape[0] // 8, 8, SEQ_LEN), axis=0)


def spread(column):
    return jnp.concatenate([column] * (SEQ_LEN // 128), axis=1)


def gelu_pair(u):
    half_erf = 0.5 * lax.erf(u * 0.7071067811865476) + 0.5
    density = jnp.exp(u * u * -0.5) * 0.3989422804014327
    return u * half_erf, half_erf + u * density


def flip(me, j):
    return (me + j) % 2 + 2 * ((me // 2 + j // 2) % 2)


def layer_kernel(
    x_in, dy_in, seg, wqkv_in, wup_in, wdown_in, wout, params,
    lo_out, dx_out, fwd_st, bwd_st, g_qkv, g_up, g_down, g_out, g_vec,
    x, dy, wqkv, wup, wdown, table, cols, wqkv_t, wup_t, wdown_t, wout_t, vec,
    fwd, bwd, middle_s, linv_s, ctx_s, summed_s, hidden_s, act_s, slope_s, summed2_s,
    up_grad_s, hidden_grad_s, ctx_grad_s, qkv_grad_s, lo_s,
    s_x, r_x, s_dy, r_dy, s_lo, r_lo, s_dx, r_dx, s_w, r_w, s_fwd, s_bwd,
):
    count = x.shape[0]
    me = lax.axis_index("grp")
    zero = jnp.zeros((8, SEQ_LEN), F32)

    def over(n, body, init=0, unroll=False):
        return lax.fori_loop(0, n, body, init, unroll=unroll)

    def each(n, body):
        def run(at, carry):
            body(at)
            return carry

        lax.fori_loop(0, n, run, 0)

    def remote(src, dst, send, recv, to):
        return pltpu.make_async_remote_copy(
            src_ref=src, dst_ref=dst, send_sem=send, recv_sem=recv, device_id={"grp": to}, device_id_type=MESH
        )

    barrier = pltpu.get_barrier_semaphore()
    for j in range(1, GROUPS):
        pl.semaphore_signal(barrier, inc=1, device_id={"grp": flip(me, j)}, device_id_type=MESH)
    pl.semaphore_wait(barrier, GROUPS - 1)

    def move_in(src, dst, send, recv, i, j):
        to = flip(me, j)
        return remote(src.at[to * count + i], dst.at[i, me], send.at[i, j], recv.at[i, j], to)

    def start_in(src, dst, send, recv, i):
        for j in range(1, GROUPS):
            move_in(src, dst, send, recv, i, j).start()

    def own_in(src, dst, send, i):
        return pltpu.make_async_copy(src.at[me * count + i], dst.at[i, me], send.at[i, 0])

    weights = ((params, table), (wqkv_in.at[0], wqkv), (wup_in.at[0], wup), (wdown_in.at[0], wdown))

    def own_weight(k):
        src, dst = weights[k]
        return pltpu.make_async_copy(src, dst.at[me], s_w.at[k, 0])

    def send_weight(k, j):
        src, dst = weights[k]
        if j < 3:
            return remote(src, dst.at[me], s_w.at[k, j], r_w.at[k, j], flip(me, j))
        got = dst.at[flip(me, 2)]
        return remote(got, got, s_w.at[k, 3], r_w.at[k, 3], flip(me, 1))

    def got_weight(k, j):
        src, dst = weights[k]
        block = dst.at[flip(me, j)]
        remote(block, block, s_w.at[k, j], r_w.at[k, j], flip(me, 1)).wait_recv()

    for k in range(2):
        own_weight(k).start()
        send_weight(k, 2).start()
        send_weight(k, 1).start()
    own_in(x_in, x, s_x, 0).start()
    start_in(x_in, x, s_x, r_x, 0)
    for k in range(2, 4):
        own_weight(k).start()
        send_weight(k, 2).start()
        send_weight(k, 1).start()
    own_in(dy_in, dy, s_dy, 0).start()

    def own_rest(i):
        own_in(x_in, x, s_x, i + 1).start()
        own_in(dy_in, dy, s_dy, i + 1).start()

    each(count - 1, own_rest)

    g_qkv[...] = jnp.zeros_like(g_qkv)
    g_up[...] = jnp.zeros_like(g_up)
    g_down[...] = jnp.zeros_like(g_down)
    g_out[...] = jnp.zeros_like(g_out)
    vec[...] = jnp.zeros_like(vec)
    wout_t[...] = wout[...].T

    own_weight(0).wait()
    got_weight(0, 1)
    got_weight(0, 2)
    send_weight(0, 3).start()
    got_weight(0, 3)
    for g in range(GROUPS):
        cols[g, :, 0:TABLE] = table[g].T

    def col(g, at):
        return cols[g, :, at : at + 1]

    def add_sum(g, at, value):
        vec[g * COLS + at] += lane_part(value)

    def rows_of(g):
        return pl.ds(pl.multiple_of(g * WIDTH, WIDTH), WIDTH)

    def fwd_save(slot, i, g):
        return pltpu.make_async_copy(fwd.at[slot], fwd_st.at[i, g], s_fwd.at[slot])

    def bwd_save(slot, i, g):
        return pltpu.make_async_copy(bwd.at[slot], bwd_st.at[i, g], s_bwd.at[slot])

    def fwd_load(slot, i, g):
        return pltpu.make_async_copy(fwd_st.at[i, g], fwd.at[slot], s_fwd.at[slot])

    def bwd_load(slot, i, g):
        return pltpu.make_async_copy(bwd_st.at[i, g], bwd.at[slot], s_bwd.at[slot])

    def send_lo(i, j):
        to = flip(me, j)
        return remote(lo_s.at[to], lo_out.at[me * count + i], s_lo.at[i, j], r_lo.at[i, j], to)

    def own_lo(i):
        return pltpu.make_async_copy(lo_s.at[me], lo_out.at[me * count + i], s_lo.at[i, 0])

    def sequence(i):
        first = i == 0
        label = seg[pl.ds(me * count + i, 1), :]
        ids = lax.broadcasted_iota(jnp.int32, (16, SEQ_LEN), 0)
        hot = (ids == label).astype(F32)
        hot_k = hot.astype(BF16)
        hot_q = jnp.where(ids < 4, (1.0 - hot) * MASKED, 0.0).astype(BF16)

        def attend(j):
            g = flip(me, j)
            slot = j % 2

            @pl.when(j == 0)
            def _():
                own_in(x_in, x, s_x, i).wait()

            @pl.when(j > 0)
            def _():
                block = x.at[i, g]
                remote(block, block, s_x.at[i, j], r_x.at[i, j], g).wait_recv()

            @pl.when(first & (j == 0))
            def _():
                own_weight(1).wait()

            @pl.when(first & (j == 1))
            def _():
                got_weight(1, 1)

            @pl.when(first & (j == 2))
            def _():
                got_weight(1, 2)
                send_weight(1, 3).start()

            @pl.when(first & (j == 3))
            def _():
                got_weight(1, 3)

            @pl.when(first)
            def _():
                wqkv_t[g] = wqkv[g].T

            @pl.when(i * GROUPS + j >= 2)
            def _():
                fwd_save(slot, 0, 0).wait()

            xg = x[i, g]
            q = (nn(wqkv_t[g, 0:WIDTH, :], xg) + col(g, Q_BIAS)).astype(BF16) * jnp.asarray(SCALE, BF16)
            k = nn(wqkv_t[g, WIDTH : 2 * WIDTH, :], xg).astype(BF16)
            v = (nn(wqkv_t[g, 2 * WIDTH :, :], xg) + col(g, V_BIAS)).astype(BF16)
            fwd[slot, V_AT:FWD_ROWS, :] = v
            for h in range(HEADS_GROUP):
                part = slice(h * HEAD_DIM, (h + 1) * HEAD_DIM)
                qh = jnp.concatenate([q[part], hot_q])
                kh = jnp.concatenate([k[part], hot_k])
                fwd[slot, Q_AT + h * PAD : Q_AT + (h + 1) * PAD, :] = qh
                fwd[slot, K_AT + h * PAD : K_AT + (h + 1) * PAD, :] = kh
                scores = tn(kh, qh)
                largest = jnp.max(scores, axis=0, keepdims=True)
                powers = jnp.exp(scores - largest)
                inverse = 1.0 / channel_sum(powers)
                e = powers.astype(BF16)
                fwd[slot, E_AT + h * SEQ_LEN : E_AT + (h + 1) * SEQ_LEN, :] = e
                linv_s[g * HEADS_GROUP + h] = inverse
                ctx_s[pl.ds(pl.multiple_of(g * WIDTH + h * HEAD_DIM, HEAD_DIM), HEAD_DIM), :] = (
                    nn(v[part], e) * inverse
                ).astype(BF16)
            fwd_save(slot, i, g).start()

        each(GROUPS, attend)

        @pl.when(first)
        def _():
            start_in(dy_in, dy, s_dy, r_dy, 0)
            for k in range(2, 4):
                got_weight(k, 2)
                send_weight(k, 3).start()

        @pl.when(i + 1 < count)
        def _():
            start_in(x_in, x, s_x, r_x, i + 1)

        def mix(g, carry):
            total, square = carry
            branch = (nn(wout_t[rows_of(g), :], ctx_s[...]) + col(g, OUT_BIAS)).astype(BF16)
            summed = branch.astype(F32) + x[i, g].astype(F32)
            summed_s[g] = summed
            return total + fold(summed), square + fold(summed * summed)

        total, square = over(GROUPS, mix, (zero, zero))
        center1 = channel_sum(total) / D
        inverse1 = lax.rsqrt(channel_sum(square) / D - center1 * center1 + EPS)

        @pl.when(first)
        def _():
            for k in range(2, 4):
                own_weight(k).wait()
                got_weight(k, 1)
                got_weight(k, 3)

            def turn(g):
                wup_t[g] = wup[g].T
                wdown_t[g] = wdown[g].T

            each(GROUPS, turn)

        def feed(g, carry):
            total, square = carry
            normed = (summed_s[g] - center1) * inverse1
            hidden = (normed * col(g, GAIN_ONE) + col(g, SHIFT_ONE)).astype(BF16)
            hidden_s[g] = hidden
            for part in range(PARTS):
                rows = slice(part * WIDTH, (part + 1) * WIDTH)
                u = nn(wup_t[g, rows, :], hidden) + col(g, UP_BIAS + part)
                act, slope = gelu_pair(u)
                act_s[g, rows, :] = act.astype(BF16)
                slope_s[g, rows, :] = slope.astype(BF16)
            summed2 = hidden.astype(F32) + nn(wdown[g], act_s[g]) + col(g, DOWN_BIAS)
            summed2_s[g] = summed2
            return total + fold(summed2), square + fold(summed2 * summed2)

        total, square = over(GROUPS, feed, (zero, zero))
        center2 = channel_sum(total) / D
        inverse2 = lax.rsqrt(channel_sum(square) / D - center2 * center2 + EPS)

        @pl.when(i > 0)
        def _():
            own_lo(i - 1).wait()
            for j in range(1, GROUPS):
                send_lo(i - 1, j).wait_send()

        own_in(dy_in, dy, s_dy, i).wait()
        for j in range(1, GROUPS):
            block = dy.at[i, flip(me, j)]
            remote(block, block, s_dy.at[i, j], r_dy.at[i, j], flip(me, j)).wait_recv()

        @pl.when(i + 1 < count)
        def _():
            start_in(dy_in, dy, s_dy, r_dy, i + 1)

        def finish(g, carry):
            sum_e, sum_en = carry
            normed = (summed2_s[g] - center2) * inverse2
            gain = col(g, GAIN_TWO)
            lo_s[g] = (normed * gain + col(g, SHIFT_TWO)).astype(BF16)
            grad = dy[i, g].astype(F32)
            product = grad * normed
            add_sum(g, GAIN_TWO, product)
            add_sum(g, SHIFT_TWO, grad)
            summed2_s[g] = normed
            return sum_e + fold(grad * gain), sum_en + fold(product * gain)

        sum_e, sum_en = over(GROUPS, finish, (zero, zero))
        mean_e = channel_sum(sum_e) / D
        mean_en = channel_sum(sum_en) / D

        own_lo(i).start()
        for j in range(1, GROUPS):
            send_lo(i, j).start()

        def feed_back(g, carry):
            sum_h, sum_hn = carry
            normed2 = summed2_s[g]
            scaled = dy[i, g].astype(F32) * col(g, GAIN_TWO)
            grad2 = (inverse2 * (scaled - mean_e - normed2 * mean_en)).astype(BF16)
            wide = grad2.astype(F32)
            add_sum(g, DOWN_BIAS, wide)
            for part in range(PARTS):
                rows = slice(part * WIDTH, (part + 1) * WIDTH)
                up_grad = (nn(wdown_t[g, rows, :], grad2) * slope_s[g, rows, :].astype(F32)).astype(BF16)
                up_grad_s[rows, :] = up_grad
                add_sum(g, UP_BIAS + part, up_grad.astype(F32))
            g_up[g] += nt(hidden_s[g], up_grad_s[...])
            g_down[g] += nt(grad2, act_s[g])
            hidden_grad = (wide + nn(wup[g], up_grad_s[...])).astype(BF16)
            hidden_grad_s[rows_of(g), :] = hidden_grad
            grad1 = hidden_grad.astype(F32)
            normed1 = (summed_s[g] - center1) * inverse1
            product = grad1 * normed1
            gain = col(g, GAIN_ONE)
            add_sum(g, GAIN_ONE, product)
            add_sum(g, SHIFT_ONE, grad1)
            return sum_h + fold(grad1 * gain), sum_hn + fold(product * gain)

        sum_h, sum_hn = over(GROUPS, feed_back, (zero, zero))
        mean_h = channel_sum(sum_h) / D
        mean_hn = channel_sum(sum_hn) / D

        def norm_back(g):
            normed1 = (summed_s[g] - center1) * inverse1
            scaled = hidden_grad_s[rows_of(g), :].astype(F32) * col(g, GAIN_ONE)
            summed_grad = (inverse1 * (scaled - mean_h - normed1 * mean_hn)).astype(BF16)
            hidden_grad_s[rows_of(g), :] = summed_grad
            add_sum(g, OUT_BIAS, summed_grad.astype(F32))

        each(GROUPS, norm_back)

        def mix_back(g):
            slot = g % 2

            @pl.when(i * GROUPS + g >= 2)
            def _():
                bwd_save(slot, 0, 0).wait()

            ctx = ctx_s[rows_of(g), :]
            g_out[rows_of(g), :] += nt(ctx, hidden_grad_s[...])
            ctx_grad = nn(wout[rows_of(g), :], hidden_grad_s[...]).astype(BF16).astype(F32)
            for h in range(HEADS_GROUP):
                part = slice(h * HEAD_DIM, (h + 1) * HEAD_DIM)
                grad = (ctx_grad[part] * linv_s[g * HEADS_GROUP + h]).astype(BF16)
                bwd[slot, h * HEAD_DIM : (h + 1) * HEAD_DIM, :] = grad
                middle_s[i * HEADS + g * HEADS_GROUP + h] = channel_sum(grad.astype(F32) * ctx[part].astype(F32))
            bwd[slot, WIDTH:BWD_ROWS, :] = hidden_grad_s[rows_of(g), :]
            bwd_save(slot, i, g).start()

        each(GROUPS, mix_back)

    each(count, sequence)
    for slot in range(2):
        fwd_save(slot, 0, 0).wait()
        bwd_save(slot, 0, 0).wait()

    def unit_of(u):
        return u % count, GROUPS - 1 - u // count

    def load(u):
        i, j = unit_of(u)
        g = flip(me, j)
        fwd_load(u % 2, i, g).start()
        bwd_load(u % 2, i, g).start()

    def send_dx(i, j):
        to = flip(me, j)
        return remote(x.at[i, to], dx_out.at[me * count + i], s_dx.at[i, j], r_dx.at[i, j], to)

    def own_dx(i):
        return pltpu.make_async_copy(x.at[i, me], dx_out.at[me * count + i], s_dx.at[i, 0])

    load(0)

    def unit(u):
        i, j = unit_of(u)
        g = flip(me, j)
        slot = u % 2
        fwd_load(slot, i, g).wait()
        bwd_load(slot, i, g).wait()

        @pl.when(u + 1 < count * GROUPS)
        def _():
            load(u + 1)

        for h in range(HEADS_GROUP):
            e = fwd[slot, E_AT + h * SEQ_LEN : E_AT + (h + 1) * SEQ_LEN, :]
            q = fwd[slot, Q_AT + h * PAD : Q_AT + h * PAD + HEAD_DIM, :]
            k = fwd[slot, K_AT + h * PAD : K_AT + h * PAD + HEAD_DIM, :]
            v = fwd[slot, V_AT + h * HEAD_DIM : V_AT + (h + 1) * HEAD_DIM, :]
            grad = bwd[slot, h * HEAD_DIM : (h + 1) * HEAD_DIM, :]
            prob_grad = tn(v, grad)
            score_grad = (e.astype(F32) * (prob_grad - middle_s[i * HEADS + g * HEADS_GROUP + h])).astype(BF16)
            at = h * HEAD_DIM
            qkv_grad_s[2 * WIDTH + at : 2 * WIDTH + at + HEAD_DIM, :] = nt(grad, e).astype(BF16)
            qkv_grad_s[at : at + HEAD_DIM, :] = (nn(k, score_grad) * SCALE).astype(BF16)
            qkv_grad_s[WIDTH + at : WIDTH + at + HEAD_DIM, :] = nt(q, score_grad).astype(BF16)
        g_qkv[g] += nt(qkv_grad_s[...], x[i, g])
        add_sum(g, Q_BIAS, qkv_grad_s[0:WIDTH, :].astype(F32))
        add_sum(g, V_BIAS, qkv_grad_s[2 * WIDTH :, :].astype(F32))
        into = bwd[slot, WIDTH:BWD_ROWS, :].astype(F32) + nn(wqkv[g], qkv_grad_s[...])
        x[i, g] = into.astype(BF16)

        @pl.when(j > 0)
        def _():
            send_dx(i, j).start()

        @pl.when(j == 0)
        def _():
            own_dx(i).start()

    each(count * GROUPS, unit)

    def close(at):
        g_vec[at] = jnp.sum(vec[at].T, axis=0, keepdims=True)

    each(GROUPS * COLS, close)

    for k in range(4):
        for j in (1, 2, 3):
            send_weight(k, j).wait_send()
    own_lo(count - 1).wait()
    for j in range(1, GROUPS):
        send_lo(count - 1, j).wait_send()

    def drain(i):
        own_dx(i).wait()
        for j in range(1, GROUPS):
            move_in(x_in, x, s_x, r_x, i, j).wait_send()
            move_in(dy_in, dy, s_dy, r_dy, i, j).wait_send()
            send_lo(i, j).wait_recv()
            send_dx(i, j).wait_send()
            send_dx(i, j).wait_recv()

    each(count, drain)


def layer(x, dy, seg, wqkv, wup, wdown, wout, params):
    count = x.shape[0] // GROUPS
    here = pl.BlockSpec(memory_space=pl.ANY)
    vmem = pl.BlockSpec(memory_space=pltpu.VMEM)
    grads = [
        (GROUPS, QKV, WIDTH),
        (GROUPS, WIDTH, UNITS),
        (GROUPS, WIDTH, UNITS),
        (D, D),
        (GROUPS * COLS, 1, WIDTH),
    ]
    token = (GROUPS, WIDTH, SEQ_LEN)
    dma = pltpu.SemaphoreType.DMA
    return pl.pallas_call(
        layer_kernel,
        out_shape=[jax.ShapeDtypeStruct(x.shape, BF16)] * 2
        + [
            jax.ShapeDtypeStruct((count, GROUPS, FWD_ROWS, SEQ_LEN), BF16),
            jax.ShapeDtypeStruct((count, GROUPS, BWD_ROWS, SEQ_LEN), BF16),
        ]
        + [jax.ShapeDtypeStruct(s, F32) for s in grads],
        in_specs=[here, here, vmem, here, here, here, vmem, vmem],
        out_specs=[here] * 4 + [vmem] * len(grads),
        scratch_shapes=[
            pltpu.VMEM((count,) + token, BF16),
            pltpu.VMEM((count,) + token, BF16),
            pltpu.VMEM((GROUPS, WIDTH, QKV), BF16),
            pltpu.VMEM((GROUPS, WIDTH, UNITS), BF16),
            pltpu.VMEM((GROUPS, WIDTH, UNITS), BF16),
            pltpu.VMEM((GROUPS, TABLE, WIDTH), F32),
            pltpu.VMEM((GROUPS, WIDTH, 128), F32),
            pltpu.VMEM((GROUPS, QKV, WIDTH), BF16),
            pltpu.VMEM((GROUPS, UNITS, WIDTH), BF16),
            pltpu.VMEM((GROUPS, UNITS, WIDTH), BF16),
            pltpu.VMEM((D, D), BF16),
            pltpu.VMEM((GROUPS * COLS, WIDTH, 128), F32),
            pltpu.VMEM((2, FWD_ROWS, SEQ_LEN), BF16),
            pltpu.VMEM((2, BWD_ROWS, SEQ_LEN), BF16),
            pltpu.VMEM((count * HEADS, 1, SEQ_LEN), F32),
            pltpu.VMEM((HEADS, 1, SEQ_LEN), F32),
            pltpu.VMEM((D, SEQ_LEN), BF16),
            pltpu.VMEM(token, F32),
            pltpu.VMEM(token, BF16),
            pltpu.VMEM((GROUPS, UNITS, SEQ_LEN), BF16),
            pltpu.VMEM((GROUPS, UNITS, SEQ_LEN), BF16),
            pltpu.VMEM(token, F32),
            pltpu.VMEM((UNITS, SEQ_LEN), BF16),
            pltpu.VMEM((D, SEQ_LEN), BF16),
            pltpu.VMEM((D, SEQ_LEN), BF16),
            pltpu.VMEM((QKV, SEQ_LEN), BF16),
            pltpu.VMEM(token, BF16),
        ]
        + [dma((count, GROUPS))] * 8
        + [dma((4, GROUPS))] * 2
        + [dma((2,))] * 2,
        compiler_params=pltpu.CompilerParams(
            vmem_limit_bytes=63 << 20, collective_id=0, has_side_effects=True
        ),
    )(x, dy, seg, wqkv, wup, wdown, wout, params)


def local(
    layer_input, segment_ids, qkv_weight, qv_bias, out_weight, out_bias, gain_one, shift_one,
    up_weight, up_bias, down_weight, down_bias, gain_two, shift_two, out_grad,
):
    me = lax.axis_index("grp")

    def rows(a):
        return a.reshape(-1, WIDTH)

    def mine_of(a):
        return lax.dynamic_slice_in_dim(a, me * WIDTH, WIDTH, 0).reshape(1, WIDTH)

    params = jnp.concatenate(
        [rows(a) for a in (qv_bias, up_bias, down_bias, gain_two, shift_two)]
        + [mine_of(a) for a in (out_bias, gain_one, shift_one)]
        + [jnp.zeros((TABLE - COLS, WIDTH), F32)]
    )
    lo, dx, _, _, g_qkv, g_up, g_down, g_out, g_vec = layer(
        layer_input, out_grad, segment_ids, qkv_weight, up_weight, down_weight, out_weight, params
    )

    def total(a):
        a = lax.psum_scatter(a, "grp", scatter_dimension=0, tiled=True)
        return lax.psum(a.astype(BF16), "rows").astype(F32)

    g_vec = lax.psum(g_vec[:, 0, :], ("rows", "grp")).reshape(GROUPS, COLS, WIDTH)
    mine = lax.dynamic_slice_in_dim(g_vec, me, 1, 0)[0]
    g_out = lax.psum(g_out, ("rows", "grp"))
    return (
        lo.astype(F32),
        dx.astype(F32),
        jnp.swapaxes(total(g_qkv), 1, 2),
        mine[Q_BIAS : V_BIAS + 1].reshape(1, 2 * WIDTH),
        g_out,
        g_vec[:, OUT_BIAS].reshape(D),
        g_vec[:, GAIN_ONE].reshape(D),
        g_vec[:, SHIFT_ONE].reshape(D),
        total(g_up),
        mine[UP_BIAS:DOWN_BIAS].reshape(1, UNITS),
        total(g_down),
        mine[DOWN_BIAS].reshape(1, WIDTH),
        mine[GAIN_TWO],
        mine[SHIFT_TWO],
    )


def solution(mesh):
    group = P("grp", None, None)
    data = P("rows", "grp", None)
    in_specs = (
        data, P("rows", None), group, P("grp", None), P(), P(), P(), P(),
        group, P("grp", None), group, P("grp", None), P("grp"), P("grp"), data,
    )
    out_specs = (
        data, data, group, P("grp", None), P(), P(), P(), P(),
        group, P("grp", None), group, P("grp", None), P("grp"), P("grp"),
    )
    return jax.shard_map(local, mesh=mesh, in_specs=in_specs, out_specs=out_specs, check_vma=False)
```

time: 629 us -> 439 us (0.70)
  blocking collectives: 146 us -> 39.9 us
  waiting for transfers between devices: 275 us -> 184 us
  Pallas kernels: 148 us -> 169 us
  starting transfers between devices: 13.2 us -> 0.2 us
    psum x1, waiting for transfers between devices: 135 us -> 0.63 us  [local(): g_out = lax.psum(g_out, ('rows', 'grp'))]
    psum x1, waiting for transfers between devices: 25.7 us -> 79.9 us  [total(): return lax.psum(a.astype(BF16), 'rows').astype(F32)]
    all_gather x2 -> x0, blocking collectives: 52.9 us -> none  [the longest x1 42.7 us: local(): lax.all_gather(own, 'grp', axis=0, tiled=True)]
    all_to_all x1 -> x0, blocking collectives: 52.9 us -> none  [scatter(): return lax.all_to_all(a, 'grp', split_axis=0, concat_axis=0, tiled=True)]
    all_to_all x3 -> x0, waiting for transfers between devices: 42.6 us -> none  [scatter(): return lax.all_to_all(a, 'grp', split_axis=0, concat_axis=0, tiled=True)]
    reduce_scatter x3, waiting for transfers between devices: 68.7 us -> 102 us  [total(): a = lax.psum_scatter(a, 'grp', scatter_dimension=0, tiled=True)]
    pallas_call x1, Pallas kernels: 148 us -> 169 us  [layer(): pl.pallas_call(layer_kernel, out_shape=[jax.ShapeDtypeStruct(x.shape, BF1...]
    all_to_all x3 -> x0, starting transfers between devices: 12.7 us -> none  [scatter(): return lax.all_to_all(a, 'grp', split_axis=0, concat_axis=0, tiled=True)]
  transfers between devices with their start and end apart: 10 -> 5, of which waited for: 5 -> 5; matrix products, arithmetic and copies ran while one was open for 4% -> 4% of each run, Pallas kernels for 0% -> 0%
where the time goes in v2:
time: 439 us
  waiting for transfers between devices  184 us (42%)
  Pallas kernels  169 us (38%)
  blocking collectives  39.9 us (9%)
  other arithmetic  17.7 us (4%)
  between operations  15.3 us (3%)
  local copies, waits for them, and re-layouts  12.3 us (3%)
    pallas_call x1, Pallas kernels, layer(): pl.pallas_call(layer_kernel, out_shape=[jax.ShapeDtypeStruct(x.shape, BF1...  169 us
    reduce_scatter x3, waiting for transfers between devices, total(): a = lax.psum_scatter(a, 'grp', scatter_dimension=0, tiled=True)  102 us
    psum x1, waiting for transfers between devices, total(): return lax.psum(a.astype(BF16), 'rows').astype(F32)  79.9 us
    psum x1, blocking collectives, local(): lax.psum(g_vec[:, 0, :], ('rows', 'grp')).reshape(GROUPS, COLS, WIDTH)  39.9 us
  transfers between devices with their start and end apart: 5, of which 5 were waited for; matrix products, arithmetic and copies ran while one was open for 4% of the time, Pallas kernels for 0%

profile of v2, /device:TPU:0, one launch (start us, length us, event | category | flops | bytes accessed | tf_op | source)
XLA Modules:
  0.0 438.8 jit_solution(18356493105212389545)
XLA Ops:
  8.1 0.8 dynamic_slice.12
  8.8 0.8 dynamic_slice.13
  9.6 0.8 dynamic_slice.14
  10.3 0.7 reduce.1
  11.1 0.7 reduce
  11.9 2.6 concatenate.3.params
  14.5 169.4 %shard_map.254 = (bf16[16,192,512]{2,1,0:T(8,128)(2,1)}, bf16[16,192,512]{2,1,0:T(8,128)(2,1)}, bf16[4,4,2208,512]{3,2,1,0:T(8,128)(2,1)}, bf16[4,4,384,512]{3,2...) custom-call(bf16[16,192,512]{2,1,0:T(8,128)(2,1)} %x_in.1, ...), custom_call_target="tpu_custom_call" | custom-call | tf_op jit(solution)/shard_map/pallas_call | solution.py:518
  184.0 0.7 reduce-scatter.6.cloned.1.call-update
  184.7 0.7 reduce-scatter.8.cloned.1.call-update
  185.5 0.5 all-reduce.4.cloned.1.call-update
  186.0 32.9 %reduce-scatter.4.cloned.1.call-done = f32[1,576,192]{2,1,0:T(8,128)} async-done(((f32[4,576,192]{2,1,0:T(8,128)}), f32[1,576,192]{2,1,0:T(8,128)}) %reduce-scatter.4.cloned.1.call-update) | async-done | bytes 442384 | tf_op jit(solution)/shard_map/reduce_scatter | solution.py:588
  218.9 1.8 convert_bitcast_fusion
  220.7 34.5 %reduce-scatter.6.cloned.1.call-done = f32[1,192,768]{2,1,0:T(8,128)} async-done(((f32[4,192,768]{2,1,0:T(8,128)}), f32[1,192,768]{2,1,0:T(8,128)}) %reduce-scatter.6.cloned.1.call-update) | async-done | bytes 589840 | tf_op jit(solution)/shard_map/reduce_scatter | solution.py:588
  255.3 1.8 convert_element_type.25
  257.1 34.1 %reduce-scatter.8.cloned.1.call-done = f32[1,192,768]{2,1,0:T(8,128)} async-done(((f32[4,192,768]{2,1,0:T(8,128)}), f32[1,192,768]{2,1,0:T(8,128)}) %reduce-scatter.8.cloned.1.call-update) | async-done | bytes 589840 | tf_op jit(solution)/shard_map/reduce_scatter | solution.py:588
  291.2 1.8 convert_element_type.27
  293.0 0.1 reduce.2
  293.2 39.9 %psum.36 = f32[4,12,192]{2,1,0:T(8,128)S(1)} all-reduce(f32[4,12,192]{2,1,0:T(8,128)S(1)} %reshape.74), channel_id=1, replica_groups=mesh['rows'=8,'grp'=4] {'rows','grp'}, use_global_device_ids=true, to_apply=%region_2.0 | all-reduce | flops 9216 | bytes 73728 | tf_op jit(solution)/shard_map/psum | solution.py:591
  333.1 0.7 reshape.76
  333.8 0.6 reshape.75
  334.5 0.7 reshape_squeeze.10
  335.2 0.7 reshape_squeeze.11
  335.8 0.7 reshape_squeeze.9
  336.5 3.6 convert_element_type.22
  340.1 3.6 convert_element_type.23
  343.6 0.6 constant_dynamic-slice_fusion.4
  344.2 0.6 all-reduce.4.cloned.1.call-done
  344.8 79.9 %all-reduce.6.cloned.1.call-done = (bf16[1,192,576]{1,2,0:T(8,128)(2,1)}, bf16[1,192,768]{2,1,0:T(8,128)(2,1)}, bf16[1,192,768]{2,1,0:T(8,128)(2,1)}) async-done(((bf16[1,192,576]{1,2,0:T(8,128)(2,1)}, bf16[1,192,768]{2,1,0:T(8,128)(2,1)}, bf16[1,192,768]{2,1,0:T(8,128)(2,1)}), (bf16[1,192,576]{1,2,0:T(8,128)(2,1)}, bf16[1,192,768]{2,1,0:T(8,128)(2,1)}, ...) | async-done | bytes 811024 | tf_op jit(solution)/shard_map/psum | solution.py:589
  424.7 1.8 convert_element_type.26
  426.6 1.8 convert_element_type.28
  428.4 1.9 copy.30
  430.3 1.4 copy.37
  (22 shorter events, 0.5 us)
Async XLA Ops:
  8.0 210.9 %reduce-scatter.4.cloned.1.call-start = ((), (), s32[]{:S(2)}) async-start(), calls=%async_computation.3 | async-start | bytes 2949120 | tf_op jit(solution)/shard_map/reduce_scatter | solution.py:588
  183.9 71.3 %reduce-scatter.6.cloned.1.call-start = ((), (), s32[]{:S(2)}) async-start(), calls=%async_computation.5 | async-start | bytes 2949120 | tf_op jit(solution)/shard_map/reduce_scatter | solution.py:588
  184.7 106.5 %reduce-scatter.8.cloned.1.call-start = ((), (), s32[]{:S(2)}) async-start(), calls=%async_computation.6 | async-start | bytes 2949120 | tf_op jit(solution)/shard_map/reduce_scatter | solution.py:588
  185.4 107.6 %copy-start.3 = (f32[48,1,192]{2,1,0:T(1,128)S(1)}, f32[48,1,192]{2,1,0:T(1,128)}, u32[]{:S(2)}) copy-start(f32[48,1,192]{2,1,0:T(1,128)} %get-tuple-element.24) | copy-start | bytes 110596
  185.4 159.4 %all-reduce.4.cloned.1.call-start = ((), (), s32[]{:S(2)}) async-start(), calls=%async_computation.4 | async-start | bytes 4718592 | tf_op jit(solution)/shard_map/psum | solution.py:593
  185.5 151.0 %copy-start.1 = (bf16[16,192,512]{2,1,0:T(8,128)(2,1)S(1)}, bf16[16,192,512]{2,1,0:T(8,128)(2,1)}, u32[]{:S(2)}) copy-start(bf16[16,192,512]{2,1,0:T(8,128)(2,1)} %get-tuple-element.21) | copy-start | bytes 9437188
  186.0 238.7 %all-reduce.6.cloned.1.call-start = ((), (), s32[]{:S(2)}) async-start(), calls=%async_computation.7 | async-start | bytes 1769472 | tf_op jit(solution)/shard_map/psum | solution.py:589
  336.5 3.6 copy-start
  344.8 85.4 %copy-start.2 = (f32[768,768]{1,0:T(8,128)S(1)}, f32[768,768]{1,0:T(8,128)}, u32[]{:S(2)}) copy-start(f32[768,768]{1,0:T(8,128)} %all-reduce.4.cloned.1.call-done) | copy-start | bytes 7077892
Sparse Core Ops, SparseCore 0:
  184.0 34.8 reduce-scatter.3
  221.4 33.7 reduce-scatter.5
  258.0 33.1 reduce-scatter.7
Sparse Core Ops, SparseCore 1:
  191.4 153.4 all-reduce.3
  349.6 75.1 all-reduce.5

commit v3 on v2

--- a/solution.py
+++ b/solution.py
@@ -1,3 +1,5 @@
+import functools
+
 import jax
 import jax.numpy as jnp
 from jax import lax
@@ -19,6 +21,8 @@
 MASKED = -1e30
 EPS = 1e-05
 SCALE = HEAD_DIM ** (-0.5)
+BLOCKS = 3
+HALF = UNITS // 2
 
 F32 = jnp.float32
 BF16 = jnp.bfloat16
@@ -77,16 +81,23 @@
     return (me + j) % 2 + 2 * ((me // 2 + j // 2) % 2)
 
 
+def owners_of(rows, parts):
+    return max(n for n in range(1, min(rows, parts) + 1) if parts % n == 0)
+
+
 def layer_kernel(
-    x_in, dy_in, seg, wqkv_in, wup_in, wdown_in, wout, params,
-    lo_out, dx_out, fwd_st, bwd_st, g_qkv, g_up, g_down, g_out, g_vec,
+    size, x_in, dy_in, seg, wqkv_in, wup_in, wdown_in, wout, params,
+    lo_out, dx_out, fwd_st, bwd_st, qkv_out, up_out, down_out, mix_l, sums_out, shared_out,
     x, dy, wqkv, wup, wdown, table, cols, wqkv_t, wup_t, wdown_t, wout_t, vec,
     fwd, bwd, middle_s, linv_s, ctx_s, summed_s, hidden_s, act_s, slope_s, summed2_s,
-    up_grad_s, hidden_grad_s, ctx_grad_s, qkv_grad_s, lo_s,
-    s_x, r_x, s_dy, r_dy, s_lo, r_lo, s_dx, r_dx, s_w, r_w, s_fwd, s_bwd,
+    up_grad_s, hidden_grad_s, qkv_grad_s, lo_s,
+    acc, g_qkv, pair_t, pair_l, far_t, far_l, cut_t, cut_l, all_t, all_l,
+    qkv_t, qkv_l, qcut_t, qcut_l, qall_t, qall_l, sum_t, sum_l, sum_row_t, sum_row_l, end_t, end_l, end_row_t, end_row_l,
+    s_x, r_x, s_dy, r_dy, s_lo, r_lo, s_dx, r_dx, s_w, r_w, s_grp, r_grp, s_row, r_row, s_fwd, s_bwd,
 ):
     count = x.shape[0]
     me = lax.axis_index("grp")
+    row = lax.axis_index("rows")
     zero = jnp.zeros((8, SEQ_LEN), F32)
 
     def over(n, body, init=0, unroll=False):
@@ -107,7 +118,12 @@
     barrier = pltpu.get_barrier_semaphore()
     for j in range(1, GROUPS):
         pl.semaphore_signal(barrier, inc=1, device_id={"grp": flip(me, j)}, device_id_type=MESH)
-    pl.semaphore_wait(barrier, GROUPS - 1)
+
+    def greet(k):
+        pl.semaphore_signal(barrier, inc=1, device_id={"rows": (row + k + 1) % size}, device_id_type=MESH)
+
+    each(size - 1, greet)
+    pl.semaphore_wait(barrier, GROUPS - 1 + size - 1)
 
     def move_in(src, dst, send, recv, i, j):
         to = flip(me, j)
@@ -157,9 +173,7 @@
     each(count - 1, own_rest)
 
     g_qkv[...] = jnp.zeros_like(g_qkv)
-    g_up[...] = jnp.zeros_like(g_up)
-    g_down[...] = jnp.zeros_like(g_down)
-    g_out[...] = jnp.zeros_like(g_out)
+    acc[...] = jnp.zeros_like(acc)
     vec[...] = jnp.zeros_like(vec)
     wout_t[...] = wout[...].T
 
@@ -371,8 +385,8 @@
                 up_grad = (nn(wdown_t[g, rows, :], grad2) * slope_s[g, rows, :].astype(F32)).astype(BF16)
                 up_grad_s[rows, :] = up_grad
                 add_sum(g, UP_BIAS + part, up_grad.astype(F32))
-            g_up[g] += nt(hidden_s[g], up_grad_s[...])
-            g_down[g] += nt(grad2, act_s[g])
+            acc[0, g] += nt(hidden_s[g], up_grad_s[...])
+            acc[1, g] += nt(grad2, act_s[g])
             hidden_grad = (wide + nn(wup[g], up_grad_s[...])).astype(BF16)
             hidden_grad_s[rows_of(g), :] = hidden_grad
             grad1 = hidden_grad.astype(F32)
@@ -404,7 +418,7 @@
                 bwd_save(slot, 0, 0).wait()
 
             ctx = ctx_s[rows_of(g), :]
-            g_out[rows_of(g), :] += nt(ctx, hidden_grad_s[...])
+            acc[2, g] += nt(ctx, hidden_grad_s[...])
             ctx_grad = nn(wout[rows_of(g), :], hidden_grad_s[...]).astype(BF16).astype(F32)
             for h in range(HEADS_GROUP):
                 part = slice(h * HEAD_DIM, (h + 1) * HEAD_DIM)
@@ -437,7 +451,192 @@
     def own_dx(i):
         return pltpu.make_async_copy(x.at[i, me], dx_out.at[me * count + i], s_dx.at[i, 0])
 
+    def across(kind, src, dst, j, to):
+        return remote(src, dst, s_grp.at[kind, j], r_grp.at[kind, j], flip(me, to))
+
+    def along(kind, src, dst, k):
+        return pltpu.make_async_remote_copy(
+            src_ref=src, dst_ref=dst, send_sem=s_row.at[kind, k], recv_sem=r_row.at[kind, k],
+            device_id={"rows": (row + k) % size}, device_id_type=MESH,
+        )
+
+    def when(condition, body):
+        if condition is True:
+            body()
+        else:
+            pl.when(condition)(body)
+
+    def owns(at, owners):
+        return True if owners == size else at % size < owners
+
+    def peers(body):
+        each(size - 1, lambda k: body(k + 1))
+
+    def scatter(kind, parts, landing, act):
+        owners = parts.shape[0]
+
+        def one(k):
+            to = (row + k) % size
+            piece = parts.at[to if owners == size else jnp.minimum(to, owners - 1)]
+            when(owns(to, owners), lambda: act(along(kind, piece, landing.at[k], k)))
+
+        peers(one)
+
+    def scatter_got(kind, parts, landing):
+        peers(lambda k: along(kind, parts.at[0], landing.at[k], k).wait_recv())
+
+    def spread_out(kind, piece, landing, act):
+        owners = landing.shape[0]
+        own = row if owners == size else jnp.minimum(row, owners - 1)
+        when(owns(row, owners), lambda: peers(lambda k: act(along(kind, piece, landing.at[own], k))))
+
+    def spread_got(kind, piece, landing):
+        owners = landing.shape[0]
+        peers(
+            lambda k: when(
+                owns(row + size - k, owners), lambda: along(kind, piece, landing.at[0], k).wait_recv()
+            )
+        )
+
+    def start(copy):
+        copy.start()
+
+    def sent(copy):
+        copy.wait_send()
+
+    owners = all_l.shape[0]
+    per_half = owners // 2
+    cut = WIDTH // per_half
+
+    def place(o):
+        return pl.ds(pl.multiple_of(o % per_half * cut, 16), cut)
+
+    def pair_send():
+        for at, bits in enumerate((1, 3)):
+            for b in range(BLOCKS):
+                pair_t[at, b] = acc[b, flip(me, bits)].astype(BF16)
+        across(0, pair_t, pair_l, 1, 1).start()
+        for g in range(GROUPS):
+            for c in range(COLS):
+                sum_t[g, c : c + 1, :] = jnp.sum(vec[g * COLS + c].T, axis=0, keepdims=True)
+            sum_t[g, COLS:TABLE, :] = jnp.zeros((TABLE - COLS, WIDTH), F32)
+        for j in range(1, GROUPS):
+            across(2, sum_t.at[flip(me, j)], sum_l.at[j], j, j).start()
+
+    def far_send():
+        across(0, pair_t, pair_l, 1, 1).wait_recv()
+        for b in range(BLOCKS):
+            far_t[b] = (acc[b, flip(me, 2)] + pair_l[1, b].astype(F32)).astype(BF16)
+        across(0, far_t, far_l, 2, 2).start()
+        total = sum_t[me]
+        for j in range(1, GROUPS):
+            across(2, sum_t.at[0], sum_l.at[j], j, j).wait_recv()
+            total = total + sum_l[j]
+        sum_row_t[...] = total
+        peers(lambda k: along(4, sum_row_t, sum_row_l.at[k], k).start())
+
+    def cut_send():
+        across(0, far_t, far_l, 2, 2).wait_recv()
+        for b in range(BLOCKS):
+            total = acc[b, me] + pair_l[0, b].astype(F32) + far_l[b].astype(F32)
+            for o in range(owners):
+                at = o % per_half * cut
+                side = o // per_half * HALF
+                cut_t[o, b] = total[at : at + cut, side : side + HALF].astype(BF16)
+        scatter(0, cut_t, cut_l, start)
+        total = sum_row_t[...]
+        peers(lambda k: along(4, sum_row_t, sum_row_l.at[k], k).wait_recv())
+        for k in range(1, size):
+            total = total + sum_row_l[k]
+        sums_out[...] = total
+        shared_out[me] = total
+        for j in range(1, GROUPS):
+            across(5, sums_out, shared_out.at[me], j, j).start()
+
+    def all_send():
+        def close():
+            scatter_got(0, cut_t, cut_l)
+            own = row if owners == size else jnp.minimum(row, owners - 1)
+            for b in range(BLOCKS):
+                total = cut_t[own, b].astype(F32)
+                for k in range(1, size):
+                    total = total + cut_l[k, b].astype(F32)
+                all_t[b] = total.astype(BF16)
+                all_l[own, b] = total.astype(BF16)
+
+        when(owns(row, owners), close)
+        spread_out(1, all_t, all_l, start)
+
+    def mix_send():
+        spread_got(1, all_t, all_l)
+        for o in range(owners):
+            rows = slice(o % per_half * cut, o % per_half * cut + cut)
+            side = slice(o // per_half * HALF, o // per_half * HALF + HALF)
+            mix_l[me, rows, side] = all_l[o, 2]
+        across(4, mix_l.at[me], mix_l.at[me], 2, 2).start()
+        across(4, mix_l.at[me], mix_l.at[me], 1, 1).start()
+        for o in range(owners):
+            rows = slice(o % per_half * cut, o % per_half * cut + cut)
+            side = slice(o // per_half * HALF, o // per_half * HALF + HALF)
+            up_out[rows, side] = all_l[o, 0]
+            down_out[rows, side] = all_l[o, 1]
+
+    def mix_forward():
+        block = mix_l.at[flip(me, 2)]
+        across(4, block, block, 2, 2).wait_recv()
+        across(4, block, block, 3, 1).start()
+
+    def mix_close():
+        for j in (1, 3):
+            block = mix_l.at[flip(me, j)]
+            across(4, block, block, j, 1).wait_recv()
+
+    def late_sums(g):
+        rows = [jnp.sum(vec[g * COLS + c].T, axis=0, keepdims=True) for c in (Q_BIAS, V_BIAS)]
+        return jnp.concatenate(rows + [jnp.zeros((6, WIDTH), F32)])
+
+    qowners = qall_l.shape[0]
+    qcut = WIDTH // qowners
+
+    def qkv_cut_send():
+        total = g_qkv[me]
+        sums = late_sums(me)
+        for j in range(1, GROUPS):
+            across(1, qkv_t.at[j - 1], qkv_l.at[j - 1], j, j).wait_recv()
+            across(3, end_t.at[j], end_l.at[j], j, j).wait_recv()
+            total = total + qkv_l[j - 1].astype(F32)
+            sums = sums + end_l[j]
+        for o in range(qowners):
+            qcut_t[o] = total[o * qcut : (o + 1) * qcut].astype(BF16)
+        end_row_t[...] = sums
+        scatter(2, qcut_t, qcut_l, start)
+        peers(lambda k: along(5, end_row_t, end_row_l.at[k], k).start())
+
+    def qkv_all_send():
+        def close():
+            scatter_got(2, qcut_t, qcut_l)
+            own = row if qowners == size else jnp.minimum(row, qowners - 1)
+            total = qcut_t[own].astype(F32)
+            for k in range(1, size):
+                total = total + qcut_l[k].astype(F32)
+            qall_t[...] = total.astype(BF16)
+            qall_l[own] = total.astype(BF16)
+
+        when(owns(row, qowners), close)
+        spread_out(3, qall_t, qall_l, start)
+
+    def qkv_close():
+        peers(lambda k: along(5, end_row_t, end_row_l.at[k], k).wait_recv())
+        sums = end_row_t[...]
+        for k in range(1, size):
+            sums = sums + end_row_l[k]
+        sums_out[0:2, :] = sums[0:2]
+        spread_got(3, qall_t, qall_l)
+        for o in range(qowners):
+            qkv_out[o * qcut : (o + 1) * qcut, :] = qall_l[o]
+
     load(0)
+    pair_send()
 
     def unit(u):
         i, j = unit_of(u)
@@ -462,12 +661,19 @@
             qkv_grad_s[2 * WIDTH + at : 2 * WIDTH + at + HEAD_DIM, :] = nt(grad, e).astype(BF16)
             qkv_grad_s[at : at + HEAD_DIM, :] = (nn(k, score_grad) * SCALE).astype(BF16)
             qkv_grad_s[WIDTH + at : WIDTH + at + HEAD_DIM, :] = nt(q, score_grad).astype(BF16)
-        g_qkv[g] += nt(qkv_grad_s[...], x[i, g])
+        g_qkv[g] += nt(x[i, g], qkv_grad_s[...])
         add_sum(g, Q_BIAS, qkv_grad_s[0:WIDTH, :].astype(F32))
         add_sum(g, V_BIAS, qkv_grad_s[2 * WIDTH :, :].astype(F32))
         into = bwd[slot, WIDTH:BWD_ROWS, :].astype(F32) + nn(wqkv[g], qkv_grad_s[...])
         x[i, g] = into.astype(BF16)
 
+        @pl.when((j > 0) & (i == count - 1))
+        def _():
+            qkv_t[j - 1] = g_qkv[g].astype(BF16)
+            end_t[j] = late_sums(g)
+            across(1, qkv_t.at[j - 1], qkv_l.at[j - 1], j, j).start()
+            across(3, end_t.at[j], end_l.at[j], j, j).start()
+
         @pl.when(j > 0)
         def _():
             send_dx(i, j).start()
@@ -476,12 +682,26 @@
         def _():
             own_dx(i).start()
 
-    each(count * GROUPS, unit)
-
-    def close(at):
-        g_vec[at] = jnp.sum(vec[at].T, axis=0, keepdims=True)
-
-    each(GROUPS * COLS, close)
+    def units(first, last):
+        each(last - first, lambda u: unit(u + first))
+
+    marks = [count * GROUPS * part // 16 for part in (1, 6, 11, 16)]
+    units(0, marks[0])
+    far_send()
+    units(marks[0], marks[1])
+    cut_send()
+    units(marks[1], marks[2])
+    all_send()
+    units(marks[2], marks[3])
+    for j in range(1, GROUPS):
+        across(5, sums_out, shared_out.at[flip(me, j)], j, j).wait_recv()
+        across(5, sums_out, shared_out.at[me], j, j).wait_send()
+    qkv_cut_send()
+    mix_send()
+    mix_forward()
+    qkv_all_send()
+    mix_close()
+    qkv_close()
 
     for k in range(4):
         for j in (1, 2, 3):
@@ -500,29 +720,47 @@
             send_dx(i, j).wait_recv()
 
     each(count, drain)
-
-
-def layer(x, dy, seg, wqkv, wup, wdown, wout, params):
+    across(0, pair_t, pair_l, 1, 1).wait_send()
+    across(0, far_t, far_l, 2, 2).wait_send()
+    for j in range(1, GROUPS):
+        across(1, qkv_t.at[j - 1], qkv_l.at[j - 1], j, j).wait_send()
+        across(2, sum_t.at[0], sum_l.at[j], j, j).wait_send()
+        across(3, end_t.at[j], end_l.at[j], j, j).wait_send()
+        across(4, mix_l.at[me], mix_l.at[me], j, 1).wait_send()
+    scatter(0, cut_t, cut_l, sent)
+    spread_out(1, all_t, all_l, sent)
+    scatter(2, qcut_t, qcut_l, sent)
+    spread_out(3, qall_t, qall_l, sent)
+    peers(lambda k: along(4, sum_row_t, sum_row_l.at[k], k).wait_send())
+    peers(lambda k: along(5, end_row_t, end_row_l.at[k], k).wait_send())
+
+
+def layer(size, x, dy, seg, wqkv, wup, wdown, wout, params):
     count = x.shape[0] // GROUPS
     here = pl.BlockSpec(memory_space=pl.ANY)
     vmem = pl.BlockSpec(memory_space=pltpu.VMEM)
     grads = [
-        (GROUPS, QKV, WIDTH),
-        (GROUPS, WIDTH, UNITS),
-        (GROUPS, WIDTH, UNITS),
-        (D, D),
-        (GROUPS * COLS, 1, WIDTH),
+        ((WIDTH, QKV), BF16),
+        ((WIDTH, UNITS), BF16),
+        ((WIDTH, UNITS), BF16),
+        ((GROUPS, WIDTH, UNITS), BF16),
+        ((TABLE, WIDTH), F32),
+        ((GROUPS, TABLE, WIDTH), F32),
     ]
+    owners = 2 * owners_of(size // 2, WIDTH // 16)
+    piece = (BLOCKS, 2 * WIDTH // owners, HALF)
+    qowners = owners_of(size, WIDTH // 16)
+    qpiece = (WIDTH // qowners, QKV)
     token = (GROUPS, WIDTH, SEQ_LEN)
     dma = pltpu.SemaphoreType.DMA
     return pl.pallas_call(
-        layer_kernel,
+        functools.partial(layer_kernel, size),
         out_shape=[jax.ShapeDtypeStruct(x.shape, BF16)] * 2
         + [
             jax.ShapeDtypeStruct((count, GROUPS, FWD_ROWS, SEQ_LEN), BF16),
             jax.ShapeDtypeStruct((count, GROUPS, BWD_ROWS, SEQ_LEN), BF16),
         ]
-        + [jax.ShapeDtypeStruct(s, F32) for s in grads],
+        + [jax.ShapeDtypeStruct(s, t) for s, t in grads],
         in_specs=[here, here, vmem, here, here, here, vmem, vmem],
         out_specs=[here] * 4 + [vmem] * len(grads),
         scratch_shapes=[
@@ -550,12 +788,37 @@
             pltpu.VMEM(token, F32),
             pltpu.VMEM((UNITS, SEQ_LEN), BF16),
             pltpu.VMEM((D, SEQ_LEN), BF16),
-            pltpu.VMEM((D, SEQ_LEN), BF16),
             pltpu.VMEM((QKV, SEQ_LEN), BF16),
             pltpu.VMEM(token, BF16),
+            pltpu.VMEM((BLOCKS, GROUPS, WIDTH, UNITS), F32),
+            pltpu.VMEM((GROUPS, WIDTH, QKV), F32),
+            pltpu.VMEM((2, BLOCKS, WIDTH, UNITS), BF16),
+            pltpu.VMEM((2, BLOCKS, WIDTH, UNITS), BF16),
+            pltpu.VMEM((BLOCKS, WIDTH, UNITS), BF16),
+            pltpu.VMEM((BLOCKS, WIDTH, UNITS), BF16),
+            pltpu.VMEM((owners,) + piece, BF16),
+            pltpu.VMEM((size,) + piece, BF16),
+            pltpu.VMEM(piece, BF16),
+            pltpu.VMEM((owners,) + piece, BF16),
+            pltpu.VMEM((GROUPS - 1, WIDTH, QKV), BF16),
+            pltpu.VMEM((GROUPS - 1, WIDTH, QKV), BF16),
+            pltpu.VMEM((qowners,) + qpiece, BF16),
+            pltpu.VMEM((size,) + qpiece, BF16),
+            pltpu.VMEM(qpiece, BF16),
+            pltpu.VMEM((qowners,) + qpiece, BF16),
+            pltpu.VMEM((GROUPS, TABLE, WIDTH), F32),
+            pltpu.VMEM((GROUPS, TABLE, WIDTH), F32),
+            pltpu.VMEM((TABLE, WIDTH), F32),
+            pltpu.VMEM((size, TABLE, WIDTH), F32),
+            pltpu.VMEM((GROUPS, 8, WIDTH), F32),
+            pltpu.VMEM((GROUPS, 8, WIDTH), F32),
+            pltpu.VMEM((8, WIDTH), F32),
+            pltpu.VMEM((size, 8, WIDTH), F32),
         ]
         + [dma((count, GROUPS))] * 8
         + [dma((4, GROUPS))] * 2
+        + [dma((6, GROUPS))] * 2
+        + [dma((6, size))] * 2
         + [dma((2,))] * 2,
         compiler_params=pltpu.CompilerParams(
             vmem_limit_bytes=63 << 20, collective_id=0, has_side_effects=True
@@ -564,7 +827,7 @@
 
 
 def local(
-    layer_input, segment_ids, qkv_weight, qv_bias, out_weight, out_bias, gain_one, shift_one,
+    size, layer_input, segment_ids, qkv_weight, qv_bias, out_weight, out_bias, gain_one, shift_one,
     up_weight, up_bias, down_weight, down_bias, gain_two, shift_two, out_grad,
 ):
     me = lax.axis_index("grp")
@@ -580,32 +843,24 @@
         + [mine_of(a) for a in (out_bias, gain_one, shift_one)]
         + [jnp.zeros((TABLE - COLS, WIDTH), F32)]
     )
-    lo, dx, _, _, g_qkv, g_up, g_down, g_out, g_vec = layer(
-        layer_input, out_grad, segment_ids, qkv_weight, up_weight, down_weight, out_weight, params
+    lo, dx, _, _, g_qkv, g_up, g_down, g_out, sums, shared = layer(
+        size, layer_input, out_grad, segment_ids, qkv_weight, up_weight, down_weight, out_weight, params
     )
-
-    def total(a):
-        a = lax.psum_scatter(a, "grp", scatter_dimension=0, tiled=True)
-        return lax.psum(a.astype(BF16), "rows").astype(F32)
-
-    g_vec = lax.psum(g_vec[:, 0, :], ("rows", "grp")).reshape(GROUPS, COLS, WIDTH)
-    mine = lax.dynamic_slice_in_dim(g_vec, me, 1, 0)[0]
-    g_out = lax.psum(g_out, ("rows", "grp"))
     return (
         lo.astype(F32),
         dx.astype(F32),
-        jnp.swapaxes(total(g_qkv), 1, 2),
-        mine[Q_BIAS : V_BIAS + 1].reshape(1, 2 * WIDTH),
-        g_out,
-        g_vec[:, OUT_BIAS].reshape(D),
-        g_vec[:, GAIN_ONE].reshape(D),
-        g_vec[:, SHIFT_ONE].reshape(D),
-        total(g_up),
-        mine[UP_BIAS:DOWN_BIAS].reshape(1, UNITS),
-        total(g_down),
-        mine[DOWN_BIAS].reshape(1, WIDTH),
-        mine[GAIN_TWO],
-        mine[SHIFT_TWO],
+        g_qkv.astype(F32)[None],
+        sums[Q_BIAS : V_BIAS + 1].reshape(1, 2 * WIDTH),
+        g_out.astype(F32).reshape(D, D),
+        shared[:, OUT_BIAS].reshape(D),
+        shared[:, GAIN_ONE].reshape(D),
+        shared[:, SHIFT_ONE].reshape(D),
+        g_up.astype(F32)[None],
+        sums[UP_BIAS:DOWN_BIAS].reshape(1, UNITS),
+        g_down.astype(F32)[None],
+        sums[DOWN_BIAS].reshape(1, WIDTH),
+        sums[GAIN_TWO],
+        sums[SHIFT_TWO],
     )
 
 
@@ -620,4 +875,4 @@
         data, data, group, P("grp", None), P(), P(), P(), P(),
         group, P("grp", None), group, P("grp", None), P("grp"), P("grp"),
     )
-    return jax.shard_map(local, mesh=mesh, in_specs=in_specs, out_specs=out_specs, check_vma=False)
+    return jax.shard_map(functools.partial(local, mesh.shape["rows"]), mesh=mesh, in_specs=in_specs, out_specs=out_specs, check_vma=False)

time: 439 us -> 244 us (0.56)
  waiting for transfers between devices: 184 us -> 0 us
  Pallas kernels: 169 us -> 215 us
  blocking collectives: 39.9 us -> 0 us
  between operations: 15.3 us -> 0.68 us
    reduce_scatter x3 -> x0, waiting for transfers between devices: 102 us -> none  [total(): a = lax.psum_scatter(a, 'grp', scatter_dimension=0, tiled=True)]
    psum x2 -> x0, waiting for transfers between devices: 80.5 us -> none  [the longest x1 79.9 us: total(): return lax.psum(a.astype(BF16), 'rows').astype(F32)]
    pallas_call x1, Pallas kernels: 169 us -> 215 us  [layer(): pl.pallas_call(functools.partial(layer_kernel, size), out_shape=[jax.Shap...]
    psum x1 -> x0, blocking collectives: 39.9 us -> none  [local(): lax.psum(g_vec[:, 0, :], ('rows', 'grp')).reshape(GROUPS, COLS, WIDTH)]
    convert_element_type x4 -> x0, other arithmetic: 7.25 us -> none  [total(): return lax.psum(a.astype(BF16), 'rows').astype(F32)]
  transfers between devices with their start and end apart: 5 -> 0, of which waited for: 5 -> 0; matrix products, arithmetic and copies ran while one was open for 4% -> 0% of each run, Pallas kernels for 0% -> 0%
where the time goes in v3:
time: 244 us; the launch traced here: 243 us
  Pallas kernels  215 us (88%)
  other arithmetic  15.3 us (6%)
  local copies, waits for them, and re-layouts  12.2 us (5%)
    pallas_call x1, Pallas kernels, layer(): pl.pallas_call(functools.partial(layer_kernel, size), out_shape=[jax.Shap...  215 us

profile of v3, /device:TPU:0, one launch (start us, length us, event | category | flops | bytes accessed | tf_op | source)
XLA Modules:
  0.0 242.8 jit_solution(17562637378214114734)
XLA Ops:
  0.7 0.8 dynamic_slice.9
  1.4 0.8 dynamic_slice.10
  2.2 0.8 dynamic_slice.11
  2.9 0.7 reduce
  3.6 0.1 reshape.61
  3.7 0.7 reduce.1
  4.4 0.1 reshape.62
  4.5 2.6 %concatenate.3.params = f32[16,192]{1,0:T(8,128)} concatenate(f32[2,192]{1,0:T(2,128)S(1)} %reshape.61, f32[4,192]{1,0:T(4,128)S(1)} %reshape.62, f32[1,192]{1,0:T(1,128)} %param.26, f32[1,192]{1,0:T(1,128)} %bitcast.22, f32[1,192]{1,0:T(1,128)} %bitcast.23, f32[1,192]{1,0:T(1,128)S(1)} %bitcast.19, f32[1,192]{1,0:T(1,128)S(1)} %bitcast.20, f32[1,192]{1,0:T(1,128)S(1)} %bitcast.21, ...), dimensions={0} | concatenate | bytes 24576 | tf_op jit(solution)/shard_map/concatenate | solution.py:841
  7.1 214.7 %shard_map.254 = (bf16[16,192,512]{2,1,0:T(8,128)(2,1)}, bf16[16,192,512]{2,1,0:T(8,128)(2,1)}, bf16[4,4,2208,512]{3,2,1,0:T(8,128)(2,1)}, bf16[4,4,384,512]{3,2...) custom-call(bf16[16,192,512]{2,1,0:T(8,128)(2,1)} %x_in.1, ...), custom_call_target="tpu_custom_call" | custom-call | tf_op jit(solution)/shard_map/pallas_call | solution.py:756
  221.8 0.0 copy-start.1
  221.8 0.8 slice.24
  222.7 0.6 reshape.68
  223.3 1.3 fusion
  224.6 0.7 slice.28
  225.3 0.7 reshape.71
  226.0 0.9 slice_reduce_fusion
  226.9 0.7 reshape_squeeze.11
  227.6 0.7 reshape_squeeze.10
  228.3 0.7 reshape_squeeze.9
  228.9 1.8 bitcast_convert_fusion.3
  230.7 2.1 bitcast_convert_fusion.1
  232.8 2.8 %bitcast_convert_fusion = f32[768,768]{1,0:T(8,128)} fusion(bf16[4,192,768]{2,1,0:T(8,128)(2,1)} %get-tuple-element.26), kind=kLoop, calls=%fused_computation | loop fusion | flops 589824 | bytes 3538944 | tf_op jit(solution)/shard_map/reshape | solution.py:854
  235.7 0.0 copy-done.1
  235.7 0.0 copy-start
  235.7 3.6 %convert_element_type.4 = f32[16,192,512]{2,1,0:T(8,128)} convert(bf16[16,192,512]{2,1,0:T(8,128)(2,1)S(1)} %copy-done.1) | non-fusion elementwise | flops 1572864 | bytes 9437184 | tf_op jit(solution)/shard_map/convert_element_type | solution.py:850
  239.2 0.0 copy-done
  239.2 3.6 %convert_element_type.5 = f32[16,192,512]{2,1,0:T(8,128)} convert(bf16[16,192,512]{2,1,0:T(8,128)(2,1)S(1)} %copy-done) | non-fusion elementwise | flops 1572864 | bytes 9437184 | tf_op jit(solution)/shard_map/convert_element_type | solution.py:851
  (1 shorter events, 0.0 us)
Async XLA Ops:
  221.8 13.9 %copy-start.1 = (bf16[16,192,512]{2,1,0:T(8,128)(2,1)S(1)}, bf16[16,192,512]{2,1,0:T(8,128)(2,1)}, u32[]{:S(2)}) copy-start(bf16[16,192,512]{2,1,0:T(8,128)(2,1)} %get-tuple-element.22) | copy-start | bytes 9437188
  235.7 3.6 %copy-start = (bf16[16,192,512]{2,1,0:T(8,128)(2,1)S(1)}, bf16[16,192,512]{2,1,0:T(8,128)(2,1)}, u32[]{:S(2)}) copy-start(bf16[16,192,512]{2,1,0:T(8,128)(2,1)} %get-tuple-element.23) | copy-start | bytes 9437188

commit v4 on v2

--- a/solution.py
+++ b/solution.py
@@ -1,3 +1,5 @@
+import functools
+
 import jax
 import jax.numpy as jnp
 from jax import lax
@@ -19,6 +21,8 @@
 MASKED = -1e30
 EPS = 1e-05
 SCALE = HEAD_DIM ** (-0.5)
+BLOCKS = 3
+HALF = UNITS // 2
 
 F32 = jnp.float32
 BF16 = jnp.bfloat16
@@ -77,16 +81,25 @@
     return (me + j) % 2 + 2 * ((me // 2 + j // 2) % 2)
 
 
+def owners_of(rows, parts):
+    return max(n for n in range(1, min(rows, parts) + 1) if parts % n == 0)
+
+
 def layer_kernel(
-    x_in, dy_in, seg, wqkv_in, wup_in, wdown_in, wout, params,
-    lo_out, dx_out, fwd_st, bwd_st, g_qkv, g_up, g_down, g_out, g_vec,
+    size, x_in, dy_in, seg, wqkv_in, wup_in, wdown_in, wout,
+    qv_bias, up_bias, down_bias, gain_two, shift_two, out_bias, gain_one, shift_one,
+    lo_out, dx_out, fwd_st, bwd_st, qkv_out, up_out, down_out, mix_out, sums_out, shared_out,
     x, dy, wqkv, wup, wdown, table, cols, wqkv_t, wup_t, wdown_t, wout_t, vec,
     fwd, bwd, middle_s, linv_s, ctx_s, summed_s, hidden_s, act_s, slope_s, summed2_s,
-    up_grad_s, hidden_grad_s, ctx_grad_s, qkv_grad_s, lo_s,
-    s_x, r_x, s_dy, r_dy, s_lo, r_lo, s_dx, r_dx, s_w, r_w, s_fwd, s_bwd,
+    up_grad_s, hidden_grad_s, qkv_grad_s, lo_s,
+    acc, g_qkv, pair_t, pair_l, side_t, side_l, cut_t, cut_l, far_t, far_l, own_s, all_l,
+    qpair_t, qpair_l, qfar_t, qfar_l, qpiece_t, qpiece_l, qcut_t, qcut_l, qall_l,
+    sum_t, sum_l, sum_row_t, sum_row_l, end_t, end_l, end_row_t, end_row_l,
+    s_x, r_x, s_dy, r_dy, s_lo, r_lo, s_dx, r_dx, s_w, r_w, s_one, r_one, s_row, r_row, s_fwd, s_bwd,
 ):
     count = x.shape[0]
     me = lax.axis_index("grp")
+    row = lax.axis_index("rows")
     zero = jnp.zeros((8, SEQ_LEN), F32)
 
     def over(n, body, init=0, unroll=False):
@@ -104,10 +117,32 @@
             src_ref=src, dst_ref=dst, send_sem=send, recv_sem=recv, device_id={"grp": to}, device_id_type=MESH
         )
 
+    half = row % 2
+    beside = row + 1 - 2 * half
+
+    def half_rows(at):
+        return pl.ds(pl.multiple_of(at * (WIDTH // 2), WIDTH // 2), WIDTH // 2)
+
+    mine_half, other_half = half_rows(half), half_rows(1 - half)
+
+    def across(at, src, dst, j):
+        return remote(src, dst, s_one.at[at], r_one.at[at], flip(me, j))
+
+    def aside(at, src, dst):
+        return pltpu.make_async_remote_copy(
+            src_ref=src, dst_ref=dst, send_sem=s_one.at[at], recv_sem=r_one.at[at],
+            device_id={"rows": beside}, device_id_type=MESH,
+        )
+
     barrier = pltpu.get_barrier_semaphore()
     for j in range(1, GROUPS):
         pl.semaphore_signal(barrier, inc=1, device_id={"grp": flip(me, j)}, device_id_type=MESH)
-    pl.semaphore_wait(barrier, GROUPS - 1)
+
+    def greet(k):
+        pl.semaphore_signal(barrier, inc=1, device_id={"rows": (row + k + 1) % size}, device_id_type=MESH)
+
+    each(size - 1, greet)
+    pl.semaphore_wait(barrier, GROUPS - 1 + size - 1)
 
     def move_in(src, dst, send, recv, i, j):
         to = flip(me, j)
@@ -120,33 +155,53 @@
     def own_in(src, dst, send, i):
         return pltpu.make_async_copy(src.at[me * count + i], dst.at[i, me], send.at[i, 0])
 
-    weights = ((params, table), (wqkv_in.at[0], wqkv), (wup_in.at[0], wup), (wdown_in.at[0], wdown))
+    weights = (None, (wqkv_in.at[0], wqkv), (wup_in.at[0], wup), (wdown_in.at[0], wdown))
 
     def own_weight(k):
         src, dst = weights[k]
         return pltpu.make_async_copy(src, dst.at[me], s_w.at[k, 0])
 
+    def send_table(j):
+        return remote(table.at[me], table.at[me], s_w.at[0, j], r_w.at[0, j], flip(me, j))
+
     def send_weight(k, j):
         src, dst = weights[k]
-        if j < 3:
-            return remote(src, dst.at[me], s_w.at[k, j], r_w.at[k, j], flip(me, j))
+        if j == 1:
+            return remote(src, dst.at[me], s_w.at[k, 1], r_w.at[k, 1], flip(me, 1))
+        if j == 2 and k == 1:
+            return remote(src, dst.at[me], s_w.at[k, 2], r_w.at[k, 2], flip(me, 2))
+        if j == 2:
+            part = weights[k][0].at[mine_half]
+            return remote(part, dst.at[me, mine_half], s_w.at[k, 2], r_w.at[k, 2], flip(me, 2))
         got = dst.at[flip(me, 2)]
         return remote(got, got, s_w.at[k, 3], r_w.at[k, 3], flip(me, 1))
 
+    def pass_weight(k, rows):
+        block = weights[k][1].at[flip(me, 2), rows]
+        return aside(30 + k, block, block)
+
     def got_weight(k, j):
-        src, dst = weights[k]
-        block = dst.at[flip(me, j)]
+        dst = weights[k][1]
+        block = dst.at[flip(me, j)] if j != 2 or k == 1 else dst.at[flip(me, j), mine_half]
         remote(block, block, s_w.at[k, j], r_w.at[k, j], flip(me, 1)).wait_recv()
 
-    for k in range(2):
-        own_weight(k).start()
-        send_weight(k, 2).start()
-        send_weight(k, 1).start()
+    for c in range(2):
+        table[me, c : c + 1, :] = qv_bias[:, c * WIDTH : (c + 1) * WIDTH]
+    for c in range(PARTS):
+        table[me, UP_BIAS + c : UP_BIAS + c + 1, :] = up_bias[:, c * WIDTH : (c + 1) * WIDTH]
+    table[me, DOWN_BIAS : DOWN_BIAS + 1, :] = down_bias[...]
+    table[me, GAIN_TWO : GAIN_TWO + 1, :] = gain_two[...].reshape(1, WIDTH)
+    table[me, SHIFT_TWO : SHIFT_TWO + 1, :] = shift_two[...].reshape(1, WIDTH)
+    table[me, OUT_BIAS:TABLE, :] = jnp.zeros((TABLE - OUT_BIAS, WIDTH), F32)
+    for j in (2, 3, 1):
+        send_table(j).start()
+    own_weight(1).start()
+    send_weight(1, 2).start()
+    send_weight(1, 1).start()
     own_in(x_in, x, s_x, 0).start()
     start_in(x_in, x, s_x, r_x, 0)
     for k in range(2, 4):
         own_weight(k).start()
-        send_weight(k, 2).start()
         send_weight(k, 1).start()
     own_in(dy_in, dy, s_dy, 0).start()
 
@@ -157,19 +212,17 @@
     each(count - 1, own_rest)
 
     g_qkv[...] = jnp.zeros_like(g_qkv)
-    g_up[...] = jnp.zeros_like(g_up)
-    g_down[...] = jnp.zeros_like(g_down)
-    g_out[...] = jnp.zeros_like(g_out)
+    acc[...] = jnp.zeros_like(acc)
     vec[...] = jnp.zeros_like(vec)
     wout_t[...] = wout[...].T
 
-    own_weight(0).wait()
-    got_weight(0, 1)
-    got_weight(0, 2)
-    send_weight(0, 3).start()
-    got_weight(0, 3)
+    for j in range(1, GROUPS):
+        block = table.at[flip(me, j)]
+        remote(block, block, s_w.at[0, j], r_w.at[0, j], flip(me, j)).wait_recv()
     for g in range(GROUPS):
-        cols[g, :, 0:TABLE] = table[g].T
+        vectors = [a[...].reshape(1, D)[:, g * WIDTH : (g + 1) * WIDTH] for a in (out_bias, gain_one, shift_one)]
+        rows = jnp.concatenate([table[g, 0:OUT_BIAS, :]] + vectors + [jnp.zeros((TABLE - COLS, WIDTH), F32)])
+        cols[g, :, 0:TABLE] = rows.T
 
     def col(g, at):
         return cols[g, :, at : at + 1]
@@ -232,6 +285,8 @@
             def _():
                 got_weight(1, 2)
                 send_weight(1, 3).start()
+                for k in range(2, 4):
+                    send_weight(k, 2).start()
 
             @pl.when(first & (j == 3))
             def _():
@@ -275,7 +330,7 @@
             start_in(dy_in, dy, s_dy, r_dy, 0)
             for k in range(2, 4):
                 got_weight(k, 2)
-                send_weight(k, 3).start()
+                pass_weight(k, mine_half).start()
 
         @pl.when(i + 1 < count)
         def _():
@@ -297,6 +352,9 @@
             for k in range(2, 4):
                 own_weight(k).wait()
                 got_weight(k, 1)
+                pass_weight(k, other_half).wait_recv()
+                send_weight(k, 3).start()
+            for k in range(2, 4):
                 got_weight(k, 3)
 
             def turn(g):
@@ -371,8 +429,8 @@
                 up_grad = (nn(wdown_t[g, rows, :], grad2) * slope_s[g, rows, :].astype(F32)).astype(BF16)
                 up_grad_s[rows, :] = up_grad
                 add_sum(g, UP_BIAS + part, up_grad.astype(F32))
-            g_up[g] += nt(hidden_s[g], up_grad_s[...])
-            g_down[g] += nt(grad2, act_s[g])
+            acc[0, g] += nt(hidden_s[g], up_grad_s[...])
+            acc[1, g] += nt(grad2, act_s[g])
             hidden_grad = (wide + nn(wup[g], up_grad_s[...])).astype(BF16)
             hidden_grad_s[rows_of(g), :] = hidden_grad
             grad1 = hidden_grad.astype(F32)
@@ -404,7 +462,7 @@
                 bwd_save(slot, 0, 0).wait()
 
             ctx = ctx_s[rows_of(g), :]
-            g_out[rows_of(g), :] += nt(ctx, hidden_grad_s[...])
+            acc[2, g] += nt(ctx, hidden_grad_s[...])
             ctx_grad = nn(wout[rows_of(g), :], hidden_grad_s[...]).astype(BF16).astype(F32)
             for h in range(HEADS_GROUP):
                 part = slice(h * HEAD_DIM, (h + 1) * HEAD_DIM)
@@ -437,7 +495,306 @@
     def own_dx(i):
         return pltpu.make_async_copy(x.at[i, me], dx_out.at[me * count + i], s_dx.at[i, 0])
 
+    def when(condition, body):
+        if condition is True:
+            body()
+        else:
+            pl.when(condition)(body)
+
+    depth = size // 2
+    level = row // 2
+    owners = all_l.shape[1]
+    per_half = owners // 2
+    cut = WIDTH // 2 // per_half
+    pair_groups = (flip(me, 1), flip(me, 3))
+    kept = (me, flip(me, 2))
+    outs = (up_out, down_out, None)
+
+    def peers(n, body):
+        def run(k):
+            body(k + 1)
+
+        each(n - 1, run)
+
+    def along(kind, src, dst, k, sided):
+        to = (level + k) % depth * 2 + half if sided else (row + k) % size
+        return pltpu.make_async_remote_copy(
+            src_ref=src, dst_ref=dst, send_sem=s_row.at[kind, k], recv_sem=r_row.at[kind, k],
+            device_id={"rows": to}, device_id_type=MESH,
+        )
+
+    def line(sided):
+        return (depth, level) if sided else (size, row)
+
+    def capped(at, n, length):
+        return at if n == length else jnp.minimum(at, n - 1)
+
+    def owns(at, n, length):
+        return True if n == length else at < n
+
+    def scatter(kind, parts, landing, sided, act):
+        n = parts.shape[0]
+        length, here = line(sided)
+
+        def one(k):
+            to = (here + k) % length
+            piece = parts.at[capped(to, n, length)]
+            when(owns(to, n, length), lambda: act(along(kind, piece, landing.at[k], k, sided)))
+
+        peers(length, one)
+
+    def scatter_got(kind, parts, landing, sided):
+        peers(line(sided)[0], lambda k: along(kind, parts.at[0], landing.at[k], k, sided).wait_recv())
+
+    def spread_out(kind, landing, sided, act):
+        n = landing.shape[0]
+        length, here = line(sided)
+        own = landing.at[capped(here, n, length)]
+        when(owns(here, n, length), lambda: peers(length, lambda k: act(along(kind, own, own, k, sided))))
+
+    def spread_got(kind, landing, sided):
+        n = landing.shape[0]
+        length, here = line(sided)
+        peers(
+            length,
+            lambda k: when(
+                owns((here + length - k) % length, n, length),
+                lambda: along(kind, landing.at[0], landing.at[0], k, sided).wait_recv(),
+            ),
+        )
+
+    def start(copy):
+        copy.start()
+
+    def sent(copy):
+        copy.wait_send()
+
+    def pair_copy(b):
+        return across(b, pair_t.at[b], pair_l.at[b], 1)
+
+    def side_copy(b):
+        return aside(3 + b, side_t.at[b], side_l.at[b])
+
+    def far_copy(b):
+        return across(6 + b, far_t.at[b], far_l.at[b], 2)
+
+    def out_copy(b, rows):
+        return aside(9 + b, outs[b].at[rows], outs[b].at[rows])
+
+    def pair_send(b):
+        for at in range(2):
+            pair_t[b, at] = acc[b, pair_groups[at]].astype(BF16)
+        pair_copy(b).start()
+
+    def side_send(b):
+        pair_copy(b).wait_recv()
+        for at in range(2):
+            acc[b, kept[at]] += pair_l[b, at].astype(F32)
+            side_t[b, at] = acc[b, kept[at], other_half, :].astype(BF16)
+        side_copy(b).start()
+
+    def cut_send(b):
+        side_copy(b).wait_recv()
+        for at in range(2):
+            total = acc[b, kept[at], mine_half, :] + side_l[b, at].astype(F32)
+            for o in range(owners):
+                rows = o % per_half * cut
+                lanes = o // per_half * HALF
+                cut_t[b, o, at] = total[rows : rows + cut, lanes : lanes + HALF].astype(BF16)
+        scatter(b, cut_t.at[b], cut_l.at[b], True, start)
+
+    def far_send(b):
+        def close():
+            scatter_got(b, cut_t.at[b], cut_l.at[b], True)
+            own = capped(level, owners, depth)
+            total = [cut_t[b, own, at].astype(F32) for at in range(2)]
+            for k in range(1, depth):
+                total = [total[at] + cut_l[b, k, at].astype(F32) for at in range(2)]
+            own_s[b] = total[0]
+            far_t[b] = total[1].astype(BF16)
+            far_copy(b).start()
+
+        when(owns(level, owners, depth), close)
+
+    def all_send(b):
+        def close():
+            far_copy(b).wait_recv()
+            all_l[b, capped(level, owners, depth)] = (own_s[b] + far_l[b].astype(F32)).astype(BF16)
+
+        when(owns(level, owners, depth), close)
+        spread_out(3 + b, all_l.at[b], True, start)
+
+    def joined(b):
+        spread_got(3 + b, all_l.at[b], True)
+        sides = [
+            jnp.concatenate([all_l[b, side * per_half + o] for o in range(per_half)]) for side in range(2)
+        ]
+        return jnp.concatenate(sides, axis=1)
+
+    def out_send(b):
+        outs[b][mine_half, :] = joined(b)
+        out_copy(b, mine_half).start()
+
+    def mix_part(g, rows):
+        return mix_out.at[g, rows]
+
+    def mix_far(g):
+        return across(12, mix_part(g, mine_half), mix_part(g, mine_half), 2)
+
+    def mix_beside(at, rows):
+        return aside(13 + at, mix_part(kept[at], rows), mix_part(kept[at], rows))
+
+    def mix_core(at, g):
+        return across(15 + at, mix_out.at[g], mix_out.at[g], 1)
+
+    def mix_far_send():
+        mix_out[me, mine_half, :] = joined(2)
+        mix_far(me).start()
+        mix_beside(0, mine_half).start()
+
+    def mix_beside_send():
+        mix_far(flip(me, 2)).wait_recv()
+        mix_beside(1, mine_half).start()
+
+    def mix_core_send():
+        for at in range(2):
+            mix_beside(at, other_half).wait_recv()
+            mix_core(at, kept[at]).start()
+
+    def early_copy(j):
+        return across(17 + j, sum_t.at[flip(me, j)], sum_l.at[j], j)
+
+    def shared_copy(j):
+        return across(20 + j, shared_out.at[me], shared_out.at[me], j)
+
+    def end_copy(j):
+        return across(23 + j, end_t.at[j], end_l.at[j], j)
+
+    def lane_rows(g, columns):
+        return [jnp.sum(vec[g * COLS + c].T, axis=0, keepdims=True) for c in columns]
+
+    def early_send():
+        for g in range(GROUPS):
+            zeros = [jnp.zeros((1, WIDTH), F32)] * 2
+            rows = zeros + lane_rows(g, range(UP_BIAS, COLS)) + zeros * ((TABLE - COLS) // 2)
+            sum_t[g] = jnp.concatenate(rows)
+        for j in range(1, GROUPS):
+            early_copy(j).start()
+
+    def early_row_send():
+        total = sum_t[me]
+        for j in range(1, GROUPS):
+            early_copy(j).wait_recv()
+            total = total + sum_l[j]
+        sum_row_t[...] = total
+        peers(size, lambda k: along(8, sum_row_t, sum_row_l.at[k], k, False).start())
+
+    def shared_send():
+        total = sum_row_t[...]
+        peers(size, lambda k: along(8, sum_row_t, sum_row_l.at[k], k, False).wait_recv())
+        for k in range(1, size):
+            total = total + sum_row_l[k]
+        sums_out[...] = total
+        shared_out[me] = total
+        for j in range(1, GROUPS):
+            shared_copy(j).start()
+
+    qowners = qall_l.shape[0]
+    qcut = WIDTH // qowners
+
+    def qpair_copy(at):
+        return across(27 + at, qpair_t.at[at], qpair_l.at[at], 1)
+
+    def qpiece_copy():
+        return across(29, qpiece_t, qpiece_l, 2)
+
+    def qpair_send(at, j):
+        qpair_t[at] = g_qkv[flip(me, j)].astype(BF16)
+        qpair_copy(at).start()
+
+    def qpieces(at, g, parts, landing, kind):
+        qpair_copy(at).wait_recv()
+        for o in range(qowners):
+            rows = slice(o * qcut, (o + 1) * qcut)
+            parts[o] = (g_qkv[g, rows, :] + qpair_l[at, rows, :].astype(F32)).astype(BF16)
+        scatter(kind, parts, landing, False, start)
+
+    def qtotal(parts, landing, kind):
+        scatter_got(kind, parts, landing, False)
+        total = parts[capped(row, qowners, size)].astype(F32)
+        for k in range(1, size):
+            total = total + landing[k].astype(F32)
+        return total
+
+    def qfar_send():
+        qpieces(0, flip(me, 2), qfar_t, qfar_l, 6)
+
+    def qpiece_send():
+        def close():
+            qpiece_t[...] = qtotal(qfar_t, qfar_l, 6).astype(BF16)
+            qpiece_copy().start()
+
+        when(owns(row, qowners, size), close)
+
+    def end_sums(g):
+        return jnp.concatenate(lane_rows(g, (Q_BIAS, V_BIAS)) + [jnp.zeros((6, WIDTH), F32)])
+
+    def qcut_send():
+        qpieces(1, me, qcut_t, qcut_l, 7)
+        sums = end_sums(me)
+        for j in range(1, GROUPS):
+            end_copy(j).wait_recv()
+            sums = sums + end_l[j]
+        end_row_t[...] = sums
+        peers(size, lambda k: along(9, end_row_t, end_row_l.at[k], k, False).start())
+
+    def qall_send():
+        def close():
+            total = qtotal(qcut_t, qcut_l, 7)
+            qpiece_copy().wait_recv()
+            qall_l[capped(row, qowners, size)] = (total + qpiece_l[...].astype(F32)).astype(BF16)
+
+        when(owns(row, qowners, size), close)
+        spread_out(10, qall_l, False, start)
+
+    def qclose():
+        peers(size, lambda k: along(9, end_row_t, end_row_l.at[k], k, False).wait_recv())
+        sums = end_row_t[...]
+        for k in range(1, size):
+            sums = sums + end_row_l[k]
+        sums_out[0:2, :] = sums[0:2]
+        spread_got(10, qall_l, False)
+        for o in range(qowners):
+            qkv_out[o * qcut : (o + 1) * qcut, :] = qall_l[o]
+
+    UP, DOWN, MIX = 0, 1, 2
+    plan = {
+        1: [lambda: side_send(MIX), early_row_send],
+        2: [lambda: side_send(UP)],
+        4: [lambda: qpair_send(0, 3), lambda: side_send(DOWN)],
+        5: [lambda: cut_send(MIX), shared_send],
+        7: [lambda: cut_send(UP)],
+        8: [qfar_send],
+        9: [lambda: far_send(MIX), lambda: cut_send(DOWN)],
+        11: [lambda: all_send(MIX), lambda: far_send(UP)],
+        12: [lambda: qpair_send(1, 1), lambda: all_send(UP)],
+        13: [qpiece_send, lambda: far_send(DOWN), mix_far_send],
+        14: [lambda: out_send(UP), lambda: all_send(DOWN)],
+        15: [mix_beside_send],
+    }
+
+    def follow(u):
+        for at, steps in plan.items():
+
+            @pl.when(u == count * GROUPS * at // 16 - 1)
+            def _():
+                for step in steps:
+                    step()
+
     load(0)
+    for b in (MIX, UP, DOWN):
+        pair_send(b)
+    early_send()
 
     def unit(u):
         i, j = unit_of(u)
@@ -462,12 +819,17 @@
             qkv_grad_s[2 * WIDTH + at : 2 * WIDTH + at + HEAD_DIM, :] = nt(grad, e).astype(BF16)
             qkv_grad_s[at : at + HEAD_DIM, :] = (nn(k, score_grad) * SCALE).astype(BF16)
             qkv_grad_s[WIDTH + at : WIDTH + at + HEAD_DIM, :] = nt(q, score_grad).astype(BF16)
-        g_qkv[g] += nt(qkv_grad_s[...], x[i, g])
+        g_qkv[g] += nt(x[i, g], qkv_grad_s[...])
         add_sum(g, Q_BIAS, qkv_grad_s[0:WIDTH, :].astype(F32))
         add_sum(g, V_BIAS, qkv_grad_s[2 * WIDTH :, :].astype(F32))
         into = bwd[slot, WIDTH:BWD_ROWS, :].astype(F32) + nn(wqkv[g], qkv_grad_s[...])
         x[i, g] = into.astype(BF16)
 
+        @pl.when((j > 0) & (i == count - 1))
+        def _():
+            end_t[j] = end_sums(g)
+            end_copy(j).start()
+
         @pl.when(j > 0)
         def _():
             send_dx(i, j).start()
@@ -476,16 +838,28 @@
         def _():
             own_dx(i).start()
 
+        follow(u)
+
     each(count * GROUPS, unit)
-
-    def close(at):
-        g_vec[at] = jnp.sum(vec[at].T, axis=0, keepdims=True)
-
-    each(GROUPS * COLS, close)
-
-    for k in range(4):
-        for j in (1, 2, 3):
+    qcut_send()
+    out_send(DOWN)
+    mix_core_send()
+    qall_send()
+    for j in range(1, GROUPS):
+        block = shared_out.at[flip(me, j)]
+        across(20 + j, block, block, j).wait_recv()
+    for b in (UP, DOWN):
+        out_copy(b, other_half).wait_recv()
+    for at, j in enumerate((1, 3)):
+        mix_core(at, flip(me, j)).wait_recv()
+    qclose()
+
+    for j in range(1, GROUPS):
+        send_table(j).wait_send()
+        for k in range(1, 4):
             send_weight(k, j).wait_send()
+    for k in range(2, 4):
+        pass_weight(k, mine_half).wait_send()
     own_lo(count - 1).wait()
     for j in range(1, GROUPS):
         send_lo(count - 1, j).wait_send()
@@ -500,30 +874,59 @@
             send_dx(i, j).wait_recv()
 
     each(count, drain)
-
-
-def layer(x, dy, seg, wqkv, wup, wdown, wout, params):
+    for b in range(BLOCKS):
+        pair_copy(b).wait_send()
+        side_copy(b).wait_send()
+        scatter(b, cut_t.at[b], cut_l.at[b], True, sent)
+        when(owns(level, owners, depth), lambda: far_copy(b).wait_send())
+        spread_out(3 + b, all_l.at[b], True, sent)
+    for b in (UP, DOWN):
+        out_copy(b, mine_half).wait_send()
+    mix_far(me).wait_send()
+    for at in range(2):
+        mix_beside(at, mine_half).wait_send()
+        mix_core(at, kept[at]).wait_send()
+        qpair_copy(at).wait_send()
+    when(owns(row, qowners, size), lambda: qpiece_copy().wait_send())
+    for j in range(1, GROUPS):
+        early_copy(j).wait_send()
+        shared_copy(j).wait_send()
+        end_copy(j).wait_send()
+    scatter(6, qfar_t, qfar_l, False, sent)
+    scatter(7, qcut_t, qcut_l, False, sent)
+    spread_out(10, qall_l, False, sent)
+    peers(size, lambda k: along(8, sum_row_t, sum_row_l.at[k], k, False).wait_send())
+    peers(size, lambda k: along(9, end_row_t, end_row_l.at[k], k, False).wait_send())
+
+
+def layer(size, x, dy, *rest):
     count = x.shape[0] // GROUPS
     here = pl.BlockSpec(memory_space=pl.ANY)
     vmem = pl.BlockSpec(memory_space=pltpu.VMEM)
     grads = [
-        (GROUPS, QKV, WIDTH),
-        (GROUPS, WIDTH, UNITS),
-        (GROUPS, WIDTH, UNITS),
-        (D, D),
-        (GROUPS * COLS, 1, WIDTH),
+        ((WIDTH, QKV), BF16),
+        ((WIDTH, UNITS), BF16),
+        ((WIDTH, UNITS), BF16),
+        ((GROUPS, WIDTH, UNITS), BF16),
+        ((TABLE, WIDTH), F32),
+        ((GROUPS, TABLE, WIDTH), F32),
     ]
+    depth = size // 2
+    owners = 2 * owners_of(depth // 2, WIDTH // 32)
+    piece = (WIDTH // owners, HALF)
+    qowners = owners_of(size, WIDTH // 16)
+    qpiece = (WIDTH // qowners, QKV)
     token = (GROUPS, WIDTH, SEQ_LEN)
     dma = pltpu.SemaphoreType.DMA
     return pl.pallas_call(
-        layer_kernel,
+        functools.partial(layer_kernel, size),
         out_shape=[jax.ShapeDtypeStruct(x.shape, BF16)] * 2
         + [
             jax.ShapeDtypeStruct((count, GROUPS, FWD_ROWS, SEQ_LEN), BF16),
             jax.ShapeDtypeStruct((count, GROUPS, BWD_ROWS, SEQ_LEN), BF16),
         ]
-        + [jax.ShapeDtypeStruct(s, F32) for s in grads],
-        in_specs=[here, here, vmem, here, here, here, vmem, vmem],
+        + [jax.ShapeDtypeStruct(s, t) for s, t in grads],
+        in_specs=[here, here, vmem, here, here, here] + [vmem] * 9,
         out_specs=[here] * 4 + [vmem] * len(grads),
         scratch_shapes=[
             pltpu.VMEM((count,) + token, BF16),
@@ -550,63 +953,110 @@
             pltpu.VMEM(token, F32),
             pltpu.VMEM((UNITS, SEQ_LEN), BF16),
             pltpu.VMEM((D, SEQ_LEN), BF16),
-            pltpu.VMEM((D, SEQ_LEN), BF16),
             pltpu.VMEM((QKV, SEQ_LEN), BF16),
             pltpu.VMEM(token, BF16),
+            pltpu.VMEM((BLOCKS, GROUPS, WIDTH, UNITS), F32),
+            pltpu.VMEM((GROUPS, WIDTH, QKV), F32),
+            pltpu.VMEM((BLOCKS, 2, WIDTH, UNITS), BF16),
+            pltpu.VMEM((BLOCKS, 2, WIDTH, UNITS), BF16),
+            pltpu.VMEM((BLOCKS, 2, WIDTH // 2, UNITS), BF16),
+            pltpu.VMEM((BLOCKS, 2, WIDTH // 2, UNITS), BF16),
+            pltpu.VMEM((BLOCKS, owners, 2) + piece, BF16),
+            pltpu.VMEM((BLOCKS, depth, 2) + piece, BF16),
+            pltpu.VMEM((BLOCKS,) + piece, BF16),
+            pltpu.VMEM((BLOCKS,) + piece, BF16),
+            pltpu.VMEM((BLOCKS,) + piece, F32),
+            pltpu.VMEM((BLOCKS, owners) + piece, BF16),
+            pltpu.VMEM((2, WIDTH, QKV), BF16),
+            pltpu.VMEM((2, WIDTH, QKV), BF16),
+            pltpu.VMEM((qowners,) + qpiece, BF16),
+            pltpu.VMEM((size,) + qpiece, BF16),
+            pltpu.VMEM(qpiece, BF16),
+            pltpu.VMEM(qpiece, BF16),
+            pltpu.VMEM((qowners,) + qpiece, BF16),
+            pltpu.VMEM((size,) + qpiece, BF16),
+            pltpu.VMEM((qowners,) + qpiece, BF16),
+            pltpu.VMEM((GROUPS, TABLE, WIDTH), F32),
+            pltpu.VMEM((GROUPS, TABLE, WIDTH), F32),
+            pltpu.VMEM((TABLE, WIDTH), F32),
+            pltpu.VMEM((size, TABLE, WIDTH), F32),
+            pltpu.VMEM((GROUPS, 8, WIDTH), F32),
+            pltpu.VMEM((GROUPS, 8, WIDTH), F32),
+            pltpu.VMEM((8, WIDTH), F32),
+            pltpu.VMEM((size, 8, WIDTH), F32),
         ]
         + [dma((count, GROUPS))] * 8
         + [dma((4, GROUPS))] * 2
+        + [dma((34,))] * 2
+        + [dma((11, size))] * 2
         + [dma((2,))] * 2,
         compiler_params=pltpu.CompilerParams(
             vmem_limit_bytes=63 << 20, collective_id=0, has_side_effects=True
         ),
-    )(x, dy, seg, wqkv, wup, wdown, wout, params)
+    )(x, dy, *rest)
 
 
 def local(
-    layer_input, segment_ids, qkv_weight, qv_bias, out_weight, out_bias, gain_one, shift_one,
+    size, layer_input, segment_ids, qkv_weight, qv_bias, out_weight, out_bias, gain_one, shift_one,
     up_weight, up_bias, down_weight, down_bias, gain_two, shift_two, out_grad,
 ):
-    me = lax.axis_index("grp")
-
-    def rows(a):
-        return a.reshape(-1, WIDTH)
-
-    def mine_of(a):
-        return lax.dynamic_slice_in_dim(a, me * WIDTH, WIDTH, 0).reshape(1, WIDTH)
-
-    params = jnp.concatenate(
-        [rows(a) for a in (qv_bias, up_bias, down_bias, gain_two, shift_two)]
-        + [mine_of(a) for a in (out_bias, gain_one, shift_one)]
-        + [jnp.zeros((TABLE - COLS, WIDTH), F32)]
+    lo, dx, _, _, *grads = layer(
+        size, layer_input, out_grad, segment_ids, qkv_weight, up_weight, down_weight, out_weight,
+        qv_bias, up_bias, down_bias, gain_two, shift_two, out_bias, gain_one, shift_one,
     )
-    lo, dx, _, _, g_qkv, g_up, g_down, g_out, g_vec = layer(
-        layer_input, out_grad, segment_ids, qkv_weight, up_weight, down_weight, out_weight, params
-    )
-
-    def total(a):
-        a = lax.psum_scatter(a, "grp", scatter_dimension=0, tiled=True)
-        return lax.psum(a.astype(BF16), "rows").astype(F32)
-
-    g_vec = lax.psum(g_vec[:, 0, :], ("rows", "grp")).reshape(GROUPS, COLS, WIDTH)
-    mine = lax.dynamic_slice_in_dim(g_vec, me, 1, 0)[0]
-    g_out = lax.psum(g_out, ("rows", "grp"))
-    return (
-        lo.astype(F32),
-        dx.astype(F32),
-        jnp.swapaxes(total(g_qkv), 1, 2),
-        mine[Q_BIAS : V_BIAS + 1].reshape(1, 2 * WIDTH),
-        g_out,
-        g_vec[:, OUT_BIAS].reshape(D),
-        g_vec[:, GAIN_ONE].reshape(D),
-        g_vec[:, SHIFT_ONE].reshape(D),
-        total(g_up),
-        mine[UP_BIAS:DOWN_BIAS].reshape(1, UNITS),
-        total(g_down),
-        mine[DOWN_BIAS].reshape(1, WIDTH),
-        mine[GAIN_TWO],
-        mine[SHIFT_TWO],
-    )
+    lo, dx, g_qkv, g_up, g_down, g_out, qv, out_b, gain1, shift1, up_b, down_b, gain2, shift2 = widen(lo, dx, *grads)
+    return lo, dx, g_qkv, qv, g_out, out_b, gain1, shift1, g_up, up_b, g_down, down_b, gain2, shift2
+
+
+def widen_kernel(
+    lo, dx, qkv, up, down, mix, sums, shared,
+    lo_o, dx_o, qkv_o, up_o, down_o, mix_o, qv_o, out_o, gain1_o, shift1_o, up_b_o, down_b_o, gain2_o, shift2_o,
+):
+    for src, out in ((lo, lo_o), (dx, dx_o), (qkv, qkv_o), (up, up_o), (down, down_o), (mix, mix_o)):
+        out[...] = src[...].astype(F32).reshape(out.shape)
+
+    @pl.when(pl.program_id(0) == 0)
+    def _():
+        def own(first, n):
+            return jnp.concatenate([sums[first + c : first + c + 1, :] for c in range(n)], axis=1)
+
+        def joint(at):
+            return jnp.concatenate([shared[g, at : at + 1, :] for g in range(GROUPS)], axis=1)
+
+        qv_o[...] = own(Q_BIAS, 2)
+        up_b_o[...] = own(UP_BIAS, PARTS)
+        down_b_o[...] = own(DOWN_BIAS, 1)
+        gain2_o[...] = own(GAIN_TWO, 1).reshape(WIDTH)
+        shift2_o[...] = own(SHIFT_TWO, 1).reshape(WIDTH)
+        for out, at in ((out_o, OUT_BIAS), (gain1_o, GAIN_ONE), (shift1_o, SHIFT_ONE)):
+            out[...] = joint(at).reshape(D)
+
+
+def widen(lo, dx, *grads):
+    steps = 8
+    part = WIDTH // steps
+    data = pl.BlockSpec((lo.shape[0] // steps, WIDTH, SEQ_LEN), lambda i: (i, 0, 0))
+
+    def slab(columns):
+        return pl.BlockSpec((part, columns), lambda i: (i, 0)), pl.BlockSpec((1, part, columns), lambda i: (0, i, 0))
+
+    def whole(shape):
+        return pl.BlockSpec(shape, lambda i: (0,) * len(shape), pipeline_mode=pl.Buffered(1))
+
+    qkv_in, qkv_out = slab(QKV)
+    unit_in, unit_out = slab(UNITS)
+    mix_in = pl.BlockSpec((1, WIDTH // 2, D), lambda i: (i // 2, i % 2, 0))
+    mix_out = pl.BlockSpec((WIDTH // 2, D), lambda i: (i, 0))
+    wide = [(1, WIDTH, QKV), (1, WIDTH, UNITS), (1, WIDTH, UNITS), (D, D)]
+    vectors = [(1, 2 * WIDTH), (D,), (D,), (D,), (1, UNITS), (1, WIDTH), (WIDTH,), (WIDTH,)]
+    return pl.pallas_call(
+        widen_kernel,
+        grid=(steps,),
+        out_shape=[jax.ShapeDtypeStruct(s, F32) for s in [lo.shape, dx.shape] + wide + vectors],
+        in_specs=[data, data, qkv_in, unit_in, unit_in, mix_in] + [whole(a.shape) for a in grads[4:]],
+        out_specs=[data, data, qkv_out, unit_out, unit_out, mix_out] + [whole(s) for s in vectors],
+        compiler_params=pltpu.CompilerParams(vmem_limit_bytes=62 << 20),
+    )(lo, dx, *grads)
 
 
 def solution(mesh):
@@ -620,4 +1070,4 @@
         data, data, group, P("grp", None), P(), P(), P(), P(),
         group, P("grp", None), group, P("grp", None), P("grp"), P("grp"),
     )
-    return jax.shard_map(local, mesh=mesh, in_specs=in_specs, out_specs=out_specs, check_vma=False)
+    return jax.shard_map(functools.partial(local, mesh.shape["rows"]), mesh=mesh, in_specs=in_specs, out_specs=out_specs, check_vma=False)

time: 439 us -> 212 us (0.48)
  waiting for transfers between devices: 184 us -> 0 us
  Pallas kernels: 169 us -> 210 us
  blocking collectives: 39.9 us -> 0 us
  other arithmetic: 17.7 us -> 0 us
  between operations: 15.3 us -> 0.66 us
  local copies, waits for them, and re-layouts: 12.3 us -> 0 us
    reduce_scatter x3 -> x0, waiting for transfers between devices: 102 us -> none  [total(): a = lax.psum_scatter(a, 'grp', scatter_dimension=0, tiled=True)]
    psum x2 -> x0, waiting for transfers between devices: 80.5 us -> none  [the longest x1 79.9 us: total(): return lax.psum(a.astype(BF16), 'rows').astype(F32)]
    pallas_call x1 -> x2, Pallas kernels: 169 us -> 210 us  [the longest x1 199 us: layer(): pl.pallas_call(functools.partial(layer_kernel, size), out_shape=[jax.Shap...]
    psum x1 -> x0, blocking collectives: 39.9 us -> none  [local(): lax.psum(g_vec[:, 0, :], ('rows', 'grp')).reshape(GROUPS, COLS, WIDTH)]
    convert_element_type x6 -> x0, other arithmetic: 14.4 us -> none  [the longest x4 7.25 us: total(): return lax.psum(a.astype(BF16), 'rows').astype(F32)]
  transfers between devices with their start and end apart: 5 -> 0, of which waited for: 5 -> 0; matrix products, arithmetic and copies ran while one was open for 4% -> 0% of each run, Pallas kernels for 0% -> 0%
where the time goes in v4:
time: 212 us; the launch traced here: 211 us
  Pallas kernels  210 us (99%)
    pallas_call x1, Pallas kernels, layer(): pl.pallas_call(functools.partial(layer_kernel, size), out_shape=[jax.Shap...  199 us
    pallas_call x1, Pallas kernels, widen(): pl.pallas_call(widen_kernel, grid=(steps,), out_shape=[jax.ShapeDtypeStru...  10.7 us

profile of v4, /device:TPU:0, one launch (start us, length us, event | category | flops | bytes accessed | tf_op | source)
XLA Modules:
  0.0 210.5 jit_solution(8881149439922237472)
XLA Ops:
  0.7 199.2 %shard_map.254 = (bf16[16,192,512]{2,1,0:T(8,128)(2,1)}, bf16[16,192,512]{2,1,0:T(8,128)(2,1)}, bf16[4,4,2208,512]{3,2,1,0:T(8,128)(2,1)}, bf16[4,4,384,512]{3,2...) custom-call(bf16[16,192,512]{2,1,0:T(8,128)(2,1)} %x_in.1, ...), custom_call_target="tpu_custom_call" | custom-call | tf_op jit(solution)/shard_map/pallas_call | solution.py:921
  199.8 10.7 %shard_map.255 = (f32[16,192,512]{2,1,0:T(8,128)}, f32[16,192,512]{2,1,0:T(8,128)}, f32[1,192,576]{2,1,0:T(8,128)}, f32[1,192,768]{2,1,0:T(8,128)}, f32[1,192,76...) custom-call(bf16[16,192,512]{2,1,0:T(8,128)(2,1)} %get-tuple-element, ...), custom_call_target="tpu_custom_call" | custom-call | tf_op jit(solution)/shard_map/pallas_call | solution.py:1052

commit v5 on v4

--- a/solution.py
+++ b/solution.py
@@ -22,6 +22,7 @@
 EPS = 1e-05
 SCALE = HEAD_DIM ** (-0.5)
 BLOCKS = 3
+EARLY = 2
 HALF = UNITS // 2
 
 F32 = jnp.float32
@@ -30,6 +31,7 @@
 
 Q_BIAS, V_BIAS, UP_BIAS, DOWN_BIAS, GAIN_TWO, SHIFT_TWO, OUT_BIAS, GAIN_ONE, SHIFT_ONE = 0, 1, 2, 6, 7, 8, 9, 10, 11
 COLS = 12
+LANE_COLS = COLS - PARTS
 TABLE = 16
 
 E_AT = 0
@@ -89,15 +91,16 @@
     size, x_in, dy_in, seg, wqkv_in, wup_in, wdown_in, wout,
     qv_bias, up_bias, down_bias, gain_two, shift_two, out_bias, gain_one, shift_one,
     lo_out, dx_out, fwd_st, bwd_st, qkv_out, up_out, down_out, mix_out, sums_out, shared_out,
-    x, dy, wqkv, wup, wdown, table, cols, wqkv_t, wup_t, wdown_t, wout_t, vec,
+    x, dy, wqkv, wup, wdown, table, cols, wqkv_t, wup_t, wdown_t, wout_t, vec, up_sum,
     fwd, bwd, middle_s, linv_s, ctx_s, summed_s, hidden_s, act_s, slope_s, summed2_s,
-    up_grad_s, hidden_grad_s, qkv_grad_s, lo_s,
-    acc, g_qkv, pair_t, pair_l, side_t, side_l, cut_t, cut_l, far_t, far_l, own_s, all_l,
+    up_grad_s, hidden_grad_s, lo_s,
+    acc, g_qkv, pair_t, pair_l, side_t, side_l, cut_t, cut_l, far_t, far_l, all_l,
     qpair_t, qpair_l, qfar_t, qfar_l, qpiece_t, qpiece_l, qcut_t, qcut_l, qall_l,
     sum_t, sum_l, sum_row_t, sum_row_l, end_t, end_l, end_row_t, end_row_l,
     s_x, r_x, s_dy, r_dy, s_lo, r_lo, s_dx, r_dx, s_w, r_w, s_one, r_one, s_row, r_row, s_fwd, s_bwd,
 ):
     count = x.shape[0]
+    early = ctx_s.shape[0]
     me = lax.axis_index("grp")
     row = lax.axis_index("rows")
     zero = jnp.zeros((8, SEQ_LEN), F32)
@@ -149,7 +152,7 @@
         return remote(src.at[to * count + i], dst.at[i, me], send.at[i, j], recv.at[i, j], to)
 
     def start_in(src, dst, send, recv, i):
-        for j in range(1, GROUPS):
+        for j in (2, 3):
             move_in(src, dst, send, recv, i, j).start()
 
     def own_in(src, dst, send, i):
@@ -198,22 +201,29 @@
     own_weight(1).start()
     send_weight(1, 2).start()
     send_weight(1, 1).start()
-    own_in(x_in, x, s_x, 0).start()
-    start_in(x_in, x, s_x, r_x, 0)
     for k in range(2, 4):
         own_weight(k).start()
+        send_weight(k, 2).start()
+
+    def near_x(i):
+        own_in(x_in, x, s_x, i).start()
+        move_in(x_in, x, s_x, r_x, i, 1).start()
+
+    def near_dy(i):
+        own_in(dy_in, dy, s_dy, i).start()
+        move_in(dy_in, dy, s_dy, r_dy, i, 1).start()
+
+    each(count, near_x)
+    for k in range(2, 4):
         send_weight(k, 1).start()
-    own_in(dy_in, dy, s_dy, 0).start()
-
-    def own_rest(i):
-        own_in(x_in, x, s_x, i + 1).start()
-        own_in(dy_in, dy, s_dy, i + 1).start()
-
-    each(count - 1, own_rest)
+    each(count, near_dy)
 
     g_qkv[...] = jnp.zeros_like(g_qkv)
     acc[...] = jnp.zeros_like(acc)
     vec[...] = jnp.zeros_like(vec)
+    up_sum[...] = jnp.zeros_like(up_sum)
+    for g in range(GROUPS):
+        hidden_s[g, WIDTH:, :] = jnp.ones((16, SEQ_LEN), BF16)
     wout_t[...] = wout[...].T
 
     for j in range(1, GROUPS):
@@ -227,8 +237,11 @@
     def col(g, at):
         return cols[g, :, at : at + 1]
 
+    def lane_col(g, at):
+        return g * LANE_COLS + (at if at < UP_BIAS else at - PARTS)
+
     def add_sum(g, at, value):
-        vec[g * COLS + at] += lane_part(value)
+        vec[lane_col(g, at)] += lane_part(value)
 
     def rows_of(g):
         return pl.ds(pl.multiple_of(g * WIDTH, WIDTH), WIDTH)
@@ -252,7 +265,7 @@
     def own_lo(i):
         return pltpu.make_async_copy(lo_s.at[me], lo_out.at[me * count + i], s_lo.at[i, 0])
 
-    def sequence(i):
+    def attend(i, j):
         first = i == 0
         label = seg[pl.ds(me * count + i, 1), :]
         ids = lax.broadcasted_iota(jnp.int32, (16, SEQ_LEN), 0)
@@ -260,90 +273,108 @@
         hot_k = hot.astype(BF16)
         hot_q = jnp.where(ids < 4, (1.0 - hot) * MASKED, 0.0).astype(BF16)
 
-        def attend(j):
-            g = flip(me, j)
-            slot = j % 2
-
-            @pl.when(j == 0)
-            def _():
-                own_in(x_in, x, s_x, i).wait()
-
-            @pl.when(j > 0)
-            def _():
-                block = x.at[i, g]
-                remote(block, block, s_x.at[i, j], r_x.at[i, j], g).wait_recv()
-
-            @pl.when(first & (j == 0))
-            def _():
-                own_weight(1).wait()
-
-            @pl.when(first & (j == 1))
-            def _():
-                got_weight(1, 1)
-
-            @pl.when(first & (j == 2))
-            def _():
-                got_weight(1, 2)
-                send_weight(1, 3).start()
-                for k in range(2, 4):
-                    send_weight(k, 2).start()
-
-            @pl.when(first & (j == 3))
-            def _():
-                got_weight(1, 3)
-
-            @pl.when(first)
-            def _():
-                wqkv_t[g] = wqkv[g].T
-
-            @pl.when(i * GROUPS + j >= 2)
-            def _():
-                fwd_save(slot, 0, 0).wait()
-
-            xg = x[i, g]
-            q = (nn(wqkv_t[g, 0:WIDTH, :], xg) + col(g, Q_BIAS)).astype(BF16) * jnp.asarray(SCALE, BF16)
-            k = nn(wqkv_t[g, WIDTH : 2 * WIDTH, :], xg).astype(BF16)
-            v = (nn(wqkv_t[g, 2 * WIDTH :, :], xg) + col(g, V_BIAS)).astype(BF16)
-            fwd[slot, V_AT:FWD_ROWS, :] = v
-            for h in range(HEADS_GROUP):
-                part = slice(h * HEAD_DIM, (h + 1) * HEAD_DIM)
-                qh = jnp.concatenate([q[part], hot_q])
-                kh = jnp.concatenate([k[part], hot_k])
-                fwd[slot, Q_AT + h * PAD : Q_AT + (h + 1) * PAD, :] = qh
-                fwd[slot, K_AT + h * PAD : K_AT + (h + 1) * PAD, :] = kh
-                scores = tn(kh, qh)
-                largest = jnp.max(scores, axis=0, keepdims=True)
-                powers = jnp.exp(scores - largest)
-                inverse = 1.0 / channel_sum(powers)
-                e = powers.astype(BF16)
-                fwd[slot, E_AT + h * SEQ_LEN : E_AT + (h + 1) * SEQ_LEN, :] = e
-                linv_s[g * HEADS_GROUP + h] = inverse
-                ctx_s[pl.ds(pl.multiple_of(g * WIDTH + h * HEAD_DIM, HEAD_DIM), HEAD_DIM), :] = (
-                    nn(v[part], e) * inverse
-                ).astype(BF16)
-            fwd_save(slot, i, g).start()
-
-        each(GROUPS, attend)
+        g = flip(me, j)
+        slot = j % 2
+
+        @pl.when(j == 0)
+        def _():
+            own_in(x_in, x, s_x, i).wait()
+
+        @pl.when(j > 0)
+        def _():
+            block = x.at[i, g]
+            remote(block, block, s_x.at[i, j], r_x.at[i, j], g).wait_recv()
+
+        @pl.when(first & (j == 0))
+        def _():
+            own_weight(1).wait()
+
+        @pl.when(first & (j == 1))
+        def _():
+            got_weight(1, 1)
+
+        @pl.when(first & (j == 3))
+        def _():
+            got_weight(1, 3)
 
         @pl.when(first)
         def _():
-            start_in(dy_in, dy, s_dy, r_dy, 0)
+            wqkv_t[g] = wqkv[g].T
+
+        @pl.when(i * GROUPS + j >= 2)
+        def _():
+            fwd_save(slot, 0, 0).wait()
+
+        xg = x[i, g]
+        q = (nn(wqkv_t[g, 0:WIDTH, :], xg) + col(g, Q_BIAS)).astype(BF16) * jnp.asarray(SCALE, BF16)
+        k = nn(wqkv_t[g, WIDTH : 2 * WIDTH, :], xg).astype(BF16)
+        v = (nn(wqkv_t[g, 2 * WIDTH :, :], xg) + col(g, V_BIAS)).astype(BF16)
+        fwd[slot, V_AT:FWD_ROWS, :] = v
+        for h in range(HEADS_GROUP):
+            part = slice(h * HEAD_DIM, (h + 1) * HEAD_DIM)
+            qh = jnp.concatenate([q[part], hot_q])
+            kh = jnp.concatenate([k[part], hot_k])
+            fwd[slot, Q_AT + h * PAD : Q_AT + (h + 1) * PAD, :] = qh
+            fwd[slot, K_AT + h * PAD : K_AT + (h + 1) * PAD, :] = kh
+            scores = tn(kh, qh)
+            largest = jnp.max(scores, axis=0, keepdims=True)
+            powers = jnp.exp(scores - largest)
+            inverse = 1.0 / channel_sum(powers)
+            e = powers.astype(BF16)
+            fwd[slot, E_AT + h * SEQ_LEN : E_AT + (h + 1) * SEQ_LEN, :] = e
+            linv_s[i % early * HEADS + g * HEADS_GROUP + h] = inverse
+            ctx_s[i % early, pl.ds(pl.multiple_of(g * WIDTH + h * HEAD_DIM, HEAD_DIM), HEAD_DIM), :] = (
+                nn(v[part], e) * inverse
+            ).astype(BF16)
+        fwd_save(slot, i, g).start()
+
+    def prepare(n):
+        attend(n // 2, n % 2)
+
+        @pl.when(n == 0)
+        def _():
+            start_in(x_in, x, s_x, r_x, 0)
+
+        @pl.when(n == early)
+        def _():
+            got_weight(1, 2)
+            send_weight(1, 3).start()
             for k in range(2, 4):
                 got_weight(k, 2)
                 pass_weight(k, mine_half).start()
+            start_in(dy_in, dy, s_dy, r_dy, 0)
+
+        @pl.when(n == 2 * early - 2)
+        def _():
+            for k in range(2, 4):
+                pass_weight(k, other_half).wait_recv()
+                send_weight(k, 3).start()
+
+    def sequence(i):
+        first = i == 0
 
         @pl.when(i + 1 < count)
         def _():
             start_in(x_in, x, s_x, r_x, i + 1)
+
+        def attend_from(j, carry):
+            attend(i, j)
+            return carry
+
+        lax.fori_loop(2 if early == count else jnp.where(i < early, 2, 0), GROUPS, attend_from, 0)
+
+        @pl.when(i + 1 < count)
+        def _():
+            start_in(dy_in, dy, s_dy, r_dy, i + 1)
 
         def mix(g, carry):
             total, square = carry
-            branch = (nn(wout_t[rows_of(g), :], ctx_s[...]) + col(g, OUT_BIAS)).astype(BF16)
+            branch = (nn(wout_t[rows_of(g), :], ctx_s[i % early]) + col(g, OUT_BIAS)).astype(BF16)
             summed = branch.astype(F32) + x[i, g].astype(F32)
             summed_s[g] = summed
             return total + fold(summed), square + fold(summed * summed)
 
-        total, square = over(GROUPS, mix, (zero, zero))
+        total, square = over(GROUPS, mix, (zero, zero), 4)
         center1 = channel_sum(total) / D
         inverse1 = lax.rsqrt(channel_sum(square) / D - center1 * center1 + EPS)
 
@@ -352,9 +383,6 @@
             for k in range(2, 4):
                 own_weight(k).wait()
                 got_weight(k, 1)
-                pass_weight(k, other_half).wait_recv()
-                send_weight(k, 3).start()
-            for k in range(2, 4):
                 got_weight(k, 3)
 
             def turn(g):
@@ -367,7 +395,7 @@
             total, square = carry
             normed = (summed_s[g] - center1) * inverse1
             hidden = (normed * col(g, GAIN_ONE) + col(g, SHIFT_ONE)).astype(BF16)
-            hidden_s[g] = hidden
+            hidden_s[g, 0:WIDTH, :] = hidden
             for part in range(PARTS):
                 rows = slice(part * WIDTH, (part + 1) * WIDTH)
                 u = nn(wup_t[g, rows, :], hidden) + col(g, UP_BIAS + part)
@@ -378,7 +406,7 @@
             summed2_s[g] = summed2
             return total + fold(summed2), square + fold(summed2 * summed2)
 
-        total, square = over(GROUPS, feed, (zero, zero))
+        total, square = over(GROUPS, feed, (zero, zero), 4)
         center2 = channel_sum(total) / D
         inverse2 = lax.rsqrt(channel_sum(square) / D - center2 * center2 + EPS)
 
@@ -392,10 +420,6 @@
         for j in range(1, GROUPS):
             block = dy.at[i, flip(me, j)]
             remote(block, block, s_dy.at[i, j], r_dy.at[i, j], flip(me, j)).wait_recv()
-
-        @pl.when(i + 1 < count)
-        def _():
-            start_in(dy_in, dy, s_dy, r_dy, i + 1)
 
         def finish(g, carry):
             sum_e, sum_en = carry
@@ -409,7 +433,7 @@
             summed2_s[g] = normed
             return sum_e + fold(grad * gain), sum_en + fold(product * gain)
 
-        sum_e, sum_en = over(GROUPS, finish, (zero, zero))
+        sum_e, sum_en = over(GROUPS, finish, (zero, zero), 4)
         mean_e = channel_sum(sum_e) / D
         mean_en = channel_sum(sum_en) / D
 
@@ -428,8 +452,9 @@
                 rows = slice(part * WIDTH, (part + 1) * WIDTH)
                 up_grad = (nn(wdown_t[g, rows, :], grad2) * slope_s[g, rows, :].astype(F32)).astype(BF16)
                 up_grad_s[rows, :] = up_grad
-                add_sum(g, UP_BIAS + part, up_grad.astype(F32))
-            acc[0, g] += nt(hidden_s[g], up_grad_s[...])
+            both = nt(hidden_s[g], up_grad_s[...])
+            acc[0, g] += both[0:WIDTH]
+            up_sum[g] += both[WIDTH : WIDTH + 8]
             acc[1, g] += nt(grad2, act_s[g])
             hidden_grad = (wide + nn(wup[g], up_grad_s[...])).astype(BF16)
             hidden_grad_s[rows_of(g), :] = hidden_grad
@@ -441,7 +466,7 @@
             add_sum(g, SHIFT_ONE, grad1)
             return sum_h + fold(grad1 * gain), sum_hn + fold(product * gain)
 
-        sum_h, sum_hn = over(GROUPS, feed_back, (zero, zero))
+        sum_h, sum_hn = over(GROUPS, feed_back, (zero, zero), 4)
         mean_h = channel_sum(sum_h) / D
         mean_hn = channel_sum(sum_hn) / D
 
@@ -452,31 +477,35 @@
             hidden_grad_s[rows_of(g), :] = summed_grad
             add_sum(g, OUT_BIAS, summed_grad.astype(F32))
 
-        each(GROUPS, norm_back)
+        for g in range(GROUPS):
+            norm_back(g)
 
         def mix_back(g):
-            slot = g % 2
-
-            @pl.when(i * GROUPS + g >= 2)
-            def _():
-                bwd_save(slot, 0, 0).wait()
-
-            ctx = ctx_s[rows_of(g), :]
+            slot = g
+            ctx = ctx_s[i % early, rows_of(g), :]
             acc[2, g] += nt(ctx, hidden_grad_s[...])
             ctx_grad = nn(wout[rows_of(g), :], hidden_grad_s[...]).astype(BF16).astype(F32)
             for h in range(HEADS_GROUP):
                 part = slice(h * HEAD_DIM, (h + 1) * HEAD_DIM)
-                grad = (ctx_grad[part] * linv_s[g * HEADS_GROUP + h]).astype(BF16)
+                grad = (ctx_grad[part] * linv_s[i % early * HEADS + g * HEADS_GROUP + h]).astype(BF16)
                 bwd[slot, h * HEAD_DIM : (h + 1) * HEAD_DIM, :] = grad
                 middle_s[i * HEADS + g * HEADS_GROUP + h] = channel_sum(grad.astype(F32) * ctx[part].astype(F32))
             bwd[slot, WIDTH:BWD_ROWS, :] = hidden_grad_s[rows_of(g), :]
             bwd_save(slot, i, g).start()
 
-        each(GROUPS, mix_back)
-
+        @pl.when(i > 0)
+        def _():
+            for g in range(GROUPS):
+                bwd_save(g, 0, 0).wait()
+
+        for g in range(GROUPS):
+            mix_back(g)
+
+    each(2 * early, prepare)
     each(count, sequence)
     for slot in range(2):
         fwd_save(slot, 0, 0).wait()
+    for slot in range(GROUPS):
         bwd_save(slot, 0, 0).wait()
 
     def unit_of(u):
@@ -593,33 +622,29 @@
             side_t[b, at] = acc[b, kept[at], other_half, :].astype(BF16)
         side_copy(b).start()
 
+    def far_send(b):
+        side_copy(b).wait_recv()
+        acc[b, me, mine_half, :] += side_l[b, 0].astype(F32)
+        far_t[b] = (acc[b, kept[1], mine_half, :] + side_l[b, 1].astype(F32)).astype(BF16)
+        far_copy(b).start()
+
     def cut_send(b):
-        side_copy(b).wait_recv()
-        for at in range(2):
-            total = acc[b, kept[at], mine_half, :] + side_l[b, at].astype(F32)
-            for o in range(owners):
-                rows = o % per_half * cut
-                lanes = o // per_half * HALF
-                cut_t[b, o, at] = total[rows : rows + cut, lanes : lanes + HALF].astype(BF16)
+        far_copy(b).wait_recv()
+        total = acc[b, me, mine_half, :] + far_l[b].astype(F32)
+        for o in range(owners):
+            rows = o % per_half * cut
+            lanes = o // per_half * HALF
+            cut_t[b, o] = total[rows : rows + cut, lanes : lanes + HALF].astype(BF16)
         scatter(b, cut_t.at[b], cut_l.at[b], True, start)
 
-    def far_send(b):
+    def all_send(b):
         def close():
             scatter_got(b, cut_t.at[b], cut_l.at[b], True)
             own = capped(level, owners, depth)
-            total = [cut_t[b, own, at].astype(F32) for at in range(2)]
+            total = cut_t[b, own].astype(F32)
             for k in range(1, depth):
-                total = [total[at] + cut_l[b, k, at].astype(F32) for at in range(2)]
-            own_s[b] = total[0]
-            far_t[b] = total[1].astype(BF16)
-            far_copy(b).start()
-
-        when(owns(level, owners, depth), close)
-
-    def all_send(b):
-        def close():
-            far_copy(b).wait_recv()
-            all_l[b, capped(level, owners, depth)] = (own_s[b] + far_l[b].astype(F32)).astype(BF16)
+                total = total + cut_l[b, k].astype(F32)
+            all_l[b, own] = total.astype(BF16)
 
         when(owns(level, owners, depth), close)
         spread_out(3 + b, all_l.at[b], True, start)
@@ -671,12 +696,13 @@
         return across(23 + j, end_t.at[j], end_l.at[j], j)
 
     def lane_rows(g, columns):
-        return [jnp.sum(vec[g * COLS + c].T, axis=0, keepdims=True) for c in columns]
+        return [jnp.sum(vec[lane_col(g, c)].T, axis=0, keepdims=True) for c in columns]
 
     def early_send():
         for g in range(GROUPS):
             zeros = [jnp.zeros((1, WIDTH), F32)] * 2
-            rows = zeros + lane_rows(g, range(UP_BIAS, COLS)) + zeros * ((TABLE - COLS) // 2)
+            up = [up_sum[g, 0:1, c * WIDTH : (c + 1) * WIDTH] for c in range(PARTS)]
+            rows = zeros + up + lane_rows(g, range(DOWN_BIAS, COLS)) + zeros * ((TABLE - COLS) // 2)
             sum_t[g] = jnp.concatenate(rows)
         for j in range(1, GROUPS):
             early_copy(j).start()
@@ -772,15 +798,16 @@
         1: [lambda: side_send(MIX), early_row_send],
         2: [lambda: side_send(UP)],
         4: [lambda: qpair_send(0, 3), lambda: side_send(DOWN)],
-        5: [lambda: cut_send(MIX), shared_send],
-        7: [lambda: cut_send(UP)],
-        8: [qfar_send],
-        9: [lambda: far_send(MIX), lambda: cut_send(DOWN)],
-        11: [lambda: all_send(MIX), lambda: far_send(UP)],
-        12: [lambda: qpair_send(1, 1), lambda: all_send(UP)],
-        13: [qpiece_send, lambda: far_send(DOWN), mix_far_send],
-        14: [lambda: out_send(UP), lambda: all_send(DOWN)],
-        15: [mix_beside_send],
+        5: [lambda: far_send(MIX), shared_send],
+        7: [lambda: far_send(UP)],
+        8: [qfar_send, lambda: cut_send(MIX)],
+        9: [lambda: far_send(DOWN)],
+        10: [lambda: cut_send(UP)],
+        11: [lambda: all_send(MIX)],
+        12: [lambda: qpair_send(1, 1), lambda: cut_send(DOWN)],
+        13: [qpiece_send, lambda: all_send(UP)],
+        14: [mix_far_send],
+        15: [lambda: all_send(DOWN), lambda: out_send(UP)],
     }
 
     def follow(u):
@@ -816,13 +843,13 @@
             prob_grad = tn(v, grad)
             score_grad = (e.astype(F32) * (prob_grad - middle_s[i * HEADS + g * HEADS_GROUP + h])).astype(BF16)
             at = h * HEAD_DIM
-            qkv_grad_s[2 * WIDTH + at : 2 * WIDTH + at + HEAD_DIM, :] = nt(grad, e).astype(BF16)
-            qkv_grad_s[at : at + HEAD_DIM, :] = (nn(k, score_grad) * SCALE).astype(BF16)
-            qkv_grad_s[WIDTH + at : WIDTH + at + HEAD_DIM, :] = nt(q, score_grad).astype(BF16)
-        g_qkv[g] += nt(x[i, g], qkv_grad_s[...])
-        add_sum(g, Q_BIAS, qkv_grad_s[0:WIDTH, :].astype(F32))
-        add_sum(g, V_BIAS, qkv_grad_s[2 * WIDTH :, :].astype(F32))
-        into = bwd[slot, WIDTH:BWD_ROWS, :].astype(F32) + nn(wqkv[g], qkv_grad_s[...])
+            act_s[0, 2 * WIDTH + at : 2 * WIDTH + at + HEAD_DIM, :] = nt(grad, e).astype(BF16)
+            act_s[0, at : at + HEAD_DIM, :] = (nn(k, score_grad) * SCALE).astype(BF16)
+            act_s[0, WIDTH + at : WIDTH + at + HEAD_DIM, :] = nt(q, score_grad).astype(BF16)
+        g_qkv[g] += nt(x[i, g], act_s[0, 0:QKV, :])
+        add_sum(g, Q_BIAS, act_s[0, 0:WIDTH, :].astype(F32))
+        add_sum(g, V_BIAS, act_s[0, 2 * WIDTH : QKV, :].astype(F32))
+        into = bwd[slot, WIDTH:BWD_ROWS, :].astype(F32) + nn(wqkv[g], act_s[0, 0:QKV, :])
         x[i, g] = into.astype(BF16)
 
         @pl.when((j > 0) & (i == count - 1))
@@ -830,9 +857,14 @@
             end_t[j] = end_sums(g)
             end_copy(j).start()
 
-        @pl.when(j > 0)
-        def _():
-            send_dx(i, j).start()
+        @pl.when(j == 1)
+        def _():
+            send_dx(i, 1).start()
+
+        @pl.when(u % 2 == 1)
+        def _():
+            late_i, late_j = unit_of(u // 2)
+            send_dx(late_i, late_j).start()
 
         @pl.when(j == 0)
         def _():
@@ -842,9 +874,10 @@
 
     each(count * GROUPS, unit)
     qcut_send()
+    qall_send()
+    mix_beside_send()
     out_send(DOWN)
     mix_core_send()
-    qall_send()
     for j in range(1, GROUPS):
         block = shared_out.at[flip(me, j)]
         across(20 + j, block, block, j).wait_recv()
@@ -878,7 +911,7 @@
         pair_copy(b).wait_send()
         side_copy(b).wait_send()
         scatter(b, cut_t.at[b], cut_l.at[b], True, sent)
-        when(owns(level, owners, depth), lambda: far_copy(b).wait_send())
+        far_copy(b).wait_send()
         spread_out(3 + b, all_l.at[b], True, sent)
     for b in (UP, DOWN):
         out_copy(b, mine_half).wait_send()
@@ -911,6 +944,7 @@
         ((TABLE, WIDTH), F32),
         ((GROUPS, TABLE, WIDTH), F32),
     ]
+    early = min(count, EARLY)
     depth = size // 2
     owners = 2 * owners_of(depth // 2, WIDTH // 32)
     piece = (WIDTH // owners, HALF)
@@ -940,20 +974,20 @@
             pltpu.VMEM((GROUPS, UNITS, WIDTH), BF16),
             pltpu.VMEM((GROUPS, UNITS, WIDTH), BF16),
             pltpu.VMEM((D, D), BF16),
-            pltpu.VMEM((GROUPS * COLS, WIDTH, 128), F32),
+            pltpu.VMEM((GROUPS * LANE_COLS, WIDTH, 128), F32),
+            pltpu.VMEM((GROUPS, 8, UNITS), F32),
             pltpu.VMEM((2, FWD_ROWS, SEQ_LEN), BF16),
-            pltpu.VMEM((2, BWD_ROWS, SEQ_LEN), BF16),
+            pltpu.VMEM((GROUPS, BWD_ROWS, SEQ_LEN), BF16),
             pltpu.VMEM((count * HEADS, 1, SEQ_LEN), F32),
-            pltpu.VMEM((HEADS, 1, SEQ_LEN), F32),
-            pltpu.VMEM((D, SEQ_LEN), BF16),
+            pltpu.VMEM((early * HEADS, 1, SEQ_LEN), F32),
+            pltpu.VMEM((early, D, SEQ_LEN), BF16),
             pltpu.VMEM(token, F32),
-            pltpu.VMEM(token, BF16),
+            pltpu.VMEM((GROUPS, WIDTH + 16, SEQ_LEN), BF16),
             pltpu.VMEM((GROUPS, UNITS, SEQ_LEN), BF16),
             pltpu.VMEM((GROUPS, UNITS, SEQ_LEN), BF16),
             pltpu.VMEM(token, F32),
             pltpu.VMEM((UNITS, SEQ_LEN), BF16),
             pltpu.VMEM((D, SEQ_LEN), BF16),
-            pltpu.VMEM((QKV, SEQ_LEN), BF16),
             pltpu.VMEM(token, BF16),
             pltpu.VMEM((BLOCKS, GROUPS, WIDTH, UNITS), F32),
             pltpu.VMEM((GROUPS, WIDTH, QKV), F32),
@@ -961,11 +995,10 @@
             pltpu.VMEM((BLOCKS, 2, WIDTH, UNITS), BF16),
             pltpu.VMEM((BLOCKS, 2, WIDTH // 2, UNITS), BF16),
             pltpu.VMEM((BLOCKS, 2, WIDTH // 2, UNITS), BF16),
-            pltpu.VMEM((BLOCKS, owners, 2) + piece, BF16),
-            pltpu.VMEM((BLOCKS, depth, 2) + piece, BF16),
-            pltpu.VMEM((BLOCKS,) + piece, BF16),
-            pltpu.VMEM((BLOCKS,) + piece, BF16),
-            pltpu.VMEM((BLOCKS,) + piece, F32),
+            pltpu.VMEM((BLOCKS, owners) + piece, BF16),
+            pltpu.VMEM((BLOCKS, depth) + piece, BF16),
+            pltpu.VMEM((BLOCKS, WIDTH // 2, UNITS), BF16),
+            pltpu.VMEM((BLOCKS, WIDTH // 2, UNITS), BF16),
             pltpu.VMEM((BLOCKS, owners) + piece, BF16),
             pltpu.VMEM((2, WIDTH, QKV), BF16),
             pltpu.VMEM((2, WIDTH, QKV), BF16),
@@ -989,9 +1022,9 @@
         + [dma((4, GROUPS))] * 2
         + [dma((34,))] * 2
         + [dma((11, size))] * 2
-        + [dma((2,))] * 2,
+        + [dma((2,)), dma((GROUPS,))],
         compiler_params=pltpu.CompilerParams(
-            vmem_limit_bytes=63 << 20, collective_id=0, has_side_effects=True
+            vmem_limit_bytes=(64 << 20) - (1 << 17), collective_id=0, has_side_effects=True
         ),
     )(x, dy, *rest)
 

time: 212 us -> 203 us (0.958)
  Pallas kernels: 210 us -> 202 us
    pallas_call x1, Pallas kernels: 199 us -> 191 us  [layer(): pl.pallas_call(functools.partial(layer_kernel, size), out_shape=[jax.Shap...]
where the time goes in v5:
time: 203 us
  Pallas kernels  202 us (100%)
    pallas_call x1, Pallas kernels, layer(): pl.pallas_call(functools.partial(layer_kernel, size), out_shape=[jax.Shap...  191 us
    pallas_call x1, Pallas kernels, widen(): pl.pallas_call(widen_kernel, grid=(steps,), out_shape=[jax.ShapeDtypeStru...  10.7 us

profile of v5, /device:TPU:0, one launch (start us, length us, event | category | flops | bytes accessed | tf_op | source)
XLA Modules:
  0.0 203.0 jit_solution(3350013021567958495)
XLA Ops:
  0.7 191.5 %shard_map.254 = (bf16[16,192,512]{2,1,0:T(8,128)(2,1)}, bf16[16,192,512]{2,1,0:T(8,128)(2,1)}, bf16[4,4,2208,512]{3,2,1,0:T(8,128)(2,1)}, bf16[4,4,384,512]{3,2...) custom-call(bf16[16,192,512]{2,1,0:T(8,128)(2,1)} %x_in.1, ...), custom_call_target="tpu_custom_call" | custom-call | tf_op jit(solution)/shard_map/pallas_call | solution.py:955
  192.1 10.7 %shard_map.255 = (f32[16,192,512]{2,1,0:T(8,128)}, f32[16,192,512]{2,1,0:T(8,128)}, f32[1,192,576]{2,1,0:T(8,128)}, f32[1,192,768]{2,1,0:T(8,128)}, f32[1,192,76...) custom-call(bf16[16,192,512]{2,1,0:T(8,128)(2,1)} %get-tuple-element, ...), custom_call_target="tpu_custom_call" | custom-call | tf_op jit(solution)/shard_map/pallas_call | solution.py:1085

commit v6 on v5

--- a/solution.py
+++ b/solution.py
@@ -556,10 +556,11 @@
         return (depth, level) if sided else (size, row)
 
     def capped(at, n, length):
-        return at if n == length else jnp.minimum(at, n - 1)
+        return at if n == length else jnp.clip(at - (length - n) // 2, 0, n - 1)
 
     def owns(at, n, length):
-        return True if n == length else at < n
+        first = (length - n) // 2
+        return True if n == length else (at >= first) & (at < first + n)
 
     def scatter(kind, parts, landing, sided, act):
         n = parts.shape[0]
@@ -799,14 +800,13 @@
         2: [lambda: side_send(UP)],
         4: [lambda: qpair_send(0, 3), lambda: side_send(DOWN)],
         5: [lambda: far_send(MIX), shared_send],
-        7: [lambda: far_send(UP)],
-        8: [qfar_send, lambda: cut_send(MIX)],
-        9: [lambda: far_send(DOWN)],
-        10: [lambda: cut_send(UP)],
-        11: [lambda: all_send(MIX)],
-        12: [lambda: qpair_send(1, 1), lambda: cut_send(DOWN)],
-        13: [qpiece_send, lambda: all_send(UP)],
-        14: [mix_far_send],
+        6: [lambda: far_send(UP)],
+        7: [lambda: cut_send(MIX)],
+        8: [qfar_send],
+        9: [lambda: cut_send(UP), lambda: far_send(DOWN)],
+        10: [lambda: all_send(MIX)],
+        12: [lambda: qpair_send(1, 1), lambda: cut_send(DOWN), lambda: all_send(UP)],
+        13: [mix_far_send, qpiece_send],
         15: [lambda: all_send(DOWN), lambda: out_send(UP)],
     }
 
@@ -874,8 +874,8 @@
 
     each(count * GROUPS, unit)
     qcut_send()
+    mix_beside_send()
     qall_send()
-    mix_beside_send()
     out_send(DOWN)
     mix_core_send()
     for j in range(1, GROUPS):
@@ -1066,7 +1066,7 @@
 
 
 def widen(lo, dx, *grads):
-    steps = 8
+    steps = 4
     part = WIDTH // steps
     data = pl.BlockSpec((lo.shape[0] // steps, WIDTH, SEQ_LEN), lambda i: (i, 0, 0))
 
@@ -1078,8 +1078,8 @@
 
     qkv_in, qkv_out = slab(QKV)
     unit_in, unit_out = slab(UNITS)
-    mix_in = pl.BlockSpec((1, WIDTH // 2, D), lambda i: (i // 2, i % 2, 0))
-    mix_out = pl.BlockSpec((WIDTH // 2, D), lambda i: (i, 0))
+    mix_in = pl.BlockSpec((1, D // steps, D), lambda i: (i, 0, 0))
+    mix_out = pl.BlockSpec((D // steps, D), lambda i: (i, 0))
     wide = [(1, WIDTH, QKV), (1, WIDTH, UNITS), (1, WIDTH, UNITS), (D, D)]
     vectors = [(1, 2 * WIDTH), (D,), (D,), (D,), (1, UNITS), (1, WIDTH), (WIDTH,), (WIDTH,)]
     return pl.pallas_call(

time: 203 us -> 198 us (0.975)
  Pallas kernels: 202 us -> 197 us
    pallas_call x1, Pallas kernels: 191 us -> 187 us  [layer(): pl.pallas_call(functools.partial(layer_kernel, size), out_shape=[jax.Shap...]
where the time goes in v6:
time: 198 us
  Pallas kernels  197 us (99%)
    pallas_call x1, Pallas kernels, layer(): pl.pallas_call(functools.partial(layer_kernel, size), out_shape=[jax.Shap...  187 us
    pallas_call x1, Pallas kernels, widen(): pl.pallas_call(widen_kernel, grid=(steps,), out_shape=[jax.ShapeDtypeStru...  9.93 us

profile of v6, /device:TPU:0, one launch (start us, length us, event | category | flops | bytes accessed | tf_op | source)
XLA Modules:
  0.0 198.0 jit_solution(64489987502396)
XLA Ops:
  0.7 187.2 %shard_map.254 = (bf16[16,192,512]{2,1,0:T(8,128)(2,1)}, bf16[16,192,512]{2,1,0:T(8,128)(2,1)}, bf16[4,4,2208,512]{3,2,1,0:T(8,128)(2,1)}, bf16[4,4,384,512]{3,2...) custom-call(bf16[16,192,512]{2,1,0:T(8,128)(2,1)} %x_in.1, ...), custom_call_target="tpu_custom_call" | custom-call | tf_op jit(solution)/shard_map/pallas_call | solution.py:955
  187.9 9.9 %shard_map.255 = (f32[16,192,512]{2,1,0:T(8,128)}, f32[16,192,512]{2,1,0:T(8,128)}, f32[1,192,576]{2,1,0:T(8,128)}, f32[1,192,768]{2,1,0:T(8,128)}, f32[1,192,76...) custom-call(bf16[16,192,512]{2,1,0:T(8,128)(2,1)} %get-tuple-element, ...), custom_call_target="tpu_custom_call" | custom-call | tf_op jit(solution)/shard_map/pallas_call | solution.py:1085

commit v7 on v6

--- a/solution.py
+++ b/solution.py
@@ -805,9 +805,10 @@
         8: [qfar_send],
         9: [lambda: cut_send(UP), lambda: far_send(DOWN)],
         10: [lambda: all_send(MIX)],
-        12: [lambda: qpair_send(1, 1), lambda: cut_send(DOWN), lambda: all_send(UP)],
-        13: [mix_far_send, qpiece_send],
-        15: [lambda: all_send(DOWN), lambda: out_send(UP)],
+        11: [lambda: cut_send(DOWN)],
+        12: [lambda: qpair_send(1, 1), lambda: all_send(UP), mix_far_send],
+        13: [qpiece_send],
+        14: [lambda: all_send(DOWN), lambda: out_send(UP)],
     }
 
     def follow(u):

time: 198 us -> 200 us (1.010)
  Pallas kernels: 197 us -> 199 us
    pallas_call x1, Pallas kernels: 187 us -> 189 us  [layer(): pl.pallas_call(functools.partial(layer_kernel, size), out_shape=[jax.Shap...]
where the time goes in v7:
time: 200 us
  Pallas kernels  199 us (100%)
    pallas_call x1, Pallas kernels, layer(): pl.pallas_call(functools.partial(layer_kernel, size), out_shape=[jax.Shap...  189 us
    pallas_call x1, Pallas kernels, widen(): pl.pallas_call(widen_kernel, grid=(steps,), out_shape=[jax.ShapeDtypeStru...  9.93 us

profile of v7, /device:TPU:0, one launch (start us, length us, event | category | flops | bytes accessed | tf_op | source)
XLA Modules:
  0.0 200.0 jit_solution(15599419147799175971)
XLA Ops:
  0.7 189.2 %shard_map.254 = (bf16[16,192,512]{2,1,0:T(8,128)(2,1)}, bf16[16,192,512]{2,1,0:T(8,128)(2,1)}, bf16[4,4,2208,512]{3,2,1,0:T(8,128)(2,1)}, bf16[4,4,384,512]{3,2...) custom-call(bf16[16,192,512]{2,1,0:T(8,128)(2,1)} %x_in.1, ...), custom_call_target="tpu_custom_call" | custom-call | tf_op jit(solution)/shard_map/pallas_call | solution.py:956
  189.9 9.9 %shard_map.255 = (f32[16,192,512]{2,1,0:T(8,128)}, f32[16,192,512]{2,1,0:T(8,128)}, f32[1,192,576]{2,1,0:T(8,128)}, f32[1,192,768]{2,1,0:T(8,128)}, f32[1,192,76...) custom-call(bf16[16,192,512]{2,1,0:T(8,128)(2,1)} %get-tuple-element, ...), custom_call_target="tpu_custom_call" | custom-call | tf_op jit(solution)/shard_map/pallas_call | solution.py:1086
